TPU v7x, 256 devices: a whole 4x4x8 slice. The times are simulated.
256 devices in a mesh: gx: 4 (over y_hi, core), gy: 8 (over z), gz: 8 (over y_lo, x).
Axes of the slice: x: 4, y: 4 (y_hi: 2, y_lo: 2; y = y_hi * 2 + y_lo), z: 8, core: 2. Of those that a mesh axis runs over, the one named last changes fastest.
Arguments:
- order_param: float32 [16, 128, 1024], P('gx', 'gy', 'gz'), may hold values from -1 to 1
- density: float32 [16, 128, 1024], P('gx', 'gy', 'gz'), may hold values from 0.7 to 1.3
- velocity: float32 [3, 16, 128, 1024], P(None, 'gx', 'gy', 'gz'), may hold values from -0.3 to 0.3
Outputs:
- final_order: float32 [16, 128, 1024], P('gx', 'gy', 'gz')
- populations: float32 [19, 16, 128, 1024], P(None, 'gx', 'gy', 'gz')
All inputs are finite; a program needn't handle non-finite values.
Results may differ from a plain program's by a relative error of at most 0.0001.
Values sent between devices are 32-bit elements; how exact they have to be, the bound alone decides.
No kernel may reach another device: no remote copies, remote signals or barrier semaphores. Data moves between devices by JAX's collectives and lax.ppermute only.
A program may use at most 64 MiB of HBM per device.

v0:
```python
import jax
import jax.numpy as jnp
from jax import lax
from jax.experimental import pallas as pl
from jax.experimental.pallas import tpu as pltpu
from jax.sharding import PartitionSpec as P

ITERS = 5
DIRECTIONS = [
    (0, 0, 0),
    (1, 0, 0),
    (-1, 0, 0),
    (0, 1, 0),
    (0, -1, 0),
    (0, 0, 1),
    (0, 0, -1),
    (1, 1, 0),
    (-1, -1, 0),
    (1, -1, 0),
    (-1, 1, 0),
    (1, 0, 1),
    (-1, 0, -1),
    (1, 0, -1),
    (-1, 0, 1),
    (0, 1, 1),
    (0, -1, -1),
    (0, 1, -1),
    (0, -1, 1),
]
INDEX = {c: i for i, c in enumerate(DIRECTIONS)}
quadratic = -0.1
quartic = 0.1
stiffness = 0.02
mobility = 0.5

AXES = ("gx", "gy", "gz")
F32 = jnp.float32
NX = 16
BY = 16
LANES = 128
EDGE = 20
GAP = 24
ROWS = 80
OWN = 30


def tiles(radius):
    low = (OWN - radius) // 8 * 8
    high = -(-(OWN + BY + radius) // 8) * 8
    return list(range(low, high, 8))


def lane_masks(core, shape):
    lane = lax.broadcasted_iota(jnp.int32, shape, len(shape) - 1)
    low, high = lane < EDGE, lane >= LANES - EDGE
    first = core == 0
    send = (first & low) | (jnp.logical_not(first) & high)
    take = (first & high) | (jnp.logical_not(first) & low)
    return send, take


def gather_pair(core_ref, mine_ref, other_ref, both_ref, edge_ref):
    core = core_ref[0]
    lo, hi = core * 4, 4 - core * 4
    send, _ = lane_masks(core, (BY, LANES))
    for source, base in ((mine_ref, lo), (other_ref, hi)):
        for x in range(4):
            packed = None
            for f in range(5):
                value = source[f, x]
                both_ref[f, base + x] = value
                part = jnp.where(send, value, 0.0)
                part = pltpu.roll(part, GAP * f, 1) if f else part
                packed = part if packed is None else packed + part
            edge_ref[base + x] = packed


def merge_edges(core_ref, near_ref, far_ref, near_edge, far_edge, out_ref, up_ref, down_ref):
    _, take = lane_masks(core_ref[0], (BY, LANES))
    for x in range(NX):
        source, edges = (near_ref, near_edge) if x < 8 else (far_ref, far_edge)
        edge = edges[x % 8]
        row = (x % 2) * 12
        for f in range(5):
            moved = pltpu.roll(edge, LANES - GAP * f, 1) if f else edge
            value = jnp.where(take, moved, source[f, x % 8])
            out_ref[f, x] = value
            count = 4 if f == 0 else 2
            up_ref[x // 2, row : row + count, :] = value[BY - count :]
            down_ref[x // 2, row : row + count, :] = value[:count]
            row += count


def prev_lane(v):
    return pltpu.roll(v, 1, 1)


def next_lane(v):
    return pltpu.roll(v, LANES - 1, 1)


def collide(rho, vel, kick, old):
    moved = [v + g for v, g in zip(vel, kick)]
    pairs = ((0, 1), (0, 2), (1, 2))
    unit = rho * (1.0 / 36.0)
    if old is None:
        square = [m * m for m in moved]
        cross = [moved[d] * moved[e] for d, e in pairs]
        drift = moved
        rest = 1.0
    else:
        square = [0.25 * (v * v) + m * m for v, m in zip(vel, moved)]
        cross = [0.25 * (vel[d] * vel[e]) + moved[d] * moved[e] for d, e in pairs]
        drift = [1.25 * v + g for v, g in zip(vel, kick)]
        rest = 1.25
    base = unit * (rest - 1.5 * (square[0] + square[1] + square[2]))
    unit45 = unit * 4.5
    unit9 = unit * 9.0
    unit3 = unit * 3.0
    sq = [unit45 * s for s in square]
    cr = [unit9 * q for q in cross]
    dr = [unit3 * b for b in drift]

    def settle(i, value):
        return value if old is None else value - 0.25 * old(i)

    post = {0: settle(0, 12.0 * base)}
    for d in range(3):
        even = 2.0 * (base + sq[d])
        odd = 2.0 * dr[d]
        c = [0, 0, 0]
        c[d] = 1
        i = INDEX[tuple(c)]
        post[i] = settle(i, even + odd)
        c[d] = -1
        i = INDEX[tuple(c)]
        post[i] = settle(i, even - odd)
    for k, (d, e) in enumerate(pairs):
        even = base + (sq[d] + sq[e])
        for sign in (1, -1):
            part = even + cr[k] if sign == 1 else even - cr[k]
            odd = dr[d] + dr[e] if sign == 1 else dr[d] - dr[e]
            c = [0, 0, 0]
            c[d], c[e] = 1, sign
            i = INDEX[tuple(c)]
            post[i] = settle(i, part + odd)
            c[d], c[e] = -1, -sign
            i = INDEX[tuple(c)]
            post[i] = settle(i, part - odd)
    return post


def moments(f):
    both, diff = {}, {}
    for i in range(1, 19, 2):
        both[i] = f[i] + f[i + 1]
        diff[i] = f[i] - f[i + 1]
    rho = ((f[0] + both[1]) + (both[3] + both[5])) + (
        ((both[7] + both[9]) + (both[11] + both[13])) + (both[15] + both[17])
    )
    mx = (diff[1] + (diff[7] + diff[9])) + (diff[11] + diff[13])
    my = (diff[3] + (diff[7] - diff[9])) + (diff[15] + diff[17])
    mz = (diff[5] + (diff[11] - diff[13])) + (diff[15] - diff[17])
    return rho, (mx, my, mz)


def steps_kernel(core_ref, own, low, high, low2, high2, mine_ref, send_ref, pops_a, pops_b, order_a, order_b, chem, rho, inv, vel):
    core = core_ref[0]

    def load(x, _):
        odd = lax.rem(x, 2)
        pair = lax.div(x, 2)
        for f, target in enumerate((order_a, rho, vel.at[0], vel.at[1], vel.at[2])):
            target[x, pl.ds(OWN - 16, 16), :] = low[f, x]
            target[x, pl.ds(OWN, 16), :] = own[f, x]
            target[x, pl.ds(OWN + 16, 16), :] = high[f, x]
            count = 4 if f == 0 else 2
            row = 0 if f == 0 else 2 + 2 * f
            for half in range(2):

                @pl.when(odd == half)
                def _():
                    target[x, pl.ds(OWN - 16 - count, count), :] = low2[pair, half * 12 + row : half * 12 + row + count, :]
                    target[x, pl.ds(OWN + 32, count), :] = high2[pair, half * 12 + row : half * 12 + row + count, :]
        return 0

    lax.fori_loop(0, NX, load, 0)

    order, order_next = order_a, order_b
    pops, pops_next = pops_a, pops_b
    for step in range(ITERS):
        left = 4 * (ITERS - 1 - step)
        last = step == ITERS - 1

        def chem_of(n, _, order=order, left=left, first=-3 if last else 0):
            x = (n + first) & 15
            up, down = (x + 1) & 15, (x - 1) & 15
            for r in tiles(left + 3):
                here = order[x, pl.ds(r, 8), :]
                beside = (order[up, pl.ds(r, 8), :] + order[down, pl.ds(r, 8), :]) + (
                    order[x, pl.ds(r + 1, 8), :] + order[x, pl.ds(r - 1, 8), :]
                )
                beside = beside + (next_lane(here) + prev_lane(here))
                chem[x, pl.ds(r, 8), :] = here * ((quadratic + 6.0 * stiffness) + quartic * (here * here)) - stiffness * beside
            return 0

        lax.fori_loop(0, 14 if last else 16, chem_of, 0)

        def collide_of(n, _, step=step, order=order, pops=pops, pops_next=pops_next, left=left, first=-2 if last else 0):
            x = (n + first) & 15
            up, down = (x + 1) & 15, (x - 1) & 15
            to = {0: x, 1: up, -1: down}
            for r in tiles(left + 2):
                at = pl.ds(r, 8)
                mu = chem[x, at, :]
                density = rho[x, at, :]
                inverse = 1.0 / density if step == 0 else inv[x, at, :]
                pull = (-0.5 * order[x, at, :]) * inverse
                kick = [
                    pull * (chem[up, at, :] - chem[down, at, :]),
                    pull * (chem[x, pl.ds(r + 1, 8), :] - chem[x, pl.ds(r - 1, 8), :]),
                    pull * (next_lane(mu) - prev_lane(mu)),
                ]
                old = None if step == 0 else (lambda i: pops[i, x, at, :])
                post = collide(density, [vel[d, x, at, :] for d in range(3)], kick, old)
                for i in range(19):
                    cx, cy, cz = DIRECTIONS[i]
                    value = post[i]
                    if cz:
                        value = prev_lane(value) if cz == 1 else next_lane(value)
                    pops_next[i, to[cx], pl.ds(r + cy, 8), :] = value
            return 0

        lax.fori_loop(0, 12 if last else 16, collide_of, 0)

        def flow_of(n, _, pops_next=pops_next, left=left, first=-1 if last else 0):
            x = (n + first) & 15
            for r in tiles(left + 1):
                at = pl.ds(r, 8)
                total, moms = moments([pops_next[i, x, at, :] for i in range(19)])
                inverse = 1.0 / total
                rho[x, at, :] = total
                inv[x, at, :] = inverse
                for d in range(3):
                    vel[d, x, at, :] = moms[d] * inverse
            return 0

        lax.fori_loop(0, 10 if last else 16, flow_of, 0)

        def order_of(x, _, order=order, order_next=order_next, left=left):
            up, down = (x + 1) & 15, (x - 1) & 15
            for r in tiles(left):
                at, north, south = pl.ds(r, 8), pl.ds(r + 1, 8), pl.ds(r - 1, 8)
                here = order[x, at, :]
                mu = chem[x, at, :]
                ux, uy, uz = (vel[d, x, at, :] for d in range(3))
                total = (ux + vel[0, up, at, :]) * (here + order[up, at, :]) - (ux + vel[0, down, at, :]) * (here + order[down, at, :])
                total = total + (uy + vel[1, x, north, :]) * (here + order[x, north, :])
                total = total - (uy + vel[1, x, south, :]) * (here + order[x, south, :])
                spread = (chem[up, at, :] + chem[down, at, :]) + (chem[x, north, :] + chem[x, south, :]) - 4.0 * mu
                face = (0.25 * (uz + next_lane(uz))) * (here + next_lane(here)) - mobility * (next_lane(mu) - mu)
                order_next[x, at, :] = here - ((0.25 * total - mobility * spread) + (face - prev_lane(face)))
            return 0

        lax.fori_loop(0, 8 if last else 16, order_of, 0)
        order, order_next = order_next, order
        pops, pops_next = pops_next, pops

    for target, base in ((mine_ref, core * 4), (send_ref, 4 - core * 4)):
        for x in range(4):
            for i in range(19):
                target[i, x] = pops[i, base + x, pl.ds(OWN, 16), :]
            target[19, x] = order[base + x, pl.ds(OWN, 16), :]


def vmem_call(kernel, outs, scratch=(), limit=None):
    space = pl.BlockSpec(memory_space=pltpu.VMEM)

    def call(core, *args):
        return pl.pallas_call(
            kernel,
            out_shape=[jax.ShapeDtypeStruct(s, F32) for s in outs],
            in_specs=[pl.BlockSpec(memory_space=pltpu.SMEM)] + [space] * len(args),
            out_specs=[space] * len(outs),
            scratch_shapes=[pltpu.VMEM(s, F32) for s in scratch],
            compiler_params=pltpu.CompilerParams(vmem_limit_bytes=limit or 24 << 20),
        )(core, *args)

    return call


def on_device(order_param, density, velocity):
    sizes = [lax.axis_size(a) for a in AXES]

    def send(value, to):
        pairs = []
        for x in range(sizes[0]):
            for y in range(sizes[1]):
                for z in range(sizes[2]):
                    tx, ty, tz = to(x, y, z)
                    there = (tx % sizes[0] * sizes[1] + ty % sizes[1]) * sizes[2] + tz % sizes[2]
                    pairs.append(((x * sizes[1] + y) * sizes[2] + z, there))
        return lax.ppermute(value, AXES, pairs)

    core = lax.rem(lax.axis_index("gx"), 2)
    core_arg = core.astype(jnp.int32).reshape(1)
    fields = jnp.concatenate([order_param[None], density[None], velocity])
    other = lax.ppermute(fields, "gx", [(i, i ^ 1) for i in range(sizes[0])])
    near, edge = vmem_call(gather_pair, [(5, 8, BY, LANES), (8, BY, LANES)])(core_arg, fields, other)
    far = lax.ppermute(near, "gx", [(i, i ^ 2) for i in range(sizes[0])])
    near_edge = send(edge, lambda x, y, z: (x ^ 1, y, z + 1 if x & 1 else z - 1))
    far_edge = send(edge, lambda x, y, z: (x ^ 3, y, z + 1 if x & 1 else z - 1))
    whole, last_rows, first_rows = vmem_call(merge_edges, [(5, NX, BY, LANES), (8, 24, LANES), (8, 24, LANES)])(
        core_arg, near, far, near_edge, far_edge
    )
    low = lax.ppermute(whole, "gy", [(i, (i + 1) % sizes[1]) for i in range(sizes[1])])
    high = lax.ppermute(whole, "gy", [(i, (i - 1) % sizes[1]) for i in range(sizes[1])])
    low2 = lax.ppermute(last_rows, "gy", [(i, (i + 2) % sizes[1]) for i in range(sizes[1])])
    high2 = lax.ppermute(first_rows, "gy", [(i, (i - 2) % sizes[1]) for i in range(sizes[1])])
    field = (NX, ROWS, LANES)
    mine, away = vmem_call(
        steps_kernel,
        [(20, 4, BY, LANES)] * 2,
        [(19,) + field, (19,) + field, field, field, field, field, field, (3,) + field],
        60 << 20,
    )(core_arg, whole, low, high, low2, high2)
    back = lax.ppermute(away, "gx", [(i, i ^ 1) for i in range(sizes[0])])
    half = lax.broadcasted_iota(jnp.int32, (1, 1, 1, LANES), 3) >= LANES // 2
    full = jnp.where(half == (core == 1), mine, back)
    return (full[19], full[:19])


def solution(mesh):
    return jax.shard_map(
        on_device,
        mesh=mesh,
        in_specs=(P("gx", "gy", "gz"), P("gx", "gy", "gz"), P(None, "gx", "gy", "gz")),
        out_specs=(P("gx", "gy", "gz"), P(None, "gx", "gy", "gz")),
        check_vma=False,
    )
```

profile of v0, /device:TPU:1, one launch (start us, length us, event | category | flops | bytes accessed | tf_op | source)
XLA Modules:
  0.0 89.2 jit_solution(8884539835110065410)
XLA Ops:
  0.6 0.9 %pad_maximum_fusion.mine_ref = f32[5,4,16,128]{3,2,1,0:T(8,128)S(1)} fusion(f32[3,4,16,128]{3,2,1,0:T(8,128)} %param.5, f32[1,4,16,128]{3,2,1,0:T(8,128)} %bitcast.5, f32[1,4,16,128]{3,2,1,0:T(8,128)} %bitcast.6), kind=kLoop, calls=%fused_computation.1 | loop fusion | flops 81920 | bytes 327680 | tf_op jit(solution)/shard_map/concatenate | solution.py:307
  1.6 3.3 %collective-permute-start = (f32[5,4,16,128]{3,2,1,0:T(8,128)S(1)}, f32[5,4,16,128]{3,2,1,0:T(8,128)S(1)}, u32[]{:S(2)}, u32[]{:S(2)}) collective-permute-start(f32[5,4,16,128]{3,2,1,0:T(8,128)S(1)} %pad_maximum_fusion.mine_ref), channel_id=1, source_target_pairs={{0,64},{64,0},{128,192},{192,128},{1,65},{65,1},{129,193},{193,129... | collective-permute-start | bytes 491528 | tf_op jit(solution)/shard_map/ppermute | solution.py:308
  4.9 1.0 %collective-permute-done.other_ref = f32[5,4,16,128]{3,2,1,0:T(8,128)S(1)} collective-permute-done((f32[5,4,16,128]{3,2,1,0:T(8,128)S(1)}, f32[5,4,16,128]{3,2,1,0:T(8,128)S(1)}, u32[]{:S(2)}, u32[]{:S(2)}) %collective-permute-start) | collective-permute-done | bytes 163872 | tf_op jit(solution)/shard_map/ppermute | solution.py:308
  5.9 0.1 shard_map.50
  6.1 1.3 %collective-permute-start.1 = (f32[5,8,16,128]{3,2,1,0:T(8,128)S(1)}, f32[5,8,16,128]{3,2,1,0:T(8,128)S(1)}, u32[]{:S(2)}, u32[]{:S(2)}) collective-permute-start(f32[5,8,16,128]{3,2,1,0:T(8,128)S(1)} %get-tuple-element.9.near_ref), channel_id=1, source_target_pairs={{0,128},{64,192},{128,0},{192,64},{1,129},{65,193},{129,1},{193,65... | collective-permute-start | bytes 983048 | tf_op jit(solution)/shard_map/ppermute | solution.py:310
  7.3 1.7 %collective-permute-start.2 = (f32[8,16,128]{2,1,0:T(8,128)S(1)}, f32[8,16,128]{2,1,0:T(8,128)S(1)}, u32[]{:S(2)}, u32[]{:S(2)}) collective-permute-start(f32[8,16,128]{2,1,0:T(8,128)S(1)} %get-tuple-element.10), channel_id=1, source_target_pairs={{0,71},{1,64},{2,65},{3,66},{4,67},{5,68},{6,69},{7,70},{8,79},{9,... | collective-permute-start | bytes 196616 | tf_op jit(solution)/shard_map/ppermute | solution.py:303
  9.1 1.5 %collective-permute-start.3 = (f32[8,16,128]{2,1,0:T(8,128)S(1)}, f32[8,16,128]{2,1,0:T(8,128)S(1)}, u32[]{:S(2)}, u32[]{:S(2)}) collective-permute-start(f32[8,16,128]{2,1,0:T(8,128)S(1)} %get-tuple-element.10), channel_id=1, source_target_pairs={{0,199},{1,192},{2,193},{3,194},{4,195},{5,196},{6,197},{7,198},{8... | collective-permute-start | bytes 196616 | tf_op jit(solution)/shard_map/ppermute | solution.py:303
  10.6 0.7 collective-permute-done.2.near_edge
  11.3 4.0 %collective-permute-done.3.far_edge = f32[8,16,128]{2,1,0:T(8,128)S(1)} collective-permute-done((f32[8,16,128]{2,1,0:T(8,128)S(1)}, f32[8,16,128]{2,1,0:T(8,128)S(1)}, u32[]{:S(2)}, u32[]{:S(2)}) %collective-permute-start.3) | collective-permute-done | bytes 65568 | tf_op jit(solution)/shard_map/ppermute | solution.py:303
  15.3 3.4 %collective-permute-done.1.far_ref = f32[5,8,16,128]{3,2,1,0:T(8,128)S(1)} collective-permute-done((f32[5,8,16,128]{3,2,1,0:T(8,128)S(1)}, f32[5,8,16,128]{3,2,1,0:T(8,128)S(1)}, u32[]{:S(2)}, u32[]{:S(2)}) %collective-permute-start.1) | collective-permute-done | bytes 327712 | tf_op jit(solution)/shard_map/ppermute | solution.py:310
  18.6 0.2 shard_map.51
  18.8 0.0 copy-start
  18.8 0.1 collective-permute-start.4
  18.9 3.3 %collective-permute-start.5 = (f32[5,16,16,128]{3,2,1,0:T(8,128)S(1)}, f32[5,16,16,128]{3,2,1,0:T(8,128)S(1)}, u32[]{:S(2)}, u32[]{:S(2)}) collective-permute-start(f32[5,16,16,128]{3,2,1,0:T(8,128)S(1)} %get-tuple-element.11.own), channel_id=1, source_target_pairs={{0,56},{8,0},{16,8},{24,16},{32,24},{40,32},{48,40},{56,48},{1,57}... | collective-permute-start | bytes 1966088 | tf_op jit(solution)/shard_map/ppermute | solution.py:317
  22.2 0.0 collective-permute-start.6
  22.2 3.6 %collective-permute-start.7 = (f32[8,24,128]{2,1,0:T(8,128)S(1)}, f32[8,24,128]{2,1,0:T(8,128)S(1)}, u32[]{:S(2)}, u32[]{:S(2)}) collective-permute-start(f32[8,24,128]{2,1,0:T(8,128)S(1)} %get-tuple-element.13), channel_id=1, source_target_pairs={{0,48},{8,56},{16,0},{24,8},{32,16},{40,24},{48,32},{56,40},{1,49}... | collective-permute-start | bytes 294920 | tf_op jit(solution)/shard_map/ppermute | solution.py:319
  25.8 12.9 %collective-permute-done.6.low2 = f32[8,24,128]{2,1,0:T(8,128)S(1)} collective-permute-done((f32[8,24,128]{2,1,0:T(8,128)S(1)}, f32[8,24,128]{2,1,0:T(8,128)S(1)}, u32[]{:S(2)}, u32[]{:S(2)}) %collective-permute-start.6) | collective-permute-done | bytes 98336 | tf_op jit(solution)/shard_map/ppermute | solution.py:318
  38.7 0.0 copy-start.3
  38.7 0.0 collective-permute-done.7.high2
  38.7 0.0 copy-start.4
  38.7 0.0 collective-permute-done.4.low
  38.7 0.0 copy-start.1
  38.7 0.0 collective-permute-done.5.high
  38.7 0.0 copy-done
  38.7 0.6 copy-done.3
  39.3 0.0 copy-done.4
  39.4 0.3 copy-done.1
  39.6 0.0 copy-start.2
  39.6 0.8 copy-done.2
  40.4 40.3 %shard_map.52 = (f32[20,4,16,128]{3,2,1,0:T(8,128)}, f32[20,4,16,128]{3,2,1,0:T(8,128)}) custom-call(s32[1]{0:T(128)} %bitcast.core_ref, f32[5,16,16,128]{3,2,1,0:T(8,128)} %copy-done, f32[5,16,16,128]{3,2,1,0:T(8,128)} %copy-done.1, f32[5,16,16,128]{3,2,1,0:T(8,128)} %copy-done.2, f32[8,24,128]{2,1,0:T(8,128)} %copy-done.3, f32[8,24,128]{2,1,0:T(8,128)} %copy-done.4), custom_call_target="tpu_custom_call" | custom-call | tf_op jit(solution)/shard_map/pallas_call | solution.py:280
  80.8 3.9 %collective-permute-start.8 = (f32[20,4,16,128]{3,2,1,0:T(8,128)}, f32[20,4,16,128]{3,2,1,0:T(8,128)S(1)}, u32[]{:S(2)}, u32[]{:S(2)}) collective-permute-start(f32[20,4,16,128]{3,2,1,0:T(8,128)} %get-tuple-element.15), channel_id=1, source_target_pairs={{0,64},{64,0},{128,192},{192,128},{1,65},{65,1},{129,193},{193,129... | collective-permute-start | bytes 1966088 | tf_op jit(solution)/shard_map/ppermute | solution.py:327
  84.6 1.9 %collective-permute-done.8 = f32[20,4,16,128]{3,2,1,0:T(8,128)S(1)} collective-permute-done((f32[20,4,16,128]{3,2,1,0:T(8,128)}, f32[20,4,16,128]{3,2,1,0:T(8,128)S(1)}, u32[]{:S(2)}, u32[]{:S(2)}) %collective-permute-start.8) | collective-permute-done | bytes 655392 | tf_op jit(solution)/shard_map/ppermute | solution.py:327
  86.6 1.2 %broadcast_select_fusion = f32[20,4,16,128]{3,2,1,0:T(8,128)S(1)} fusion(f32[20,4,16,128]{3,2,1,0:T(8,128)} %get-tuple-element.14, f32[20,4,16,128]{3,2,1,0:T(8,128)S(1)} %collective-permute-done.8, pred[128]{0:T(512)(128)(4,1)S(1)} %compare_compare_fusion), kind=kLoop, calls=%fused_computation | loop fusion | flops 163840 | bytes 1966208 | tf_op jit(solution)/shard_map/jit(_where)/select_n | solution.py:329
  87.7 0.9 slice.9
  88.6 0.6 slice_bitcast_fusion
  (1 shorter events, 0.0 us)
Async XLA Ops:
  1.6 4.4 %collective-permute-start = (f32[5,4,16,128]{3,2,1,0:T(8,128)S(1)}, f32[5,4,16,128]{3,2,1,0:T(8,128)S(1)}, u32[]{:S(2)}, u32[]{:S(2)}) collective-permute-start(f32[5,4,16,128]{3,2,1,0:T(8,128)S(1)} %pad_maximum_fusion.mine_ref), channel_id=1, source_target_pairs={{0,64},{64,0},{128,192},{192,128},{1,65},{65,1},{129,193},{193,129... | collective-permute-start | bytes 491528 | tf_op jit(solution)/shard_map/ppermute | solution.py:308
  6.1 12.6 %collective-permute-start.1 = (f32[5,8,16,128]{3,2,1,0:T(8,128)S(1)}, f32[5,8,16,128]{3,2,1,0:T(8,128)S(1)}, u32[]{:S(2)}, u32[]{:S(2)}) collective-permute-start(f32[5,8,16,128]{3,2,1,0:T(8,128)S(1)} %get-tuple-element.9.near_ref), channel_id=1, source_target_pairs={{0,128},{64,192},{128,0},{192,64},{1,129},{65,193},{129,1},{193,65... | collective-permute-start | bytes 983048 | tf_op jit(solution)/shard_map/ppermute | solution.py:310
  7.3 4.0 %collective-permute-start.2 = (f32[8,16,128]{2,1,0:T(8,128)S(1)}, f32[8,16,128]{2,1,0:T(8,128)S(1)}, u32[]{:S(2)}, u32[]{:S(2)}) collective-permute-start(f32[8,16,128]{2,1,0:T(8,128)S(1)} %get-tuple-element.10), channel_id=1, source_target_pairs={{0,71},{1,64},{2,65},{3,66},{4,67},{5,68},{6,69},{7,70},{8,79},{9,... | collective-permute-start | bytes 196616 | tf_op jit(solution)/shard_map/ppermute | solution.py:303
  9.1 6.2 %collective-permute-start.3 = (f32[8,16,128]{2,1,0:T(8,128)S(1)}, f32[8,16,128]{2,1,0:T(8,128)S(1)}, u32[]{:S(2)}, u32[]{:S(2)}) collective-permute-start(f32[8,16,128]{2,1,0:T(8,128)S(1)} %get-tuple-element.10), channel_id=1, source_target_pairs={{0,199},{1,192},{2,193},{3,194},{4,195},{5,196},{6,197},{7,198},{8... | collective-permute-start | bytes 196616 | tf_op jit(solution)/shard_map/ppermute | solution.py:303
  18.8 19.9 %copy-start = (f32[5,16,16,128]{3,2,1,0:T(8,128)}, f32[5,16,16,128]{3,2,1,0:T(8,128)S(1)}, u32[]{:S(2)}) copy-start(f32[5,16,16,128]{3,2,1,0:T(8,128)S(1)} %get-tuple-element.11.own) | copy-start | bytes 1966084
  18.8 19.8 %collective-permute-start.4 = (f32[5,16,16,128]{3,2,1,0:T(8,128)S(1)}, f32[5,16,16,128]{3,2,1,0:T(8,128)S(1)}, u32[]{:S(2)}, u32[]{:S(2)}) collective-permute-start(f32[5,16,16,128]{3,2,1,0:T(8,128)S(1)} %get-tuple-element.11.own), channel_id=1, source_target_pairs={{0,8},{8,16},{16,24},{24,32},{32,40},{40,48},{48,56},{56,0},{1,9},... | collective-permute-start | bytes 1966088 | tf_op jit(solution)/shard_map/ppermute | solution.py:316
  18.9 19.8 %collective-permute-start.5 = (f32[5,16,16,128]{3,2,1,0:T(8,128)S(1)}, f32[5,16,16,128]{3,2,1,0:T(8,128)S(1)}, u32[]{:S(2)}, u32[]{:S(2)}) collective-permute-start(f32[5,16,16,128]{3,2,1,0:T(8,128)S(1)} %get-tuple-element.11.own), channel_id=1, source_target_pairs={{0,56},{8,0},{16,8},{24,16},{32,24},{40,32},{48,40},{56,48},{1,57}... | collective-permute-start | bytes 1966088 | tf_op jit(solution)/shard_map/ppermute | solution.py:317
  22.2 16.5 %collective-permute-start.6 = (f32[8,24,128]{2,1,0:T(8,128)S(1)}, f32[8,24,128]{2,1,0:T(8,128)S(1)}, u32[]{:S(2)}, u32[]{:S(2)}) collective-permute-start(f32[8,24,128]{2,1,0:T(8,128)S(1)} %get-tuple-element.12), channel_id=1, source_target_pairs={{0,16},{8,24},{16,32},{24,40},{32,48},{40,56},{48,0},{56,8},{1,17}... | collective-permute-start | bytes 294920 | tf_op jit(solution)/shard_map/ppermute | solution.py:318
  22.2 16.5 %collective-permute-start.7 = (f32[8,24,128]{2,1,0:T(8,128)S(1)}, f32[8,24,128]{2,1,0:T(8,128)S(1)}, u32[]{:S(2)}, u32[]{:S(2)}) collective-permute-start(f32[8,24,128]{2,1,0:T(8,128)S(1)} %get-tuple-element.13), channel_id=1, source_target_pairs={{0,48},{8,56},{16,0},{24,8},{32,16},{40,24},{48,32},{56,40},{1,49}... | collective-permute-start | bytes 294920 | tf_op jit(solution)/shard_map/ppermute | solution.py:319
  38.7 0.6 copy-start.3
  38.7 0.7 copy-start.4
  38.7 0.9 %copy-start.1 = (f32[5,16,16,128]{3,2,1,0:T(8,128)}, f32[5,16,16,128]{3,2,1,0:T(8,128)S(1)}, u32[]{:S(2)}) copy-start(f32[5,16,16,128]{3,2,1,0:T(8,128)S(1)} %collective-permute-done.4.low) | copy-start | bytes 1966084
  39.6 0.8 copy-start.2
  80.8 5.8 %collective-permute-start.8 = (f32[20,4,16,128]{3,2,1,0:T(8,128)}, f32[20,4,16,128]{3,2,1,0:T(8,128)S(1)}, u32[]{:S(2)}, u32[]{:S(2)}) collective-permute-start(f32[20,4,16,128]{3,2,1,0:T(8,128)} %get-tuple-element.15), channel_id=1, source_target_pairs={{0,64},{64,0},{128,192},{192,128},{1,65},{65,1},{129,193},{193,129... | collective-permute-start | bytes 1966088 | tf_op jit(solution)/shard_map/ppermute | solution.py:327
where the time goes:
time: 90 us; the launch traced here: 89.2 us
  Pallas kernels  40.7 us (45%)
  waiting for transfers between devices  23.9 us (27%)
  starting transfers between devices  18.6 us (21%)
  local copies, waits for them, and re-layouts  3.24 us (4%)
  other arithmetic  2.11 us (2%)
    pallas_call x3, Pallas kernels, call(): pl.pallas_call(kernel, out_shape=[jax.ShapeDtypeStruct(s, F32) for s in o...  40.7 us
    ppermute x1, waiting for transfers between devices, on_device(): lax.ppermute(last_rows, 'gy', [(i, (i + 2) % sizes[1]) for i in range(siz...  12.9 us
    ppermute x2, waiting for transfers between devices, send(): return lax.ppermute(value, AXES, pairs)  4.68 us
    ppermute x1, starting transfers between devices, on_device(): back = lax.ppermute(away, 'gx', [(i, i ^ 1) for i in range(sizes[0])])  3.86 us
    ppermute x1, starting transfers between devices, on_device(): lax.ppermute(first_rows, 'gy', [(i, (i - 2) % sizes[1]) for i in range(si...  3.57 us
    ppermute x1, waiting for transfers between devices, on_device(): far = lax.ppermute(near, 'gx', [(i, i ^ 2) for i in range(sizes[0])])  3.37 us
    ppermute x1, starting transfers between devices, on_device(): other = lax.ppermute(fields, 'gx', [(i, i ^ 1) for i in range(sizes[0])])  3.33 us
    ppermute x1, starting transfers between devices, on_device(): lax.ppermute(whole, 'gy', [(i, (i - 1) % sizes[1]) for i in range(sizes[1...  3.27 us
  transfers between devices with their start and end apart: 9, of which 6 were waited for; matrix products, arithmetic and copies ran while one was open for 0% of the time, Pallas kernels for 0%

commit v1 on v0

--- a/solution.py
+++ b/solution.py
@@ -99,34 +99,36 @@
     return pltpu.roll(v, LANES - 1, 1)
 
 
-def collide(rho, vel, kick, old):
+def collide(density, vel, kick, old):
     moved = [v + g for v, g in zip(vel, kick)]
     pairs = ((0, 1), (0, 2), (1, 2))
-    unit = rho * (1.0 / 36.0)
     if old is None:
+        unit = density * (1.0 / 36.0)
+        rest = unit
+        drift = moved
         square = [m * m for m in moved]
         cross = [moved[d] * moved[e] for d, e in pairs]
-        drift = moved
-        rest = 1.0
     else:
-        square = [0.25 * (v * v) + m * m for v, m in zip(vel, moved)]
-        cross = [0.25 * (vel[d] * vel[e]) + moved[d] * moved[e] for d, e in pairs]
+        unit = density * (-4.0 / 36.0)
+        rest = density * (-5.0 / 36.0)
         drift = [1.25 * v + g for v, g in zip(vel, kick)]
-        rest = 1.25
-    base = unit * (rest - 1.5 * (square[0] + square[1] + square[2]))
+        square = [v * b + g * m for v, g, b, m in zip(vel, kick, drift, moved)]
+        cross = [vel[d] * drift[e] + kick[d] * moved[e] for d, e in pairs]
+    unit3 = unit * 3.0
     unit45 = unit * 4.5
     unit9 = unit * 9.0
-    unit3 = unit * 3.0
-    sq = [unit45 * s for s in square]
-    cr = [unit9 * q for q in cross]
-    dr = [unit3 * b for b in drift]
+    sq = [unit45 * v for v in square]
+    cr = [unit9 * v for v in cross]
+    dr = [unit3 * v for v in drift]
+    base = rest - (1.0 / 3.0) * (sq[0] + sq[1] + sq[2])
 
     def settle(i, value):
-        return value if old is None else value - 0.25 * old(i)
+        return value if old is None else value + old(i)
 
     post = {0: settle(0, 12.0 * base)}
+    axis = [base + v for v in sq]
     for d in range(3):
-        even = 2.0 * (base + sq[d])
+        even = 2.0 * axis[d]
         odd = 2.0 * dr[d]
         c = [0, 0, 0]
         c[d] = 1
@@ -136,7 +138,7 @@
         i = INDEX[tuple(c)]
         post[i] = settle(i, even - odd)
     for k, (d, e) in enumerate(pairs):
-        even = base + (sq[d] + sq[e])
+        even = axis[d] + sq[e]
         for sign in (1, -1):
             part = even + cr[k] if sign == 1 else even - cr[k]
             odd = dr[d] + dr[e] if sign == 1 else dr[d] - dr[e]
@@ -167,24 +169,19 @@
 def steps_kernel(core_ref, own, low, high, low2, high2, mine_ref, send_ref, pops_a, pops_b, order_a, order_b, chem, rho, inv, vel):
     core = core_ref[0]
 
-    def load(x, _):
-        odd = lax.rem(x, 2)
-        pair = lax.div(x, 2)
-        for f, target in enumerate((order_a, rho, vel.at[0], vel.at[1], vel.at[2])):
-            target[x, pl.ds(OWN - 16, 16), :] = low[f, x]
-            target[x, pl.ds(OWN, 16), :] = own[f, x]
-            target[x, pl.ds(OWN + 16, 16), :] = high[f, x]
-            count = 4 if f == 0 else 2
-            row = 0 if f == 0 else 2 + 2 * f
-            for half in range(2):
-
-                @pl.when(odd == half)
-                def _():
-                    target[x, pl.ds(OWN - 16 - count, count), :] = low2[pair, half * 12 + row : half * 12 + row + count, :]
-                    target[x, pl.ds(OWN + 32, count), :] = high2[pair, half * 12 + row : half * 12 + row + count, :]
+    def load(pair, _):
+        for half in range(2):
+            x = 2 * pair + half
+            for f, target in enumerate((order_a, rho, vel.at[0], vel.at[1], vel.at[2])):
+                target[x, pl.ds(OWN - 16, 16), :] = low[f, x]
+                target[x, pl.ds(OWN, 16), :] = own[f, x]
+                target[x, pl.ds(OWN + 16, 16), :] = high[f, x]
+                count, row = (4, 12 * half) if f == 0 else (2, 12 * half + 2 + 2 * f)
+                target[x, pl.ds(OWN - 16 - count, count), :] = low2[pair, row : row + count, :]
+                target[x, pl.ds(OWN + 32, count), :] = high2[pair, row : row + count, :]
         return 0
 
-    lax.fori_loop(0, NX, load, 0)
+    lax.fori_loop(0, NX // 2, load, 0)
 
     order, order_next = order_a, order_b
     pops, pops_next = pops_a, pops_b
@@ -204,7 +201,7 @@
                 chem[x, pl.ds(r, 8), :] = here * ((quadratic + 6.0 * stiffness) + quartic * (here * here)) - stiffness * beside
             return 0
 
-        lax.fori_loop(0, 14 if last else 16, chem_of, 0)
+        lax.fori_loop(0, 14 if last else 16, chem_of, 0, unroll=4)
 
         def collide_of(n, _, step=step, order=order, pops=pops, pops_next=pops_next, left=left, first=-2 if last else 0):
             x = (n + first) & 15
@@ -215,7 +212,7 @@
                 mu = chem[x, at, :]
                 density = rho[x, at, :]
                 inverse = 1.0 / density if step == 0 else inv[x, at, :]
-                pull = (-0.5 * order[x, at, :]) * inverse
+                pull = ((-0.5 * (-4.0) ** max(step - 1, 0)) * order[x, at, :]) * inverse
                 kick = [
                     pull * (chem[up, at, :] - chem[down, at, :]),
                     pull * (chem[x, pl.ds(r + 1, 8), :] - chem[x, pl.ds(r - 1, 8), :]),
@@ -231,7 +228,7 @@
                     pops_next[i, to[cx], pl.ds(r + cy, 8), :] = value
             return 0
 
-        lax.fori_loop(0, 12 if last else 16, collide_of, 0)
+        lax.fori_loop(0, 12 if last else 16, collide_of, 0, unroll=2)
 
         def flow_of(n, _, pops_next=pops_next, left=left, first=-1 if last else 0):
             x = (n + first) & 15
@@ -245,7 +242,7 @@
                     vel[d, x, at, :] = moms[d] * inverse
             return 0
 
-        lax.fori_loop(0, 10 if last else 16, flow_of, 0)
+        lax.fori_loop(0, 10 if last else 16, flow_of, 0, unroll=2)
 
         def order_of(x, _, order=order, order_next=order_next, left=left):
             up, down = (x + 1) & 15, (x - 1) & 15
@@ -262,15 +259,24 @@
                 order_next[x, at, :] = here - ((0.25 * total - mobility * spread) + (face - prev_lane(face)))
             return 0
 
-        lax.fori_loop(0, 8 if last else 16, order_of, 0)
+        lax.fori_loop(0, 8 if last else 16, order_of, 0, unroll=4)
         order, order_next = order_next, order
         pops, pops_next = pops_next, pops
 
     for target, base in ((mine_ref, core * 4), (send_ref, 4 - core * 4)):
         for x in range(4):
             for i in range(19):
-                target[i, x] = pops[i, base + x, pl.ds(OWN, 16), :]
+                target[i, x] = pops[i, base + x, pl.ds(OWN, 16), :] * (1.0 / 256.0)
             target[19, x] = order[base + x, pl.ds(OWN, 16), :]
+
+
+def join_halves(core_ref, mine_ref, back_ref, order_ref, pops_ref):
+    lane = lax.broadcasted_iota(jnp.int32, (4, BY, LANES), 2)
+    first = core_ref[0] == 0
+    keep = (first & (lane < LANES // 2)) | (jnp.logical_not(first) & (lane >= LANES // 2))
+    for i in range(19):
+        pops_ref[i] = jnp.where(keep, mine_ref[i], back_ref[i])
+    order_ref[...] = jnp.where(keep, mine_ref[19], back_ref[19])
 
 
 def vmem_call(kernel, outs, scratch=(), limit=None):
@@ -325,9 +331,7 @@
         60 << 20,
     )(core_arg, whole, low, high, low2, high2)
     back = lax.ppermute(away, "gx", [(i, i ^ 1) for i in range(sizes[0])])
-    half = lax.broadcasted_iota(jnp.int32, (1, 1, 1, LANES), 3) >= LANES // 2
-    full = jnp.where(half == (core == 1), mine, back)
-    return (full[19], full[:19])
+    return tuple(vmem_call(join_halves, [(4, BY, LANES), (19, 4, BY, LANES)])(core_arg, mine, back))
 
 
 def solution(mesh):

time: 90 us -> 73.2 us (0.81)
  Pallas kernels: 40.7 us -> 24.5 us
  waiting for transfers between devices: 23.9 us -> 25.1 us
  other arithmetic: 2.11 us -> 0.93 us
    pallas_call x3 -> x4, Pallas kernels: 40.7 us -> 24.5 us  [call(): pl.pallas_call(kernel, out_shape=[jax.ShapeDtypeStruct(s, F32) for s in o...]
    ppermute x2, waiting for transfers between devices: 4.68 us -> 2.94 us  [send(): return lax.ppermute(value, AXES, pairs)]
    ppermute x1, waiting for transfers between devices: 3.37 us -> 5.11 us  [on_device(): far = lax.ppermute(near, 'gx', [(i, i ^ 2) for i in range(sizes[0])])]
    ppermute x1, waiting for transfers between devices: 12.9 us -> 14.1 us  [on_device(): lax.ppermute(last_rows, 'gy', [(i, (i + 2) % sizes[1]) for i in range(siz...]
    select_n x1 -> x0, other arithmetic: 1.17 us -> none  [on_device(): full = jnp.where(half == (core == 1), mine, back)]
    unnamed x10 -> x12, local copies, waits for them, and re-layouts: 1.74 us -> 2.81 us
  transfers between devices with their start and end apart: 9 -> 9, of which waited for: 6 -> 5; matrix products, arithmetic and copies ran while one was open for 0% -> 0% of each run, Pallas kernels for 0% -> 0%
where the time goes in v1:
time: 73.2 us; the launch traced here: 72.4 us
  waiting for transfers between devices  25.1 us (34%)
  Pallas kernels  24.5 us (33%)
  starting transfers between devices  18.3 us (25%)
  local copies, waits for them, and re-layouts  2.81 us (4%)
  other arithmetic  0.93 us (1%)
    pallas_call x4, Pallas kernels, call(): pl.pallas_call(kernel, out_shape=[jax.ShapeDtypeStruct(s, F32) for s in o...  24.5 us
    ppermute x1, waiting for transfers between devices, on_device(): lax.ppermute(last_rows, 'gy', [(i, (i + 2) % sizes[1]) for i in range(siz...  14.1 us
    ppermute x1, waiting for transfers between devices, on_device(): far = lax.ppermute(near, 'gx', [(i, i ^ 2) for i in range(sizes[0])])  5.11 us
    ppermute x1, starting transfers between devices, on_device(): back = lax.ppermute(away, 'gx', [(i, i ^ 1) for i in range(sizes[0])])  3.68 us
    ppermute x1, starting transfers between devices, on_device(): lax.ppermute(first_rows, 'gy', [(i, (i - 2) % sizes[1]) for i in range(si...  3.57 us
    ppermute x1, starting transfers between devices, on_device(): other = lax.ppermute(fields, 'gx', [(i, i ^ 1) for i in range(sizes[0])])  3.33 us
    ppermute x2, starting transfers between devices, send(): return lax.ppermute(value, AXES, pairs)  3.25 us
    ppermute x1, starting transfers between devices, on_device(): lax.ppermute(whole, 'gy', [(i, (i - 1) % sizes[1]) for i in range(sizes[1...  3.21 us
  transfers between devices with their start and end apart: 9, of which 5 were waited for; matrix products, arithmetic and copies ran while one was open for 0% of the time, Pallas kernels for 0%

profile of v1, /device:TPU:1, one launch (start us, length us, event | category | flops | bytes accessed | tf_op | source)
XLA Modules:
  0.0 72.4 jit_solution(13052252844665339380)
XLA Ops:
  0.6 0.9 %pad_maximum_fusion.mine_ref = f32[5,4,16,128]{3,2,1,0:T(8,128)S(1)} fusion(f32[3,4,16,128]{3,2,1,0:T(8,128)} %param.5, f32[1,4,16,128]{3,2,1,0:T(8,128)} %bitcast.3, f32[1,4,16,128]{3,2,1,0:T(8,128)} %bitcast.4), kind=kLoop, calls=%fused_computation | loop fusion | flops 81920 | bytes 327680 | tf_op jit(solution)/shard_map/concatenate | solution.py:313
  1.6 3.3 %collective-permute-start = (f32[5,4,16,128]{3,2,1,0:T(8,128)S(1)}, f32[5,4,16,128]{3,2,1,0:T(8,128)S(1)}, u32[]{:S(2)}, u32[]{:S(2)}) collective-permute-start(f32[5,4,16,128]{3,2,1,0:T(8,128)S(1)} %pad_maximum_fusion.mine_ref), channel_id=1, source_target_pairs={{0,64},{64,0},{128,192},{192,128},{1,65},{65,1},{129,193},{193,129... | collective-permute-start | bytes 491528 | tf_op jit(solution)/shard_map/ppermute | solution.py:314
  4.9 1.0 %collective-permute-done.other_ref = f32[5,4,16,128]{3,2,1,0:T(8,128)S(1)} collective-permute-done((f32[5,4,16,128]{3,2,1,0:T(8,128)S(1)}, f32[5,4,16,128]{3,2,1,0:T(8,128)S(1)}, u32[]{:S(2)}, u32[]{:S(2)}) %collective-permute-start) | collective-permute-done | bytes 163872 | tf_op jit(solution)/shard_map/ppermute | solution.py:314
  5.9 0.1 shard_map.50
  6.1 1.3 %collective-permute-start.1 = (f32[5,8,16,128]{3,2,1,0:T(8,128)S(1)}, f32[5,8,16,128]{3,2,1,0:T(8,128)S(1)}, u32[]{:S(2)}, u32[]{:S(2)}) collective-permute-start(f32[5,8,16,128]{3,2,1,0:T(8,128)S(1)} %get-tuple-element.9.near_ref), channel_id=1, source_target_pairs={{0,128},{64,192},{128,0},{192,64},{1,129},{65,193},{129,1},{193,65... | collective-permute-start | bytes 983048 | tf_op jit(solution)/shard_map/ppermute | solution.py:316
  7.3 1.5 %collective-permute-start.3 = (f32[8,16,128]{2,1,0:T(8,128)S(1)}, f32[8,16,128]{2,1,0:T(8,128)S(1)}, u32[]{:S(2)}, u32[]{:S(2)}) collective-permute-start(f32[8,16,128]{2,1,0:T(8,128)S(1)} %get-tuple-element.10), channel_id=1, source_target_pairs={{0,199},{1,192},{2,193},{3,194},{4,195},{5,196},{6,197},{7,198},{8... | collective-permute-start | bytes 196616 | tf_op jit(solution)/shard_map/ppermute | solution.py:309
  8.8 1.7 %collective-permute-start.2 = (f32[8,16,128]{2,1,0:T(8,128)S(1)}, f32[8,16,128]{2,1,0:T(8,128)S(1)}, u32[]{:S(2)}, u32[]{:S(2)}) collective-permute-start(f32[8,16,128]{2,1,0:T(8,128)S(1)} %get-tuple-element.10), channel_id=1, source_target_pairs={{0,71},{1,64},{2,65},{3,66},{4,67},{5,68},{6,69},{7,70},{8,79},{9,... | collective-permute-start | bytes 196616 | tf_op jit(solution)/shard_map/ppermute | solution.py:309
  10.6 2.9 %collective-permute-done.3.far_edge = f32[8,16,128]{2,1,0:T(8,128)S(1)} collective-permute-done((f32[8,16,128]{2,1,0:T(8,128)S(1)}, f32[8,16,128]{2,1,0:T(8,128)S(1)}, u32[]{:S(2)}, u32[]{:S(2)}) %collective-permute-start.3) | collective-permute-done | bytes 65568 | tf_op jit(solution)/shard_map/ppermute | solution.py:309
  13.5 0.0 collective-permute-done.2.near_edge
  13.5 5.1 %collective-permute-done.1.far_ref = f32[5,8,16,128]{3,2,1,0:T(8,128)S(1)} collective-permute-done((f32[5,8,16,128]{3,2,1,0:T(8,128)S(1)}, f32[5,8,16,128]{3,2,1,0:T(8,128)S(1)}, u32[]{:S(2)}, u32[]{:S(2)}) %collective-permute-start.1) | collective-permute-done | bytes 327712 | tf_op jit(solution)/shard_map/ppermute | solution.py:316
  18.6 0.2 shard_map.51
  18.8 0.0 copy-start
  18.8 3.2 %collective-permute-start.5 = (f32[5,16,16,128]{3,2,1,0:T(8,128)S(1)}, f32[5,16,16,128]{3,2,1,0:T(8,128)S(1)}, u32[]{:S(2)}, u32[]{:S(2)}) collective-permute-start(f32[5,16,16,128]{3,2,1,0:T(8,128)S(1)} %get-tuple-element.11.own), channel_id=1, source_target_pairs={{0,56},{8,0},{16,8},{24,16},{32,24},{40,32},{48,40},{56,48},{1,57}... | collective-permute-start | bytes 1966088 | tf_op jit(solution)/shard_map/ppermute | solution.py:323
  22.1 0.0 collective-permute-start.4
  22.1 0.0 collective-permute-start.6
  22.1 3.6 %collective-permute-start.7 = (f32[8,24,128]{2,1,0:T(8,128)S(1)}, f32[8,24,128]{2,1,0:T(8,128)S(1)}, u32[]{:S(2)}, u32[]{:S(2)}) collective-permute-start(f32[8,24,128]{2,1,0:T(8,128)S(1)} %get-tuple-element.13), channel_id=1, source_target_pairs={{0,48},{8,56},{16,0},{24,8},{32,16},{40,24},{48,32},{56,40},{1,49}... | collective-permute-start | bytes 294920 | tf_op jit(solution)/shard_map/ppermute | solution.py:325
  25.6 14.1 %collective-permute-done.6.low2 = f32[8,24,128]{2,1,0:T(8,128)S(1)} collective-permute-done((f32[8,24,128]{2,1,0:T(8,128)S(1)}, f32[8,24,128]{2,1,0:T(8,128)S(1)}, u32[]{:S(2)}, u32[]{:S(2)}) %collective-permute-start.6) | collective-permute-done | bytes 98336 | tf_op jit(solution)/shard_map/ppermute | solution.py:324
  39.7 0.0 copy-start.4
  39.7 0.0 collective-permute-done.7.high2
  39.7 0.0 copy-start.5
  39.7 0.0 collective-permute-done.5.high
  39.7 0.0 copy-start.2
  39.7 0.0 collective-permute-done.4.low
  39.7 0.0 copy-done
  39.8 0.6 copy-done.4
  40.4 0.0 copy-done.5
  40.4 0.2 copy-done.2
  40.6 0.0 copy-start.3
  40.6 0.9 %copy-done.3 = f32[5,16,16,128]{3,2,1,0:T(8,128)} copy-done((f32[5,16,16,128]{3,2,1,0:T(8,128)}, f32[5,16,16,128]{3,2,1,0:T(8,128)S(1)}, u32[]{:S(2)}) %copy-start.3) | copy-done | bytes 655384
  41.5 23.3 %shard_map.52 = (f32[20,4,16,128]{3,2,1,0:T(8,128)}, f32[20,4,16,128]{3,2,1,0:T(8,128)}) custom-call(s32[1]{0:T(128)} %bitcast.core_ref, f32[5,16,16,128]{3,2,1,0:T(8,128)} %copy-done, f32[5,16,16,128]{3,2,1,0:T(8,128)} %copy-done.3, f32[5,16,16,128]{3,2,1,0:T(8,128)} %copy-done.2, f32[8,24,128]{2,1,0:T(8,128)} %copy-done.4, f32[8,24,128]{2,1,0:T(8,128)} %copy-done.5), custom_call_target="tpu_custom_call" | custom-call | tf_op jit(solution)/shard_map/pallas_call | solution.py:286
  64.8 3.7 %collective-permute-start.8 = (f32[20,4,16,128]{3,2,1,0:T(8,128)}, f32[20,4,16,128]{3,2,1,0:T(8,128)S(1)}, u32[]{:S(2)}, u32[]{:S(2)}) collective-permute-start(f32[20,4,16,128]{3,2,1,0:T(8,128)} %get-tuple-element.15), channel_id=1, source_target_pairs={{0,64},{64,0},{128,192},{192,128},{1,65},{65,1},{129,193},{193,129... | collective-permute-start | bytes 1966088 | tf_op jit(solution)/shard_map/ppermute | solution.py:333
  68.5 1.9 %collective-permute-done.8.back_ref = f32[20,4,16,128]{3,2,1,0:T(8,128)S(1)} collective-permute-done((f32[20,4,16,128]{3,2,1,0:T(8,128)}, f32[20,4,16,128]{3,2,1,0:T(8,128)S(1)}, u32[]{:S(2)}, u32[]{:S(2)}) %collective-permute-start.8) | collective-permute-done | bytes 655392 | tf_op jit(solution)/shard_map/ppermute | solution.py:333
  70.4 0.0 copy-start.1
  70.4 1.1 %copy-done.1 = f32[20,4,16,128]{3,2,1,0:T(8,128)S(1)} copy-done((f32[20,4,16,128]{3,2,1,0:T(8,128)S(1)}, f32[20,4,16,128]{3,2,1,0:T(8,128)}, u32[]{:S(2)}) %copy-start.1) | copy-done | bytes 655384
  71.5 0.9 %shard_map.53 = (f32[4,16,128]{2,1,0:T(8,128)}, f32[19,4,16,128]{3,2,1,0:T(8,128)}) custom-call(s32[1]{0:T(128)} %bitcast.core_ref, f32[20,4,16,128]{3,2,1,0:T(8,128)S(1)} %copy-done.1, f32[20,4,16,128]{3,2,1,0:T(8,128)S(1)} %collective-permute-done.8.back_ref), custom_call_target="tpu_custom_call" | custom-call | tf_op jit(solution)/shard_map/pallas_call | solution.py:286
Async XLA Ops:
  1.6 4.4 %collective-permute-start = (f32[5,4,16,128]{3,2,1,0:T(8,128)S(1)}, f32[5,4,16,128]{3,2,1,0:T(8,128)S(1)}, u32[]{:S(2)}, u32[]{:S(2)}) collective-permute-start(f32[5,4,16,128]{3,2,1,0:T(8,128)S(1)} %pad_maximum_fusion.mine_ref), channel_id=1, source_target_pairs={{0,64},{64,0},{128,192},{192,128},{1,65},{65,1},{129,193},{193,129... | collective-permute-start | bytes 491528 | tf_op jit(solution)/shard_map/ppermute | solution.py:314
  6.1 12.6 %collective-permute-start.1 = (f32[5,8,16,128]{3,2,1,0:T(8,128)S(1)}, f32[5,8,16,128]{3,2,1,0:T(8,128)S(1)}, u32[]{:S(2)}, u32[]{:S(2)}) collective-permute-start(f32[5,8,16,128]{3,2,1,0:T(8,128)S(1)} %get-tuple-element.9.near_ref), channel_id=1, source_target_pairs={{0,128},{64,192},{128,0},{192,64},{1,129},{65,193},{129,1},{193,65... | collective-permute-start | bytes 983048 | tf_op jit(solution)/shard_map/ppermute | solution.py:316
  7.3 6.2 %collective-permute-start.3 = (f32[8,16,128]{2,1,0:T(8,128)S(1)}, f32[8,16,128]{2,1,0:T(8,128)S(1)}, u32[]{:S(2)}, u32[]{:S(2)}) collective-permute-start(f32[8,16,128]{2,1,0:T(8,128)S(1)} %get-tuple-element.10), channel_id=1, source_target_pairs={{0,199},{1,192},{2,193},{3,194},{4,195},{5,196},{6,197},{7,198},{8... | collective-permute-start | bytes 196616 | tf_op jit(solution)/shard_map/ppermute | solution.py:309
  8.8 4.7 %collective-permute-start.2 = (f32[8,16,128]{2,1,0:T(8,128)S(1)}, f32[8,16,128]{2,1,0:T(8,128)S(1)}, u32[]{:S(2)}, u32[]{:S(2)}) collective-permute-start(f32[8,16,128]{2,1,0:T(8,128)S(1)} %get-tuple-element.10), channel_id=1, source_target_pairs={{0,71},{1,64},{2,65},{3,66},{4,67},{5,68},{6,69},{7,70},{8,79},{9,... | collective-permute-start | bytes 196616 | tf_op jit(solution)/shard_map/ppermute | solution.py:309
  18.8 20.9 %copy-start = (f32[5,16,16,128]{3,2,1,0:T(8,128)}, f32[5,16,16,128]{3,2,1,0:T(8,128)S(1)}, u32[]{:S(2)}) copy-start(f32[5,16,16,128]{3,2,1,0:T(8,128)S(1)} %get-tuple-element.11.own) | copy-start | bytes 1966084
  18.8 20.9 %collective-permute-start.5 = (f32[5,16,16,128]{3,2,1,0:T(8,128)S(1)}, f32[5,16,16,128]{3,2,1,0:T(8,128)S(1)}, u32[]{:S(2)}, u32[]{:S(2)}) collective-permute-start(f32[5,16,16,128]{3,2,1,0:T(8,128)S(1)} %get-tuple-element.11.own), channel_id=1, source_target_pairs={{0,56},{8,0},{16,8},{24,16},{32,24},{40,32},{48,40},{56,48},{1,57}... | collective-permute-start | bytes 1966088 | tf_op jit(solution)/shard_map/ppermute | solution.py:323
  22.1 17.7 %collective-permute-start.4 = (f32[5,16,16,128]{3,2,1,0:T(8,128)S(1)}, f32[5,16,16,128]{3,2,1,0:T(8,128)S(1)}, u32[]{:S(2)}, u32[]{:S(2)}) collective-permute-start(f32[5,16,16,128]{3,2,1,0:T(8,128)S(1)} %get-tuple-element.11.own), channel_id=1, source_target_pairs={{0,8},{8,16},{16,24},{24,32},{32,40},{40,48},{48,56},{56,0},{1,9},... | collective-permute-start | bytes 1966088 | tf_op jit(solution)/shard_map/ppermute | solution.py:322
  22.1 17.6 %collective-permute-start.6 = (f32[8,24,128]{2,1,0:T(8,128)S(1)}, f32[8,24,128]{2,1,0:T(8,128)S(1)}, u32[]{:S(2)}, u32[]{:S(2)}) collective-permute-start(f32[8,24,128]{2,1,0:T(8,128)S(1)} %get-tuple-element.12), channel_id=1, source_target_pairs={{0,16},{8,24},{16,32},{24,40},{32,48},{40,56},{48,0},{56,8},{1,17}... | collective-permute-start | bytes 294920 | tf_op jit(solution)/shard_map/ppermute | solution.py:324
  22.1 17.7 %collective-permute-start.7 = (f32[8,24,128]{2,1,0:T(8,128)S(1)}, f32[8,24,128]{2,1,0:T(8,128)S(1)}, u32[]{:S(2)}, u32[]{:S(2)}) collective-permute-start(f32[8,24,128]{2,1,0:T(8,128)S(1)} %get-tuple-element.13), channel_id=1, source_target_pairs={{0,48},{8,56},{16,0},{24,8},{32,16},{40,24},{48,32},{56,40},{1,49}... | collective-permute-start | bytes 294920 | tf_op jit(solution)/shard_map/ppermute | solution.py:325
  39.7 0.6 copy-start.4
  39.7 0.7 copy-start.5
  39.7 0.9 %copy-start.2 = (f32[5,16,16,128]{3,2,1,0:T(8,128)}, f32[5,16,16,128]{3,2,1,0:T(8,128)S(1)}, u32[]{:S(2)}) copy-start(f32[5,16,16,128]{3,2,1,0:T(8,128)S(1)} %collective-permute-done.5.high) | copy-start | bytes 1966084
  40.6 0.9 %copy-start.3 = (f32[5,16,16,128]{3,2,1,0:T(8,128)}, f32[5,16,16,128]{3,2,1,0:T(8,128)S(1)}, u32[]{:S(2)}) copy-start(f32[5,16,16,128]{3,2,1,0:T(8,128)S(1)} %collective-permute-done.4.low) | copy-start | bytes 1966084
  64.8 5.6 %collective-permute-start.8 = (f32[20,4,16,128]{3,2,1,0:T(8,128)}, f32[20,4,16,128]{3,2,1,0:T(8,128)S(1)}, u32[]{:S(2)}, u32[]{:S(2)}) collective-permute-start(f32[20,4,16,128]{3,2,1,0:T(8,128)} %get-tuple-element.15), channel_id=1, source_target_pairs={{0,64},{64,0},{128,192},{192,128},{1,65},{65,1},{129,193},{193,129... | collective-permute-start | bytes 1966088 | tf_op jit(solution)/shard_map/ppermute | solution.py:333
  70.4 1.1 %copy-start.1 = (f32[20,4,16,128]{3,2,1,0:T(8,128)S(1)}, f32[20,4,16,128]{3,2,1,0:T(8,128)}, u32[]{:S(2)}) copy-start(f32[20,4,16,128]{3,2,1,0:T(8,128)} %get-tuple-element.14.mine_ref) | copy-start | bytes 1966084

commit v2 on v1

--- a/solution.py
+++ b/solution.py
@@ -39,15 +39,14 @@
 BY = 16
 LANES = 128
 EDGE = 20
+PART = 26
 GAP = 24
 ROWS = 80
 OWN = 30
 
 
 def tiles(radius):
-    low = (OWN - radius) // 8 * 8
-    high = -(-(OWN + BY + radius) // 8) * 8
-    return list(range(low, high, 8))
+    return [OWN - radius + 8 * k for k in range(-(-(BY + 2 * radius) // 8))]
 
 
 def lane_masks(core, shape):
@@ -75,19 +74,36 @@
             edge_ref[base + x] = packed
 
 
-def merge_edges(core_ref, near_ref, far_ref, near_edge, far_edge, out_ref, up_ref, down_ref):
-    _, take = lane_masks(core_ref[0], (BY, LANES))
-    for x in range(NX):
-        source, edges = (near_ref, near_edge) if x < 8 else (far_ref, far_edge)
-        edge = edges[x % 8]
-        row = (x % 2) * 12
+def spare_lanes(core, shape):
+    lane = lax.broadcasted_iota(jnp.int32, shape, len(shape) - 1)
+    start = jnp.where(core == 0, 82, 18)
+    return (lane >= start) & (lane < start + PART), lane, start
+
+
+def merge_edges(core_ref, near_ref, far_ref, other_ref, near_edge, far_edge, pack_ref, up_ref, down_ref):
+    core = core_ref[0]
+    lo, hi = core * 4, 4 - core * 4
+    _, take = lane_masks(core, (BY, LANES))
+    spare, _, _ = spare_lanes(core, (BY, LANES))
+    for n in range(NX):
+        if n < 8:
+            source, k, x, edge = near_ref, n, n, near_edge[n]
+        else:
+            source, k, base = (far_ref, n - 8, lo) if n < 12 else (other_ref, n - 12, hi)
+            x = base + 8 + n % 4
+            edge = far_edge[x - 8]
+        pair, row = (x // 2, (x % 2) * 12) if n < 8 else (lax.div(base, 2) + 4 + n % 4 // 2, (n % 2) * 12)
+        order = None
         for f in range(5):
             moved = pltpu.roll(edge, LANES - GAP * f, 1) if f else edge
-            value = jnp.where(take, moved, source[f, x % 8])
-            out_ref[f, x] = value
+            value = jnp.where(take, moved, source[f, k])
+            if f == 0:
+                order = value
+            else:
+                pack_ref[f - 1, x] = jnp.where(spare, pltpu.roll(order, LANES - PART * f, 1), value)
             count = 4 if f == 0 else 2
-            up_ref[x // 2, row : row + count, :] = value[BY - count :]
-            down_ref[x // 2, row : row + count, :] = value[:count]
+            up_ref[pair, row : row + count, :] = value[BY - count :]
+            down_ref[pair, row : row + count, :] = value[:count]
             row += count
 
 
@@ -169,13 +185,22 @@
 def steps_kernel(core_ref, own, low, high, low2, high2, mine_ref, send_ref, pops_a, pops_b, order_a, order_b, chem, rho, inv, vel):
     core = core_ref[0]
 
+    targets = (order_a, rho, vel.at[0], vel.at[1], vel.at[2])
+    _, lane, start = spare_lanes(core, (BY, LANES))
+    source_lane = lax.rem(lane - start + 2 * LANES - PART, LANES)
+
     def load(pair, _):
         for half in range(2):
             x = 2 * pair + half
-            for f, target in enumerate((order_a, rho, vel.at[0], vel.at[1], vel.at[2])):
-                target[x, pl.ds(OWN - 16, 16), :] = low[f, x]
-                target[x, pl.ds(OWN, 16), :] = own[f, x]
-                target[x, pl.ds(OWN + 16, 16), :] = high[f, x]
+            for source, row in ((low, OWN - 16), (own, OWN), (high, OWN + 16)):
+                order = None
+                for f in range(1, 5):
+                    value = source[f - 1, x]
+                    targets[f][x, pl.ds(row, 16), :] = value
+                    moved = pltpu.roll(value, PART * f, 1)
+                    order = moved if order is None else jnp.where(source_lane >= PART * (f - 1), moved, order)
+                order_a[x, pl.ds(row, 16), :] = order
+            for f, target in enumerate(targets):
                 count, row = (4, 12 * half) if f == 0 else (2, 12 * half + 2 + 2 * f)
                 target[x, pl.ds(OWN - 16 - count, count), :] = low2[pair, row : row + count, :]
                 target[x, pl.ds(OWN + 32, count), :] = high2[pair, row : row + count, :]
@@ -263,20 +288,36 @@
         order, order_next = order_next, order
         pops, pops_next = pops_next, pops
 
-    for target, base in ((mine_ref, core * 4), (send_ref, 4 - core * 4)):
-        for x in range(4):
-            for i in range(19):
-                target[i, x] = pops[i, base + x, pl.ds(OWN, 16), :] * (1.0 / 256.0)
-            target[19, x] = order[base + x, pl.ds(OWN, 16), :]
+    keep = kept_lanes(core, (BY, LANES))
+    for x in range(4):
+        for i in range(20):
+            source, scale = (order, None) if i == 19 else (pops.at[i], 1.0 / 256.0)
+            here = source[core * 4 + x, pl.ds(OWN, 16), :]
+            mine_ref[i, x] = here if scale is None else here * scale
+            there = source[4 - core * 4 + x, pl.ds(OWN, 16), :]
+            there = there if scale is None else there * scale
+            if i % 2 == 0:
+                first = there
+            else:
+                send_ref[i // 2, x] = jnp.where(keep, first, pltpu.roll(there, LANES // 2, 1))
+
+
+def kept_lanes(core, shape):
+    lane = lax.broadcasted_iota(jnp.int32, shape, len(shape) - 1)
+    first = core == 0
+    return (first & (lane < LANES // 2)) | (jnp.logical_not(first) & (lane >= LANES // 2))
 
 
 def join_halves(core_ref, mine_ref, back_ref, order_ref, pops_ref):
-    lane = lax.broadcasted_iota(jnp.int32, (4, BY, LANES), 2)
-    first = core_ref[0] == 0
-    keep = (first & (lane < LANES // 2)) | (jnp.logical_not(first) & (lane >= LANES // 2))
-    for i in range(19):
-        pops_ref[i] = jnp.where(keep, mine_ref[i], back_ref[i])
-    order_ref[...] = jnp.where(keep, mine_ref[19], back_ref[19])
+    keep = kept_lanes(core_ref[0], (BY, LANES))
+    for x in range(4):
+        for i in range(20):
+            back = back_ref[i // 2, x]
+            value = jnp.where(keep, mine_ref[i, x], pltpu.roll(back, LANES // 2, 1) if i % 2 else back)
+            if i == 19:
+                order_ref[x] = value
+            else:
+                pops_ref[i, x] = value
 
 
 def vmem_call(kernel, outs, scratch=(), limit=None):
@@ -311,26 +352,34 @@
     core = lax.rem(lax.axis_index("gx"), 2)
     core_arg = core.astype(jnp.int32).reshape(1)
     fields = jnp.concatenate([order_param[None], density[None], velocity])
-    other = lax.ppermute(fields, "gx", [(i, i ^ 1) for i in range(sizes[0])])
+    def along(value, axis, to):
+        return lax.ppermute(value, axis, [(i, to(i) % lax.axis_size(axis)) for i in range(lax.axis_size(axis))])
+
+    def swap(i):
+        return i ^ 1
+
+    other = along(fields, "gx", swap)
+    far = along(fields, "gx", lambda i: i ^ 2)
     near, edge = vmem_call(gather_pair, [(5, 8, BY, LANES), (8, BY, LANES)])(core_arg, fields, other)
-    far = lax.ppermute(near, "gx", [(i, i ^ 2) for i in range(sizes[0])])
     near_edge = send(edge, lambda x, y, z: (x ^ 1, y, z + 1 if x & 1 else z - 1))
     far_edge = send(edge, lambda x, y, z: (x ^ 3, y, z + 1 if x & 1 else z - 1))
-    whole, last_rows, first_rows = vmem_call(merge_edges, [(5, NX, BY, LANES), (8, 24, LANES), (8, 24, LANES)])(
-        core_arg, near, far, near_edge, far_edge
+    far_again, near_edge, far_edge = lax.optimization_barrier((far, near_edge, far_edge))
+    other_far = along(far_again, "gx", swap)
+    pack, last_rows, first_rows = vmem_call(merge_edges, [(4, NX, BY, LANES), (8, 24, LANES), (8, 24, LANES)])(
+        core_arg, near, far_again, other_far, near_edge, far_edge
     )
-    low = lax.ppermute(whole, "gy", [(i, (i + 1) % sizes[1]) for i in range(sizes[1])])
-    high = lax.ppermute(whole, "gy", [(i, (i - 1) % sizes[1]) for i in range(sizes[1])])
-    low2 = lax.ppermute(last_rows, "gy", [(i, (i + 2) % sizes[1]) for i in range(sizes[1])])
-    high2 = lax.ppermute(first_rows, "gy", [(i, (i - 2) % sizes[1]) for i in range(sizes[1])])
+    low = along(pack, "gy", lambda i: i + 1)
+    high = along(pack, "gy", lambda i: i - 1)
+    low2 = along(last_rows, "gy", lambda i: i + 2)
+    high2 = along(first_rows, "gy", lambda i: i - 2)
     field = (NX, ROWS, LANES)
     mine, away = vmem_call(
         steps_kernel,
-        [(20, 4, BY, LANES)] * 2,
+        [(20, 4, BY, LANES), (10, 4, BY, LANES)],
         [(19,) + field, (19,) + field, field, field, field, field, field, (3,) + field],
         60 << 20,
-    )(core_arg, whole, low, high, low2, high2)
-    back = lax.ppermute(away, "gx", [(i, i ^ 1) for i in range(sizes[0])])
+    )(core_arg, pack, low, high, low2, high2)
+    back = along(away, "gx", swap)
     return tuple(vmem_call(join_halves, [(4, BY, LANES), (19, 4, BY, LANES)])(core_arg, mine, back))
 
 

time: 73.2 us -> 69.9 us (0.955)
  waiting for transfers between devices: 25.1 us -> 18.1 us
  starting transfers between devices: 18.3 us -> 21.9 us
    ppermute x7 -> x8, waiting for transfers between devices: 22.2 us -> 18.1 us  [along(): lax.ppermute(value, axis, [(i, to(i) % lax.axis_size(axis)) for i in rang...]
    ppermute x7 -> x8, starting transfers between devices: 15.1 us -> 18.5 us  [along(): lax.ppermute(value, axis, [(i, to(i) % lax.axis_size(axis)) for i in rang...]
    ppermute x2, waiting for transfers between devices: 2.94 us -> 0.01 us  [send(): return lax.ppermute(value, AXES, pairs)]
  transfers between devices with their start and end apart: 9 -> 10, of which waited for: 5 -> 4; matrix products, arithmetic and copies ran while one was open for 0% -> 0% of each run, Pallas kernels for 0% -> 0%
where the time goes in v2:
time: 69.9 us; the launch traced here: 69.2 us
  Pallas kernels  24.9 us (36%)
  starting transfers between devices  21.9 us (31%)
  waiting for transfers between devices  18.1 us (26%)
  local copies, waits for them, and re-layouts  2.76 us (4%)
  other arithmetic  0.93 us (1%)
  between operations  0.7 us (1%)
    pallas_call x4, Pallas kernels, call(): pl.pallas_call(kernel, out_shape=[jax.ShapeDtypeStruct(s, F32) for s in o...  24.9 us
    ppermute x8, starting transfers between devices, along(): lax.ppermute(value, axis, [(i, to(i) % lax.axis_size(axis)) for i in rang...  18.5 us
    ppermute x8, waiting for transfers between devices, along(): lax.ppermute(value, axis, [(i, to(i) % lax.axis_size(axis)) for i in rang...  18.1 us
    ppermute x2, starting transfers between devices, send(): return lax.ppermute(value, AXES, pairs)  3.34 us
    unnamed x12, local copies, waits for them, and re-layouts  2.76 us
  transfers between devices with their start and end apart: 10, of which 4 were waited for; matrix products, arithmetic and copies ran while one was open for 0% of the time, Pallas kernels for 0%

profile of v2, /device:TPU:1, one launch (start us, length us, event | category | flops | bytes accessed | tf_op | source)
XLA Modules:
  0.0 69.2 jit_solution(5788621622366029938)
XLA Ops:
  0.6 0.9 %pad_maximum_fusion.mine_ref = f32[5,4,16,128]{3,2,1,0:T(8,128)S(1)} fusion(f32[3,4,16,128]{3,2,1,0:T(8,128)} %param.5, f32[1,4,16,128]{3,2,1,0:T(8,128)} %bitcast.3, f32[1,4,16,128]{3,2,1,0:T(8,128)} %bitcast.4), kind=kLoop, calls=%fused_computation | loop fusion | flops 81920 | bytes 327680 | tf_op jit(solution)/shard_map/concatenate | solution.py:354
  1.6 3.3 %collective-permute-start = (f32[5,4,16,128]{3,2,1,0:T(8,128)S(1)}, f32[5,4,16,128]{3,2,1,0:T(8,128)S(1)}, u32[]{:S(2)}, u32[]{:S(2)}) collective-permute-start(f32[5,4,16,128]{3,2,1,0:T(8,128)S(1)} %pad_maximum_fusion.mine_ref), channel_id=1, source_target_pairs={{0,64},{64,0},{128,192},{192,128},{1,65},{65,1},{129,193},{193,129... | collective-permute-start | bytes 491528 | tf_op jit(solution)/shard_map/ppermute | solution.py:356
  4.9 1.2 %collective-permute-start.1 = (f32[5,4,16,128]{3,2,1,0:T(8,128)S(1)}, f32[5,4,16,128]{3,2,1,0:T(8,128)S(1)}, u32[]{:S(2)}, u32[]{:S(2)}) collective-permute-start(f32[5,4,16,128]{3,2,1,0:T(8,128)S(1)} %pad_maximum_fusion.mine_ref), channel_id=1, source_target_pairs={{0,128},{64,192},{128,0},{192,64},{1,129},{65,193},{129,1},{193,65... | collective-permute-start | bytes 491528 | tf_op jit(solution)/shard_map/ppermute | solution.py:356
  6.1 0.0 collective-permute-done.other_ref
  6.1 0.1 shard_map.50
  6.2 2.3 %collective-permute-start.3 = (f32[8,16,128]{2,1,0:T(8,128)S(1)}, f32[8,16,128]{2,1,0:T(8,128)S(1)}, u32[]{:S(2)}, u32[]{:S(2)}) collective-permute-start(f32[8,16,128]{2,1,0:T(8,128)S(1)} %get-tuple-element.13), channel_id=1, source_target_pairs={{0,199},{1,192},{2,193},{3,194},{4,195},{5,196},{6,197},{7,198},{8... | collective-permute-start | bytes 196616 | tf_op jit(solution)/shard_map/ppermute | solution.py:350
  8.5 1.1 %collective-permute-start.2 = (f32[8,16,128]{2,1,0:T(8,128)S(1)}, f32[8,16,128]{2,1,0:T(8,128)S(1)}, u32[]{:S(2)}, u32[]{:S(2)}) collective-permute-start(f32[8,16,128]{2,1,0:T(8,128)S(1)} %get-tuple-element.13), channel_id=1, source_target_pairs={{0,71},{1,64},{2,65},{3,66},{4,67},{5,68},{6,69},{7,70},{8,79},{9,... | collective-permute-start | bytes 196616 | tf_op jit(solution)/shard_map/ppermute | solution.py:350
  9.6 3.3 %collective-permute-done.1.far_ref = f32[5,4,16,128]{3,2,1,0:T(8,128)S(1)} collective-permute-done((f32[5,4,16,128]{3,2,1,0:T(8,128)S(1)}, f32[5,4,16,128]{3,2,1,0:T(8,128)S(1)}, u32[]{:S(2)}, u32[]{:S(2)}) %collective-permute-start.1) | collective-permute-done | bytes 163872 | tf_op jit(solution)/shard_map/ppermute | solution.py:356
  12.9 0.0 collective-permute-done.3.far_edge
  12.9 0.0 collective-permute-done.2.near_edge
  12.9 2.7 %collective-permute-start.4 = (f32[5,4,16,128]{3,2,1,0:T(8,128)S(1)}, f32[5,4,16,128]{3,2,1,0:T(8,128)S(1)}, u32[]{:S(2)}, u32[]{:S(2)}) collective-permute-start(f32[5,4,16,128]{3,2,1,0:T(8,128)S(1)} %collective-permute-done.1.far_ref), channel_id=1, source_target_pairs={{0,64},{64,0},{128,192},{192,128},{1,65},{65,1},{129,193},{193,129... | collective-permute-start | bytes 491528 | tf_op jit(solution)/shard_map/ppermute | solution.py:356
  15.5 1.0 %collective-permute-done.4.other_ref = f32[5,4,16,128]{3,2,1,0:T(8,128)S(1)} collective-permute-done((f32[5,4,16,128]{3,2,1,0:T(8,128)S(1)}, f32[5,4,16,128]{3,2,1,0:T(8,128)S(1)}, u32[]{:S(2)}, u32[]{:S(2)}) %collective-permute-start.4) | collective-permute-done | bytes 163872 | tf_op jit(solution)/shard_map/ppermute | solution.py:356
  16.6 0.3 shard_map.51
  16.9 0.0 copy-start.1
  16.9 5.7 %collective-permute-start.6 = (f32[4,16,16,128]{3,2,1,0:T(8,128)S(1)}, f32[4,16,16,128]{3,2,1,0:T(8,128)S(1)}, u32[]{:S(2)}, u32[]{:S(2)}) collective-permute-start(f32[4,16,16,128]{3,2,1,0:T(8,128)S(1)} %get-tuple-element.17.own), channel_id=1, source_target_pairs={{0,56},{8,0},{16,8},{24,16},{32,24},{40,32},{48,40},{56,48},{1,57}... | collective-permute-start | bytes 1572872 | tf_op jit(solution)/shard_map/ppermute | solution.py:356
  22.6 0.0 collective-permute-start.5
  22.6 0.0 collective-permute-start.7
  22.6 3.6 %collective-permute-start.8 = (f32[8,24,128]{2,1,0:T(8,128)S(1)}, f32[8,24,128]{2,1,0:T(8,128)S(1)}, u32[]{:S(2)}, u32[]{:S(2)}) collective-permute-start(f32[8,24,128]{2,1,0:T(8,128)S(1)} %get-tuple-element.19), channel_id=1, source_target_pairs={{0,48},{8,56},{16,0},{24,8},{32,16},{40,24},{48,32},{56,40},{1,49}... | collective-permute-start | bytes 294920 | tf_op jit(solution)/shard_map/ppermute | solution.py:356
  26.2 12.3 %collective-permute-done.7.low2 = f32[8,24,128]{2,1,0:T(8,128)S(1)} collective-permute-done((f32[8,24,128]{2,1,0:T(8,128)S(1)}, f32[8,24,128]{2,1,0:T(8,128)S(1)}, u32[]{:S(2)}, u32[]{:S(2)}) %collective-permute-start.7) | collective-permute-done | bytes 98336 | tf_op jit(solution)/shard_map/ppermute | solution.py:356
  38.4 0.0 copy-start.4
  38.4 0.0 collective-permute-done.8.high2
  38.4 0.0 copy-start.5
  38.4 0.0 collective-permute-done.6.high
  38.4 0.0 copy-start.2
  38.5 0.0 collective-permute-done.5.low
  38.5 0.0 copy-done.1
  38.5 0.6 copy-done.4
  39.1 0.0 copy-done.5
  39.1 0.2 copy-done.2
  39.3 0.0 copy-start.3
  39.3 0.8 %copy-done.3 = f32[4,16,16,128]{3,2,1,0:T(8,128)} copy-done((f32[4,16,16,128]{3,2,1,0:T(8,128)}, f32[4,16,16,128]{3,2,1,0:T(8,128)S(1)}, u32[]{:S(2)}) %copy-start.3) | copy-done | bytes 524312
  40.1 23.4 %shard_map.52 = (f32[20,4,16,128]{3,2,1,0:T(8,128)}, f32[10,4,16,128]{3,2,1,0:T(8,128)}) custom-call(s32[1]{0:T(128)} %bitcast.core_ref, f32[4,16,16,128]{3,2,1,0:T(8,128)} %copy-done.1, f32[4,16,16,128]{3,2,1,0:T(8,128)} %copy-done.3, f32[4,16,16,128]{3,2,1,0:T(8,128)} %copy-done.2, f32[8,24,128]{2,1,0:T(8,128)} %copy-done.4, f32[8,24,128]{2,1,0:T(8,128)} %copy-done.5), custom_call_target="tpu_custom_call" | custom-call | tf_op jit(solution)/shard_map/pallas_call | solution.py:327
  63.6 2.1 %collective-permute-start.9 = (f32[10,4,16,128]{3,2,1,0:T(8,128)}, f32[10,4,16,128]{3,2,1,0:T(8,128)S(1)}, u32[]{:S(2)}, u32[]{:S(2)}) collective-permute-start(f32[10,4,16,128]{3,2,1,0:T(8,128)} %get-tuple-element.21), channel_id=1, source_target_pairs={{0,64},{64,0},{128,192},{192,128},{1,65},{65,1},{129,193},{193,129... | collective-permute-start | bytes 983048 | tf_op jit(solution)/shard_map/ppermute | solution.py:356
  65.7 1.5 %collective-permute-done.9.back_ref = f32[10,4,16,128]{3,2,1,0:T(8,128)S(1)} collective-permute-done((f32[10,4,16,128]{3,2,1,0:T(8,128)}, f32[10,4,16,128]{3,2,1,0:T(8,128)S(1)}, u32[]{:S(2)}, u32[]{:S(2)}) %collective-permute-start.9) | collective-permute-done | bytes 327712 | tf_op jit(solution)/shard_map/ppermute | solution.py:356
  67.2 0.0 copy-start
  67.2 1.1 %copy-done = f32[20,4,16,128]{3,2,1,0:T(8,128)S(1)} copy-done((f32[20,4,16,128]{3,2,1,0:T(8,128)S(1)}, f32[20,4,16,128]{3,2,1,0:T(8,128)}, u32[]{:S(2)}) %copy-start) | copy-done | bytes 655384
  68.2 1.0 %shard_map.53 = (f32[4,16,128]{2,1,0:T(8,128)}, f32[19,4,16,128]{3,2,1,0:T(8,128)}) custom-call(s32[1]{0:T(128)} %bitcast.core_ref, f32[20,4,16,128]{3,2,1,0:T(8,128)S(1)} %copy-done, f32[10,4,16,128]{3,2,1,0:T(8,128)S(1)} %collective-permute-done.9.back_ref), custom_call_target="tpu_custom_call" | custom-call | tf_op jit(solution)/shard_map/pallas_call | solution.py:327
Async XLA Ops:
  1.6 4.5 %collective-permute-start = (f32[5,4,16,128]{3,2,1,0:T(8,128)S(1)}, f32[5,4,16,128]{3,2,1,0:T(8,128)S(1)}, u32[]{:S(2)}, u32[]{:S(2)}) collective-permute-start(f32[5,4,16,128]{3,2,1,0:T(8,128)S(1)} %pad_maximum_fusion.mine_ref), channel_id=1, source_target_pairs={{0,64},{64,0},{128,192},{192,128},{1,65},{65,1},{129,193},{193,129... | collective-permute-start | bytes 491528 | tf_op jit(solution)/shard_map/ppermute | solution.py:356
  4.9 8.0 %collective-permute-start.1 = (f32[5,4,16,128]{3,2,1,0:T(8,128)S(1)}, f32[5,4,16,128]{3,2,1,0:T(8,128)S(1)}, u32[]{:S(2)}, u32[]{:S(2)}) collective-permute-start(f32[5,4,16,128]{3,2,1,0:T(8,128)S(1)} %pad_maximum_fusion.mine_ref), channel_id=1, source_target_pairs={{0,128},{64,192},{128,0},{192,64},{1,129},{65,193},{129,1},{193,65... | collective-permute-start | bytes 491528 | tf_op jit(solution)/shard_map/ppermute | solution.py:356
  6.2 6.6 %collective-permute-start.3 = (f32[8,16,128]{2,1,0:T(8,128)S(1)}, f32[8,16,128]{2,1,0:T(8,128)S(1)}, u32[]{:S(2)}, u32[]{:S(2)}) collective-permute-start(f32[8,16,128]{2,1,0:T(8,128)S(1)} %get-tuple-element.13), channel_id=1, source_target_pairs={{0,199},{1,192},{2,193},{3,194},{4,195},{5,196},{6,197},{7,198},{8... | collective-permute-start | bytes 196616 | tf_op jit(solution)/shard_map/ppermute | solution.py:350
  8.5 4.4 %collective-permute-start.2 = (f32[8,16,128]{2,1,0:T(8,128)S(1)}, f32[8,16,128]{2,1,0:T(8,128)S(1)}, u32[]{:S(2)}, u32[]{:S(2)}) collective-permute-start(f32[8,16,128]{2,1,0:T(8,128)S(1)} %get-tuple-element.13), channel_id=1, source_target_pairs={{0,71},{1,64},{2,65},{3,66},{4,67},{5,68},{6,69},{7,70},{8,79},{9,... | collective-permute-start | bytes 196616 | tf_op jit(solution)/shard_map/ppermute | solution.py:350
  12.9 3.7 %collective-permute-start.4 = (f32[5,4,16,128]{3,2,1,0:T(8,128)S(1)}, f32[5,4,16,128]{3,2,1,0:T(8,128)S(1)}, u32[]{:S(2)}, u32[]{:S(2)}) collective-permute-start(f32[5,4,16,128]{3,2,1,0:T(8,128)S(1)} %collective-permute-done.1.far_ref), channel_id=1, source_target_pairs={{0,64},{64,0},{128,192},{192,128},{1,65},{65,1},{129,193},{193,129... | collective-permute-start | bytes 491528 | tf_op jit(solution)/shard_map/ppermute | solution.py:356
  16.9 21.6 %copy-start.1 = (f32[4,16,16,128]{3,2,1,0:T(8,128)}, f32[4,16,16,128]{3,2,1,0:T(8,128)S(1)}, u32[]{:S(2)}) copy-start(f32[4,16,16,128]{3,2,1,0:T(8,128)S(1)} %get-tuple-element.17.own) | copy-start | bytes 1572868
  16.9 21.5 %collective-permute-start.6 = (f32[4,16,16,128]{3,2,1,0:T(8,128)S(1)}, f32[4,16,16,128]{3,2,1,0:T(8,128)S(1)}, u32[]{:S(2)}, u32[]{:S(2)}) collective-permute-start(f32[4,16,16,128]{3,2,1,0:T(8,128)S(1)} %get-tuple-element.17.own), channel_id=1, source_target_pairs={{0,56},{8,0},{16,8},{24,16},{32,24},{40,32},{48,40},{56,48},{1,57}... | collective-permute-start | bytes 1572872 | tf_op jit(solution)/shard_map/ppermute | solution.py:356
  22.6 15.9 %collective-permute-start.5 = (f32[4,16,16,128]{3,2,1,0:T(8,128)S(1)}, f32[4,16,16,128]{3,2,1,0:T(8,128)S(1)}, u32[]{:S(2)}, u32[]{:S(2)}) collective-permute-start(f32[4,16,16,128]{3,2,1,0:T(8,128)S(1)} %get-tuple-element.17.own), channel_id=1, source_target_pairs={{0,8},{8,16},{16,24},{24,32},{32,40},{40,48},{48,56},{56,0},{1,9},... | collective-permute-start | bytes 1572872 | tf_op jit(solution)/shard_map/ppermute | solution.py:356
  22.6 15.9 %collective-permute-start.7 = (f32[8,24,128]{2,1,0:T(8,128)S(1)}, f32[8,24,128]{2,1,0:T(8,128)S(1)}, u32[]{:S(2)}, u32[]{:S(2)}) collective-permute-start(f32[8,24,128]{2,1,0:T(8,128)S(1)} %get-tuple-element.18), channel_id=1, source_target_pairs={{0,16},{8,24},{16,32},{24,40},{32,48},{40,56},{48,0},{56,8},{1,17}... | collective-permute-start | bytes 294920 | tf_op jit(solution)/shard_map/ppermute | solution.py:356
  22.6 15.9 %collective-permute-start.8 = (f32[8,24,128]{2,1,0:T(8,128)S(1)}, f32[8,24,128]{2,1,0:T(8,128)S(1)}, u32[]{:S(2)}, u32[]{:S(2)}) collective-permute-start(f32[8,24,128]{2,1,0:T(8,128)S(1)} %get-tuple-element.19), channel_id=1, source_target_pairs={{0,48},{8,56},{16,0},{24,8},{32,16},{40,24},{48,32},{56,40},{1,49}... | collective-permute-start | bytes 294920 | tf_op jit(solution)/shard_map/ppermute | solution.py:356
  38.4 0.6 copy-start.4
  38.4 0.7 copy-start.5
  38.4 0.9 %copy-start.2 = (f32[4,16,16,128]{3,2,1,0:T(8,128)}, f32[4,16,16,128]{3,2,1,0:T(8,128)S(1)}, u32[]{:S(2)}) copy-start(f32[4,16,16,128]{3,2,1,0:T(8,128)S(1)} %collective-permute-done.6.high) | copy-start | bytes 1572868
  39.3 0.8 %copy-start.3 = (f32[4,16,16,128]{3,2,1,0:T(8,128)}, f32[4,16,16,128]{3,2,1,0:T(8,128)S(1)}, u32[]{:S(2)}) copy-start(f32[4,16,16,128]{3,2,1,0:T(8,128)S(1)} %collective-permute-done.5.low) | copy-start | bytes 1572868
  63.6 3.6 %collective-permute-start.9 = (f32[10,4,16,128]{3,2,1,0:T(8,128)}, f32[10,4,16,128]{3,2,1,0:T(8,128)S(1)}, u32[]{:S(2)}, u32[]{:S(2)}) collective-permute-start(f32[10,4,16,128]{3,2,1,0:T(8,128)} %get-tuple-element.21), channel_id=1, source_target_pairs={{0,64},{64,0},{128,192},{192,128},{1,65},{65,1},{129,193},{193,129... | collective-permute-start | bytes 983048 | tf_op jit(solution)/shard_map/ppermute | solution.py:356
  67.2 1.1 %copy-start = (f32[20,4,16,128]{3,2,1,0:T(8,128)S(1)}, f32[20,4,16,128]{3,2,1,0:T(8,128)}, u32[]{:S(2)}) copy-start(f32[20,4,16,128]{3,2,1,0:T(8,128)} %get-tuple-element.20.mine_ref) | copy-start | bytes 1966084

commit v3 on v2

--- a/solution.py
+++ b/solution.py
@@ -41,7 +41,7 @@
 EDGE = 20
 PART = 26
 GAP = 24
-ROWS = 80
+ROWS = 72
 OWN = 30
 
 
@@ -182,10 +182,92 @@
     return rho, (mx, my, mz)
 
 
-def steps_kernel(core_ref, own, low, high, low2, high2, mine_ref, send_ref, pops_a, pops_b, order_a, order_b, chem, rho, inv, vel):
+class Passes:
+    def __init__(self, pops, order, chem, rho, inv, vel):
+        self.pops, self.orders, self.chems, self.rho, self.inv, self.vel = pops, order, chem, rho, inv, vel
+
+    def run(self, first, count, names, offset=None, unroll=1):
+        behind = {"collide": 0, "flow": -3, "order": -6, "chem": 3}
+
+        def body(n, _):
+            for name, step in names:
+                shift = behind[name] - 12 * step if offset is None else offset
+                x = (n + shift) & (NX - 1)
+                getattr(self, name)(step, x, (x + 1) & (NX - 1), (x - 1) & (NX - 1))
+            return 0
+
+        lax.fori_loop(first, first + count, body, 0, unroll=unroll)
+
+    def left(self, step):
+        return 4 * (ITERS - 1 - step)
+
+    def chem(self, step, x, up, down):
+        order, chem = self.orders[step % 2], self.chems[step % 2]
+        for r in tiles(self.left(step) + 3):
+            here = order[x, pl.ds(r, 8), :]
+            beside = (order[up, pl.ds(r, 8), :] + order[down, pl.ds(r, 8), :]) + (
+                order[x, pl.ds(r + 1, 8), :] + order[x, pl.ds(r - 1, 8), :]
+            )
+            beside = beside + (next_lane(here) + prev_lane(here))
+            chem[x, pl.ds(r, 8), :] = here * ((quadratic + 6.0 * stiffness) + quartic * (here * here)) - stiffness * beside
+
+    def collide(self, step, x, up, down):
+        order, chem = self.orders[step % 2], self.chems[step % 2]
+        was = (step - 1) % 2
+        rho, inv, vel, old, new = self.rho[was], self.inv[was], self.vel[was], self.pops[was], self.pops[1 - was]
+        to = {0: x, 1: up, -1: down}
+        for r in tiles(self.left(step) + 2):
+            at = pl.ds(r, 8)
+            mu = chem[x, at, :]
+            density = rho[x, at, :]
+            inverse = 1.0 / density if step == 0 else inv[x, at, :]
+            pull = ((-0.5 * (-4.0) ** max(step - 1, 0)) * order[x, at, :]) * inverse
+            kick = [
+                pull * (chem[up, at, :] - chem[down, at, :]),
+                pull * (chem[x, pl.ds(r + 1, 8), :] - chem[x, pl.ds(r - 1, 8), :]),
+                pull * (next_lane(mu) - prev_lane(mu)),
+            ]
+            before = None if step == 0 else (lambda i: old[i, x, at, :])
+            post = collide(density, [vel[d, x, at, :] for d in range(3)], kick, before)
+            for i in range(19):
+                cx, cy, cz = DIRECTIONS[i]
+                value = post[i]
+                if cz:
+                    value = prev_lane(value) if cz == 1 else next_lane(value)
+                new[i, to[cx], pl.ds(r + cy, 8), :] = value
+
+    def flow(self, step, x, up, down):
+        now = step % 2
+        for r in tiles(self.left(step) + 1):
+            at = pl.ds(r, 8)
+            total, moms = moments([self.pops[now][i, x, at, :] for i in range(19)])
+            inverse = 1.0 / total
+            self.rho[now][x, at, :] = total
+            self.inv[now][x, at, :] = inverse
+            for d in range(3):
+                self.vel[now][d, x, at, :] = moms[d] * inverse
+
+    def order(self, step, x, up, down):
+        now = step % 2
+        order, chem, vel = self.orders[now], self.chems[now], self.vel[now]
+        for r in tiles(self.left(step)):
+            at, north, south = pl.ds(r, 8), pl.ds(r + 1, 8), pl.ds(r - 1, 8)
+            here = order[x, at, :]
+            mu = chem[x, at, :]
+            ux, uy, uz = (vel[d, x, at, :] for d in range(3))
+            total = (ux + vel[0, up, at, :]) * (here + order[up, at, :])
+            total = total - (ux + vel[0, down, at, :]) * (here + order[down, at, :])
+            total = total + (uy + vel[1, x, north, :]) * (here + order[x, north, :])
+            total = total - (uy + vel[1, x, south, :]) * (here + order[x, south, :])
+            spread = (chem[up, at, :] + chem[down, at, :]) + (chem[x, north, :] + chem[x, south, :]) - 4.0 * mu
+            face = (0.25 * (uz + next_lane(uz))) * (here + next_lane(here)) - mobility * (next_lane(mu) - mu)
+            self.orders[1 - now][x, at, :] = here - ((0.25 * total - mobility * spread) + (face - prev_lane(face)))
+
+
+def steps_kernel(core_ref, own, low, high, low2, high2, mine_ref, send_ref, pops_a, pops_b, order_a, order_b, chem_a, chem_b, rho_a, rho_b, inv_a, inv_b, vel_a, vel_b):
     core = core_ref[0]
 
-    targets = (order_a, rho, vel.at[0], vel.at[1], vel.at[2])
+    targets = (order_a, rho_b, vel_b.at[0], vel_b.at[1], vel_b.at[2])
     _, lane, start = spare_lanes(core, (BY, LANES))
     source_lane = lax.rem(lane - start + 2 * LANES - PART, LANES)
 
@@ -208,85 +290,28 @@
 
     lax.fori_loop(0, NX // 2, load, 0)
 
-    order, order_next = order_a, order_b
-    pops, pops_next = pops_a, pops_b
-    for step in range(ITERS):
-        left = 4 * (ITERS - 1 - step)
-        last = step == ITERS - 1
-
-        def chem_of(n, _, order=order, left=left, first=-3 if last else 0):
-            x = (n + first) & 15
-            up, down = (x + 1) & 15, (x - 1) & 15
-            for r in tiles(left + 3):
-                here = order[x, pl.ds(r, 8), :]
-                beside = (order[up, pl.ds(r, 8), :] + order[down, pl.ds(r, 8), :]) + (
-                    order[x, pl.ds(r + 1, 8), :] + order[x, pl.ds(r - 1, 8), :]
-                )
-                beside = beside + (next_lane(here) + prev_lane(here))
-                chem[x, pl.ds(r, 8), :] = here * ((quadratic + 6.0 * stiffness) + quartic * (here * here)) - stiffness * beside
-            return 0
-
-        lax.fori_loop(0, 14 if last else 16, chem_of, 0, unroll=4)
-
-        def collide_of(n, _, step=step, order=order, pops=pops, pops_next=pops_next, left=left, first=-2 if last else 0):
-            x = (n + first) & 15
-            up, down = (x + 1) & 15, (x - 1) & 15
-            to = {0: x, 1: up, -1: down}
-            for r in tiles(left + 2):
-                at = pl.ds(r, 8)
-                mu = chem[x, at, :]
-                density = rho[x, at, :]
-                inverse = 1.0 / density if step == 0 else inv[x, at, :]
-                pull = ((-0.5 * (-4.0) ** max(step - 1, 0)) * order[x, at, :]) * inverse
-                kick = [
-                    pull * (chem[up, at, :] - chem[down, at, :]),
-                    pull * (chem[x, pl.ds(r + 1, 8), :] - chem[x, pl.ds(r - 1, 8), :]),
-                    pull * (next_lane(mu) - prev_lane(mu)),
-                ]
-                old = None if step == 0 else (lambda i: pops[i, x, at, :])
-                post = collide(density, [vel[d, x, at, :] for d in range(3)], kick, old)
-                for i in range(19):
-                    cx, cy, cz = DIRECTIONS[i]
-                    value = post[i]
-                    if cz:
-                        value = prev_lane(value) if cz == 1 else next_lane(value)
-                    pops_next[i, to[cx], pl.ds(r + cy, 8), :] = value
-            return 0
-
-        lax.fori_loop(0, 12 if last else 16, collide_of, 0, unroll=2)
-
-        def flow_of(n, _, pops_next=pops_next, left=left, first=-1 if last else 0):
-            x = (n + first) & 15
-            for r in tiles(left + 1):
-                at = pl.ds(r, 8)
-                total, moms = moments([pops_next[i, x, at, :] for i in range(19)])
-                inverse = 1.0 / total
-                rho[x, at, :] = total
-                inv[x, at, :] = inverse
-                for d in range(3):
-                    vel[d, x, at, :] = moms[d] * inverse
-            return 0
-
-        lax.fori_loop(0, 10 if last else 16, flow_of, 0, unroll=2)
-
-        def order_of(x, _, order=order, order_next=order_next, left=left):
-            up, down = (x + 1) & 15, (x - 1) & 15
-            for r in tiles(left):
-                at, north, south = pl.ds(r, 8), pl.ds(r + 1, 8), pl.ds(r - 1, 8)
-                here = order[x, at, :]
-                mu = chem[x, at, :]
-                ux, uy, uz = (vel[d, x, at, :] for d in range(3))
-                total = (ux + vel[0, up, at, :]) * (here + order[up, at, :]) - (ux + vel[0, down, at, :]) * (here + order[down, at, :])
-                total = total + (uy + vel[1, x, north, :]) * (here + order[x, north, :])
-                total = total - (uy + vel[1, x, south, :]) * (here + order[x, south, :])
-                spread = (chem[up, at, :] + chem[down, at, :]) + (chem[x, north, :] + chem[x, south, :]) - 4.0 * mu
-                face = (0.25 * (uz + next_lane(uz))) * (here + next_lane(here)) - mobility * (next_lane(mu) - mu)
-                order_next[x, at, :] = here - ((0.25 * total - mobility * spread) + (face - prev_lane(face)))
-            return 0
-
-        lax.fori_loop(0, 8 if last else 16, order_of, 0, unroll=4)
-        order, order_next = order_next, order
-        pops, pops_next = pops_next, pops
+    passes = Passes((pops_a, pops_b), (order_a, order_b), (chem_a, chem_b), (rho_a, rho_b), (inv_a, inv_b), (vel_a, vel_b))
+    run = passes.run
+    run(0, NX, [("chem", 0)], offset=0, unroll=4)
+    for step in range(ITERS - 1):
+        start = 16 * step
+        early = step > 0
+        run(start, 4, [("collide", step)] + [("chem", step), ("order", step - 1), ("flow", step - 1)] * early)
+        run(start + 4, 4, [("flow", step), ("collide", step)] + [("chem", step), ("order", step - 1)] * early)
+        run(start + 8, 4, [("order", step), ("flow", step), ("collide", step)] + [("chem", step)] * early)
+        run(start + 12, 4, [("chem", step + 1), ("order", step), ("flow", step), ("collide", step)])
+    step = ITERS - 1
+    start = 16 * step
+    run(start, 4, [("collide", step), ("chem", step), ("order", step - 1), ("flow", step - 1)])
+    run(start + 4, 4, [("flow", step), ("collide", step), ("chem", step), ("order", step - 1)])
+    run(start + 8, 2, [("flow", step), ("collide", step), ("chem", step)])
+    run(start + 10, 2, [("chem", step)], unroll=2)
+    run(14, 2, [("collide", step)], offset=0, unroll=2)
+    run(7, 2, [("flow", step)], offset=0, unroll=2)
+    run(15, 2, [("flow", step)], offset=0, unroll=2)
+    run(0, 8, [("order", step)], offset=0, unroll=4)
+    pops = (pops_a, pops_b)[step % 2]
+    order = (order_a, order_b)[ITERS % 2]
 
     keep = kept_lanes(core, (BY, LANES))
     for x in range(4):
@@ -334,6 +359,16 @@
         )(core, *args)
 
     return call
+
+
+def make_steps():
+    field = (NX, ROWS, LANES)
+    return vmem_call(
+        steps_kernel,
+        [(20, 4, BY, LANES), (10, 4, BY, LANES)],
+        [(19,) + field] * 2 + [field] * 8 + [(3,) + field] * 2,
+        40 << 20,
+    )
 
 
 def on_device(order_param, density, velocity):
@@ -372,13 +407,7 @@
     high = along(pack, "gy", lambda i: i - 1)
     low2 = along(last_rows, "gy", lambda i: i + 2)
     high2 = along(first_rows, "gy", lambda i: i - 2)
-    field = (NX, ROWS, LANES)
-    mine, away = vmem_call(
-        steps_kernel,
-        [(20, 4, BY, LANES), (10, 4, BY, LANES)],
-        [(19,) + field, (19,) + field, field, field, field, field, field, (3,) + field],
-        60 << 20,
-    )(core_arg, pack, low, high, low2, high2)
+    mine, away = make_steps()(core_arg, pack, low, high, low2, high2)
     back = along(away, "gx", swap)
     return tuple(vmem_call(join_halves, [(4, BY, LANES), (19, 4, BY, LANES)])(core_arg, mine, back))
 

time: 69.9 us -> 64.7 us (0.926)
  local copies, waits for them, and re-layouts: 2.76 us -> 0 us
  Pallas kernels: 24.9 us -> 22.5 us
  starting transfers between devices: 21.9 us -> 22.7 us
    unnamed x12 -> x0, local copies, waits for them, and re-layouts: 2.76 us -> none
    pallas_call x4, Pallas kernels: 24.9 us -> 22.5 us  [call(): pl.pallas_call(kernel, out_shape=[jax.ShapeDtypeStruct(s, F32) for s in o...]
    ppermute x8, starting transfers between devices: 18.5 us -> 19.3 us  [along(): lax.ppermute(value, axis, [(i, to(i) % lax.axis_size(axis)) for i in rang...]
where the time goes in v3:
time: 64.7 us; the launch traced here: 64.6 us
  starting transfers between devices  22.7 us (35%)
  Pallas kernels  22.5 us (35%)
  waiting for transfers between devices  17.9 us (28%)
  other arithmetic  0.93 us (1%)
  between operations  0.67 us (1%)
    pallas_call x4, Pallas kernels, call(): pl.pallas_call(kernel, out_shape=[jax.ShapeDtypeStruct(s, F32) for s in o...  22.5 us
    ppermute x8, starting transfers between devices, along(): lax.ppermute(value, axis, [(i, to(i) % lax.axis_size(axis)) for i in rang...  19.3 us
    ppermute x8, waiting for transfers between devices, along(): lax.ppermute(value, axis, [(i, to(i) % lax.axis_size(axis)) for i in rang...  17.9 us
    ppermute x2, starting transfers between devices, send(): return lax.ppermute(value, AXES, pairs)  3.34 us
  transfers between devices with their start and end apart: 10, of which 4 were waited for; matrix products, arithmetic and copies ran while one was open for 0% of the time, Pallas kernels for 0%

profile of v3, /device:TPU:1, one launch (start us, length us, event | category | flops | bytes accessed | tf_op | source)
XLA Modules:
  0.0 64.6 jit_solution(16069838400209464355)
XLA Ops:
  0.6 0.9 %pad_maximum_fusion.mine_ref = f32[5,4,16,128]{3,2,1,0:T(8,128)S(1)} fusion(f32[3,4,16,128]{3,2,1,0:T(8,128)} %param.5, f32[1,4,16,128]{3,2,1,0:T(8,128)} %bitcast.3, f32[1,4,16,128]{3,2,1,0:T(8,128)} %bitcast.4), kind=kLoop, calls=%fused_computation | loop fusion | flops 81920 | bytes 327680 | tf_op jit(solution)/shard_map/concatenate | solution.py:389
  1.6 3.3 %collective-permute-start = (f32[5,4,16,128]{3,2,1,0:T(8,128)S(1)}, f32[5,4,16,128]{3,2,1,0:T(8,128)S(1)}, u32[]{:S(2)}, u32[]{:S(2)}) collective-permute-start(f32[5,4,16,128]{3,2,1,0:T(8,128)S(1)} %pad_maximum_fusion.mine_ref), channel_id=1, source_target_pairs={{0,64},{64,0},{128,192},{192,128},{1,65},{65,1},{129,193},{193,129... | collective-permute-start | bytes 491528 | tf_op jit(solution)/shard_map/ppermute | solution.py:391
  4.9 1.2 %collective-permute-start.1 = (f32[5,4,16,128]{3,2,1,0:T(8,128)S(1)}, f32[5,4,16,128]{3,2,1,0:T(8,128)S(1)}, u32[]{:S(2)}, u32[]{:S(2)}) collective-permute-start(f32[5,4,16,128]{3,2,1,0:T(8,128)S(1)} %pad_maximum_fusion.mine_ref), channel_id=1, source_target_pairs={{0,128},{64,192},{128,0},{192,64},{1,129},{65,193},{129,1},{193,65... | collective-permute-start | bytes 491528 | tf_op jit(solution)/shard_map/ppermute | solution.py:391
  6.1 0.0 collective-permute-done.other_ref
  6.1 0.1 shard_map.50
  6.2 2.3 %collective-permute-start.3 = (f32[8,16,128]{2,1,0:T(8,128)S(1)}, f32[8,16,128]{2,1,0:T(8,128)S(1)}, u32[]{:S(2)}, u32[]{:S(2)}) collective-permute-start(f32[8,16,128]{2,1,0:T(8,128)S(1)} %get-tuple-element.13), channel_id=1, source_target_pairs={{0,199},{1,192},{2,193},{3,194},{4,195},{5,196},{6,197},{7,198},{8... | collective-permute-start | bytes 196616 | tf_op jit(solution)/shard_map/ppermute | solution.py:385
  8.5 1.1 %collective-permute-start.2 = (f32[8,16,128]{2,1,0:T(8,128)S(1)}, f32[8,16,128]{2,1,0:T(8,128)S(1)}, u32[]{:S(2)}, u32[]{:S(2)}) collective-permute-start(f32[8,16,128]{2,1,0:T(8,128)S(1)} %get-tuple-element.13), channel_id=1, source_target_pairs={{0,71},{1,64},{2,65},{3,66},{4,67},{5,68},{6,69},{7,70},{8,79},{9,... | collective-permute-start | bytes 196616 | tf_op jit(solution)/shard_map/ppermute | solution.py:385
  9.6 3.3 %collective-permute-done.1.far_ref = f32[5,4,16,128]{3,2,1,0:T(8,128)S(1)} collective-permute-done((f32[5,4,16,128]{3,2,1,0:T(8,128)S(1)}, f32[5,4,16,128]{3,2,1,0:T(8,128)S(1)}, u32[]{:S(2)}, u32[]{:S(2)}) %collective-permute-start.1) | collective-permute-done | bytes 163872 | tf_op jit(solution)/shard_map/ppermute | solution.py:391
  12.9 0.0 collective-permute-done.3.far_edge
  12.9 0.0 collective-permute-done.2.near_edge
  12.9 2.7 %collective-permute-start.4 = (f32[5,4,16,128]{3,2,1,0:T(8,128)S(1)}, f32[5,4,16,128]{3,2,1,0:T(8,128)S(1)}, u32[]{:S(2)}, u32[]{:S(2)}) collective-permute-start(f32[5,4,16,128]{3,2,1,0:T(8,128)S(1)} %collective-permute-done.1.far_ref), channel_id=1, source_target_pairs={{0,64},{64,0},{128,192},{192,128},{1,65},{65,1},{129,193},{193,129... | collective-permute-start | bytes 491528 | tf_op jit(solution)/shard_map/ppermute | solution.py:391
  15.5 1.0 %collective-permute-done.4.other_ref = f32[5,4,16,128]{3,2,1,0:T(8,128)S(1)} collective-permute-done((f32[5,4,16,128]{3,2,1,0:T(8,128)S(1)}, f32[5,4,16,128]{3,2,1,0:T(8,128)S(1)}, u32[]{:S(2)}, u32[]{:S(2)}) %collective-permute-start.4) | collective-permute-done | bytes 163872 | tf_op jit(solution)/shard_map/ppermute | solution.py:391
  16.6 0.3 shard_map.51
  16.9 5.7 %collective-permute-start.6 = (f32[4,16,16,128]{3,2,1,0:T(8,128)S(1)}, f32[4,16,16,128]{3,2,1,0:T(8,128)S(1)}, u32[]{:S(2)}, u32[]{:S(2)}) collective-permute-start(f32[4,16,16,128]{3,2,1,0:T(8,128)S(1)} %get-tuple-element.17.own), channel_id=1, source_target_pairs={{0,56},{8,0},{16,8},{24,16},{32,24},{40,32},{48,40},{56,48},{1,57}... | collective-permute-start | bytes 1572872 | tf_op jit(solution)/shard_map/ppermute | solution.py:391
  22.6 0.0 collective-permute-start.5
  22.6 0.0 collective-permute-start.7
  22.6 3.6 %collective-permute-start.8 = (f32[8,24,128]{2,1,0:T(8,128)S(1)}, f32[8,24,128]{2,1,0:T(8,128)S(1)}, u32[]{:S(2)}, u32[]{:S(2)}) collective-permute-start(f32[8,24,128]{2,1,0:T(8,128)S(1)} %get-tuple-element.19), channel_id=1, source_target_pairs={{0,48},{8,56},{16,0},{24,8},{32,16},{40,24},{48,32},{56,40},{1,49}... | collective-permute-start | bytes 294920 | tf_op jit(solution)/shard_map/ppermute | solution.py:391
  26.1 12.3 %collective-permute-done.7.low2 = f32[8,24,128]{2,1,0:T(8,128)S(1)} collective-permute-done((f32[8,24,128]{2,1,0:T(8,128)S(1)}, f32[8,24,128]{2,1,0:T(8,128)S(1)}, u32[]{:S(2)}, u32[]{:S(2)}) %collective-permute-start.7) | collective-permute-done | bytes 98336 | tf_op jit(solution)/shard_map/ppermute | solution.py:391
  38.4 0.0 collective-permute-done.8.high2
  38.4 0.0 collective-permute-done.6.high
  38.4 0.0 collective-permute-done.5.low
  38.4 21.1 %shard_map.52 = (f32[20,4,16,128]{3,2,1,0:T(8,128)S(1)}, f32[10,4,16,128]{3,2,1,0:T(8,128)S(1)}) custom-call(s32[1]{0:T(128)} %bitcast.core_ref, f32[4,16,16,128]{3,2,1,0:T(8,128)S(1)} %get-tuple-element.17.own, f32[4,16,16,128]{3,2,1,0:T(8,128)S(1)} %collective-permute-done.5.low, f32[4,16,16,128]{3,2,1,0:T(8,128)S(1)} %collective-permute-done.6.high, ...), custom_call_target="tpu_custom_call" | custom-call | tf_op jit(solution)/shard_map/pallas_call | solution.py:352
  59.5 2.9 %collective-permute-start.9 = (f32[10,4,16,128]{3,2,1,0:T(8,128)S(1)}, f32[10,4,16,128]{3,2,1,0:T(8,128)S(1)}, u32[]{:S(2)}, u32[]{:S(2)}) collective-permute-start(f32[10,4,16,128]{3,2,1,0:T(8,128)S(1)} %get-tuple-element.21), channel_id=1, source_target_pairs={{0,64},{64,0},{128,192},{192,128},{1,65},{65,1},{129,193},{193,129... | collective-permute-start | bytes 983048 | tf_op jit(solution)/shard_map/ppermute | solution.py:391
  62.4 1.3 %collective-permute-done.9.back_ref = f32[10,4,16,128]{3,2,1,0:T(8,128)S(1)} collective-permute-done((f32[10,4,16,128]{3,2,1,0:T(8,128)S(1)}, f32[10,4,16,128]{3,2,1,0:T(8,128)S(1)}, u32[]{:S(2)}, u32[]{:S(2)}) %collective-permute-start.9) | collective-permute-done | bytes 327712 | tf_op jit(solution)/shard_map/ppermute | solution.py:391
  63.7 1.0 %shard_map.53 = (f32[4,16,128]{2,1,0:T(8,128)}, f32[19,4,16,128]{3,2,1,0:T(8,128)}) custom-call(s32[1]{0:T(128)} %bitcast.core_ref, f32[20,4,16,128]{3,2,1,0:T(8,128)S(1)} %get-tuple-element.20.mine_ref, f32[10,4,16,128]{3,2,1,0:T(8,128)S(1)} %collective-permute-done.9.back_ref), custom_call_target="tpu_custom_call" | custom-call | tf_op jit(solution)/shard_map/pallas_call | solution.py:352
Async XLA Ops:
  1.6 4.5 %collective-permute-start = (f32[5,4,16,128]{3,2,1,0:T(8,128)S(1)}, f32[5,4,16,128]{3,2,1,0:T(8,128)S(1)}, u32[]{:S(2)}, u32[]{:S(2)}) collective-permute-start(f32[5,4,16,128]{3,2,1,0:T(8,128)S(1)} %pad_maximum_fusion.mine_ref), channel_id=1, source_target_pairs={{0,64},{64,0},{128,192},{192,128},{1,65},{65,1},{129,193},{193,129... | collective-permute-start | bytes 491528 | tf_op jit(solution)/shard_map/ppermute | solution.py:391
  4.9 8.0 %collective-permute-start.1 = (f32[5,4,16,128]{3,2,1,0:T(8,128)S(1)}, f32[5,4,16,128]{3,2,1,0:T(8,128)S(1)}, u32[]{:S(2)}, u32[]{:S(2)}) collective-permute-start(f32[5,4,16,128]{3,2,1,0:T(8,128)S(1)} %pad_maximum_fusion.mine_ref), channel_id=1, source_target_pairs={{0,128},{64,192},{128,0},{192,64},{1,129},{65,193},{129,1},{193,65... | collective-permute-start | bytes 491528 | tf_op jit(solution)/shard_map/ppermute | solution.py:391
  6.2 6.6 %collective-permute-start.3 = (f32[8,16,128]{2,1,0:T(8,128)S(1)}, f32[8,16,128]{2,1,0:T(8,128)S(1)}, u32[]{:S(2)}, u32[]{:S(2)}) collective-permute-start(f32[8,16,128]{2,1,0:T(8,128)S(1)} %get-tuple-element.13), channel_id=1, source_target_pairs={{0,199},{1,192},{2,193},{3,194},{4,195},{5,196},{6,197},{7,198},{8... | collective-permute-start | bytes 196616 | tf_op jit(solution)/shard_map/ppermute | solution.py:385
  8.5 4.4 %collective-permute-start.2 = (f32[8,16,128]{2,1,0:T(8,128)S(1)}, f32[8,16,128]{2,1,0:T(8,128)S(1)}, u32[]{:S(2)}, u32[]{:S(2)}) collective-permute-start(f32[8,16,128]{2,1,0:T(8,128)S(1)} %get-tuple-element.13), channel_id=1, source_target_pairs={{0,71},{1,64},{2,65},{3,66},{4,67},{5,68},{6,69},{7,70},{8,79},{9,... | collective-permute-start | bytes 196616 | tf_op jit(solution)/shard_map/ppermute | solution.py:385
  12.9 3.7 %collective-permute-start.4 = (f32[5,4,16,128]{3,2,1,0:T(8,128)S(1)}, f32[5,4,16,128]{3,2,1,0:T(8,128)S(1)}, u32[]{:S(2)}, u32[]{:S(2)}) collective-permute-start(f32[5,4,16,128]{3,2,1,0:T(8,128)S(1)} %collective-permute-done.1.far_ref), channel_id=1, source_target_pairs={{0,64},{64,0},{128,192},{192,128},{1,65},{65,1},{129,193},{193,129... | collective-permute-start | bytes 491528 | tf_op jit(solution)/shard_map/ppermute | solution.py:391
  16.9 21.5 %collective-permute-start.6 = (f32[4,16,16,128]{3,2,1,0:T(8,128)S(1)}, f32[4,16,16,128]{3,2,1,0:T(8,128)S(1)}, u32[]{:S(2)}, u32[]{:S(2)}) collective-permute-start(f32[4,16,16,128]{3,2,1,0:T(8,128)S(1)} %get-tuple-element.17.own), channel_id=1, source_target_pairs={{0,56},{8,0},{16,8},{24,16},{32,24},{40,32},{48,40},{56,48},{1,57}... | collective-permute-start | bytes 1572872 | tf_op jit(solution)/shard_map/ppermute | solution.py:391
  22.6 15.9 %collective-permute-start.5 = (f32[4,16,16,128]{3,2,1,0:T(8,128)S(1)}, f32[4,16,16,128]{3,2,1,0:T(8,128)S(1)}, u32[]{:S(2)}, u32[]{:S(2)}) collective-permute-start(f32[4,16,16,128]{3,2,1,0:T(8,128)S(1)} %get-tuple-element.17.own), channel_id=1, source_target_pairs={{0,8},{8,16},{16,24},{24,32},{32,40},{40,48},{48,56},{56,0},{1,9},... | collective-permute-start | bytes 1572872 | tf_op jit(solution)/shard_map/ppermute | solution.py:391
  22.6 15.9 %collective-permute-start.7 = (f32[8,24,128]{2,1,0:T(8,128)S(1)}, f32[8,24,128]{2,1,0:T(8,128)S(1)}, u32[]{:S(2)}, u32[]{:S(2)}) collective-permute-start(f32[8,24,128]{2,1,0:T(8,128)S(1)} %get-tuple-element.18), channel_id=1, source_target_pairs={{0,16},{8,24},{16,32},{24,40},{32,48},{40,56},{48,0},{56,8},{1,17}... | collective-permute-start | bytes 294920 | tf_op jit(solution)/shard_map/ppermute | solution.py:391
  22.6 15.9 %collective-permute-start.8 = (f32[8,24,128]{2,1,0:T(8,128)S(1)}, f32[8,24,128]{2,1,0:T(8,128)S(1)}, u32[]{:S(2)}, u32[]{:S(2)}) collective-permute-start(f32[8,24,128]{2,1,0:T(8,128)S(1)} %get-tuple-element.19), channel_id=1, source_target_pairs={{0,48},{8,56},{16,0},{24,8},{32,16},{40,24},{48,32},{56,40},{1,49}... | collective-permute-start | bytes 294920 | tf_op jit(solution)/shard_map/ppermute | solution.py:391
  59.5 4.2 %collective-permute-start.9 = (f32[10,4,16,128]{3,2,1,0:T(8,128)S(1)}, f32[10,4,16,128]{3,2,1,0:T(8,128)S(1)}, u32[]{:S(2)}, u32[]{:S(2)}) collective-permute-start(f32[10,4,16,128]{3,2,1,0:T(8,128)S(1)} %get-tuple-element.21), channel_id=1, source_target_pairs={{0,64},{64,0},{128,192},{192,128},{1,65},{65,1},{129,193},{193,129... | collective-permute-start | bytes 983048 | tf_op jit(solution)/shard_map/ppermute | solution.py:391

commit v4 on v3

--- a/solution.py
+++ b/solution.py
@@ -74,6 +74,10 @@
             edge_ref[base + x] = packed
 
 
+def unpack_edge(edge, f):
+    return pltpu.roll(edge, LANES - GAP * f, 1) if f else edge
+
+
 def spare_lanes(core, shape):
     lane = lax.broadcasted_iota(jnp.int32, shape, len(shape) - 1)
     start = jnp.where(core == 0, 82, 18)
@@ -88,6 +92,7 @@
     for n in range(NX):
         if n < 8:
             source, k, x, edge = near_ref, n, n, near_edge[n]
+            pack_ref[4, n] = edge
         else:
             source, k, base = (far_ref, n - 8, lo) if n < 12 else (other_ref, n - 12, hi)
             x = base + 8 + n % 4
@@ -95,12 +100,11 @@
         pair, row = (x // 2, (x % 2) * 12) if n < 8 else (lax.div(base, 2) + 4 + n % 4 // 2, (n % 2) * 12)
         order = None
         for f in range(5):
-            moved = pltpu.roll(edge, LANES - GAP * f, 1) if f else edge
-            value = jnp.where(take, moved, source[f, k])
+            value = jnp.where(take, unpack_edge(edge, f), source[f, k])
             if f == 0:
                 order = value
-            else:
-                pack_ref[f - 1, x] = jnp.where(spare, pltpu.roll(order, LANES - PART * f, 1), value)
+            elif n >= 8:
+                pack_ref[f - 1, x - 8] = jnp.where(spare, pltpu.roll(order, LANES - PART * f, 1), value)
             count = 4 if f == 0 else 2
             up_ref[pair, row : row + count, :] = value[BY - count :]
             down_ref[pair, row : row + count, :] = value[:count]
@@ -264,24 +268,43 @@
             self.orders[1 - now][x, at, :] = here - ((0.25 * total - mobility * spread) + (face - prev_lane(face)))
 
 
-def steps_kernel(core_ref, own, low, high, low2, high2, mine_ref, send_ref, pops_a, pops_b, order_a, order_b, chem_a, chem_b, rho_a, rho_b, inv_a, inv_b, vel_a, vel_b):
+def steps_kernel(core_ref, near, own, low_mine, low_other, low, high_mine, high_other, high, low2, high2, mine_ref, send_ref, pops_a, pops_b, order_a, order_b, chem_a, chem_b, rho_a, rho_b, inv_a, inv_b, vel_a, vel_b):
     core = core_ref[0]
 
     targets = (order_a, rho_b, vel_b.at[0], vel_b.at[1], vel_b.at[2])
     _, lane, start = spare_lanes(core, (BY, LANES))
     source_lane = lax.rem(lane - start + 2 * LANES - PART, LANES)
 
+    _, take = lane_masks(core, (BY, LANES))
+    lo, hi = core * 4, 4 - core * 4
+    blocks = (
+        (((near, 0, 0), (near, 4, 4)), own, OWN),
+        (((low_mine, 0, lo), (low_other, 0, hi)), low, OWN - 16),
+        (((high_mine, 0, lo), (high_other, 0, hi)), high, OWN + 16),
+    )
+
+    def load_block(k, _):
+        for sources, pack, row in blocks:
+            for source, skip, base in sources:
+                x = base + k
+                edge = pack[4, x]
+                for f, target in enumerate(targets):
+                    target[x, pl.ds(row, 16), :] = jnp.where(take, unpack_edge(edge, f), source[f, skip + k])
+            for x in (k, k + 4):
+                order = None
+                for f in range(1, 5):
+                    value = pack[f - 1, x]
+                    targets[f][x + 8, pl.ds(row, 16), :] = value
+                    moved = pltpu.roll(value, PART * f, 1)
+                    order = moved if order is None else jnp.where(source_lane >= PART * (f - 1), moved, order)
+                order_a[x + 8, pl.ds(row, 16), :] = order
+        return 0
+
+    lax.fori_loop(0, 4, load_block, 0)
+
     def load(pair, _):
         for half in range(2):
             x = 2 * pair + half
-            for source, row in ((low, OWN - 16), (own, OWN), (high, OWN + 16)):
-                order = None
-                for f in range(1, 5):
-                    value = source[f - 1, x]
-                    targets[f][x, pl.ds(row, 16), :] = value
-                    moved = pltpu.roll(value, PART * f, 1)
-                    order = moved if order is None else jnp.where(source_lane >= PART * (f - 1), moved, order)
-                order_a[x, pl.ds(row, 16), :] = order
             for f, target in enumerate(targets):
                 count, row = (4, 12 * half) if f == 0 else (2, 12 * half + 2 + 2 * f)
                 target[x, pl.ds(OWN - 16 - count, count), :] = low2[pair, row : row + count, :]
@@ -398,16 +421,25 @@
     near, edge = vmem_call(gather_pair, [(5, 8, BY, LANES), (8, BY, LANES)])(core_arg, fields, other)
     near_edge = send(edge, lambda x, y, z: (x ^ 1, y, z + 1 if x & 1 else z - 1))
     far_edge = send(edge, lambda x, y, z: (x ^ 3, y, z + 1 if x & 1 else z - 1))
+    fields_again, _ = lax.optimization_barrier((fields, edge))
+    low_mine = along(fields_again, "gy", lambda i: i + 1)
+    high_mine = along(fields_again, "gy", lambda i: i - 1)
     far_again, near_edge, far_edge = lax.optimization_barrier((far, near_edge, far_edge))
     other_far = along(far_again, "gx", swap)
-    pack, last_rows, first_rows = vmem_call(merge_edges, [(4, NX, BY, LANES), (8, 24, LANES), (8, 24, LANES)])(
+    other_far, low_mine, high_mine = lax.optimization_barrier((other_far, low_mine, high_mine))
+    pack, last_rows, first_rows = vmem_call(merge_edges, [(5, 8, BY, LANES), (8, 24, LANES), (8, 24, LANES)])(
         core_arg, near, far_again, other_far, near_edge, far_edge
     )
     low = along(pack, "gy", lambda i: i + 1)
     high = along(pack, "gy", lambda i: i - 1)
+    low_other = along(low_mine, "gx", swap)
+    high_other = along(high_mine, "gx", swap)
+    last_rows, first_rows, low_other, high_other = lax.optimization_barrier((last_rows, first_rows, low_other, high_other))
     low2 = along(last_rows, "gy", lambda i: i + 2)
     high2 = along(first_rows, "gy", lambda i: i - 2)
-    mine, away = make_steps()(core_arg, pack, low, high, low2, high2)
+    mine, away = make_steps()(
+        core_arg, near, pack, low_mine, low_other, low, high_mine, high_other, high, low2, high2
+    )
     back = along(away, "gx", swap)
     return tuple(vmem_call(join_halves, [(4, BY, LANES), (19, 4, BY, LANES)])(core_arg, mine, back))
 

time: 64.7 us -> 60.2 us (0.930)
  waiting for transfers between devices: 17.9 us -> 11.2 us
  starting transfers between devices: 22.7 us -> 25.1 us
    ppermute x8 -> x12, waiting for transfers between devices: 17.9 us -> 11.2 us  [along(): lax.ppermute(value, axis, [(i, to(i) % lax.axis_size(axis)) for i in rang...]
    ppermute x8 -> x12, starting transfers between devices: 19.3 us -> 21.8 us  [along(): lax.ppermute(value, axis, [(i, to(i) % lax.axis_size(axis)) for i in rang...]
  transfers between devices with their start and end apart: 10 -> 14, of which waited for: 4 -> 6; matrix products, arithmetic and copies ran while one was open for 0% -> 0% of each run, Pallas kernels for 0% -> 0%
where the time goes in v4:
time: 60.2 us; the launch traced here: 60.1 us
  starting transfers between devices  25.1 us (42%)
  Pallas kernels  22.2 us (37%)
  waiting for transfers between devices  11.2 us (19%)
  other arithmetic  0.93 us (2%)
  between operations  0.68 us (1%)
    pallas_call x4, Pallas kernels, call(): pl.pallas_call(kernel, out_shape=[jax.ShapeDtypeStruct(s, F32) for s in o...  22.2 us
    ppermute x12, starting transfers between devices, along(): lax.ppermute(value, axis, [(i, to(i) % lax.axis_size(axis)) for i in rang...  21.8 us
    ppermute x12, waiting for transfers between devices, along(): lax.ppermute(value, axis, [(i, to(i) % lax.axis_size(axis)) for i in rang...  11.2 us
    ppermute x2, starting transfers between devices, send(): return lax.ppermute(value, AXES, pairs)  3.34 us
  transfers between devices with their start and end apart: 14, of which 6 were waited for; matrix products, arithmetic and copies ran while one was open for 0% of the time, Pallas kernels for 0%

profile of v4, /device:TPU:1, one launch (start us, length us, event | category | flops | bytes accessed | tf_op | source)
XLA Modules:
  0.0 60.1 jit_solution(5617278855304240499)
XLA Ops:
  0.6 0.9 %pad_maximum_fusion.mine_ref = f32[5,4,16,128]{3,2,1,0:T(8,128)S(1)} fusion(f32[3,4,16,128]{3,2,1,0:T(8,128)} %param.5, f32[1,4,16,128]{3,2,1,0:T(8,128)} %bitcast.3, f32[1,4,16,128]{3,2,1,0:T(8,128)} %bitcast.4), kind=kLoop, calls=%fused_computation | loop fusion | flops 81920 | bytes 327680 | tf_op jit(solution)/shard_map/concatenate | solution.py:412
  1.6 3.3 %collective-permute-start = (f32[5,4,16,128]{3,2,1,0:T(8,128)S(1)}, f32[5,4,16,128]{3,2,1,0:T(8,128)S(1)}, u32[]{:S(2)}, u32[]{:S(2)}) collective-permute-start(f32[5,4,16,128]{3,2,1,0:T(8,128)S(1)} %pad_maximum_fusion.mine_ref), channel_id=1, source_target_pairs={{0,64},{64,0},{128,192},{192,128},{1,65},{65,1},{129,193},{193,129... | collective-permute-start | bytes 491528 | tf_op jit(solution)/shard_map/ppermute | solution.py:414
  4.9 1.2 %collective-permute-start.1 = (f32[5,4,16,128]{3,2,1,0:T(8,128)S(1)}, f32[5,4,16,128]{3,2,1,0:T(8,128)S(1)}, u32[]{:S(2)}, u32[]{:S(2)}) collective-permute-start(f32[5,4,16,128]{3,2,1,0:T(8,128)S(1)} %pad_maximum_fusion.mine_ref), channel_id=1, source_target_pairs={{0,128},{64,192},{128,0},{192,64},{1,129},{65,193},{129,1},{193,65... | collective-permute-start | bytes 491528 | tf_op jit(solution)/shard_map/ppermute | solution.py:414
  6.1 0.0 collective-permute-done.other_ref
  6.1 0.1 shard_map.50
  6.2 2.3 %collective-permute-start.3 = (f32[8,16,128]{2,1,0:T(8,128)S(1)}, f32[8,16,128]{2,1,0:T(8,128)S(1)}, u32[]{:S(2)}, u32[]{:S(2)}) collective-permute-start(f32[8,16,128]{2,1,0:T(8,128)S(1)} %get-tuple-element.21), channel_id=1, source_target_pairs={{0,199},{1,192},{2,193},{3,194},{4,195},{5,196},{6,197},{7,198},{8... | collective-permute-start | bytes 196616 | tf_op jit(solution)/shard_map/ppermute | solution.py:408
  8.5 1.1 %collective-permute-start.2 = (f32[8,16,128]{2,1,0:T(8,128)S(1)}, f32[8,16,128]{2,1,0:T(8,128)S(1)}, u32[]{:S(2)}, u32[]{:S(2)}) collective-permute-start(f32[8,16,128]{2,1,0:T(8,128)S(1)} %get-tuple-element.21), channel_id=1, source_target_pairs={{0,71},{1,64},{2,65},{3,66},{4,67},{5,68},{6,69},{7,70},{8,79},{9,... | collective-permute-start | bytes 196616 | tf_op jit(solution)/shard_map/ppermute | solution.py:408
  9.6 4.8 %collective-permute-start.6 = (f32[5,4,16,128]{3,2,1,0:T(8,128)S(1)}, f32[5,4,16,128]{3,2,1,0:T(8,128)S(1)}, u32[]{:S(2)}, u32[]{:S(2)}) collective-permute-start(f32[5,4,16,128]{3,2,1,0:T(8,128)S(1)} %pad_maximum_fusion.mine_ref), channel_id=1, source_target_pairs={{0,56},{8,0},{16,8},{24,16},{32,24},{40,32},{48,40},{56,48},{1,57}... | collective-permute-start | bytes 491528 | tf_op jit(solution)/shard_map/ppermute | solution.py:414
  14.4 0.0 collective-permute-start.5
  14.4 0.0 collective-permute-done.1.far_ref
  14.4 0.0 collective-permute-done.3.far_edge
  14.4 0.0 collective-permute-done.2.near_edge
  14.4 1.3 %collective-permute-start.4 = (f32[5,4,16,128]{3,2,1,0:T(8,128)S(1)}, f32[5,4,16,128]{3,2,1,0:T(8,128)S(1)}, u32[]{:S(2)}, u32[]{:S(2)}) collective-permute-start(f32[5,4,16,128]{3,2,1,0:T(8,128)S(1)} %collective-permute-done.1.far_ref), channel_id=1, source_target_pairs={{0,64},{64,0},{128,192},{192,128},{1,65},{65,1},{129,193},{193,129... | collective-permute-start | bytes 491528 | tf_op jit(solution)/shard_map/ppermute | solution.py:414
  15.7 1.2 %collective-permute-done.6.high_mine = f32[5,4,16,128]{3,2,1,0:T(8,128)S(1)} collective-permute-done((f32[5,4,16,128]{3,2,1,0:T(8,128)S(1)}, f32[5,4,16,128]{3,2,1,0:T(8,128)S(1)}, u32[]{:S(2)}, u32[]{:S(2)}) %collective-permute-start.6) | collective-permute-done | bytes 163872 | tf_op jit(solution)/shard_map/ppermute | solution.py:414
  16.9 2.9 %collective-permute-done.5.low_mine = f32[5,4,16,128]{3,2,1,0:T(8,128)S(1)} collective-permute-done((f32[5,4,16,128]{3,2,1,0:T(8,128)S(1)}, f32[5,4,16,128]{3,2,1,0:T(8,128)S(1)}, u32[]{:S(2)}, u32[]{:S(2)}) %collective-permute-start.5) | collective-permute-done | bytes 163872 | tf_op jit(solution)/shard_map/ppermute | solution.py:414
  19.7 0.0 collective-permute-done.4.other_ref
  19.7 0.3 shard_map.51
  20.0 2.5 %collective-permute-start.10 = (f32[5,8,16,128]{3,2,1,0:T(8,128)S(1)}, f32[5,8,16,128]{3,2,1,0:T(8,128)S(1)}, u32[]{:S(2)}, u32[]{:S(2)}) collective-permute-start(f32[5,8,16,128]{3,2,1,0:T(8,128)S(1)} %get-tuple-element.27.own), channel_id=1, source_target_pairs={{0,56},{8,0},{16,8},{24,16},{32,24},{40,32},{48,40},{56,48},{1,57}... | collective-permute-start | bytes 983048 | tf_op jit(solution)/shard_map/ppermute | solution.py:414
  22.5 0.0 collective-permute-start.9
  22.5 2.1 %collective-permute-start.7 = (f32[5,4,16,128]{3,2,1,0:T(8,128)S(1)}, f32[5,4,16,128]{3,2,1,0:T(8,128)S(1)}, u32[]{:S(2)}, u32[]{:S(2)}) collective-permute-start(f32[5,4,16,128]{3,2,1,0:T(8,128)S(1)} %collective-permute-done.5.low_mine), channel_id=1, source_target_pairs={{0,64},{64,0},{128,192},{192,128},{1,65},{65,1},{129,193},{193,129... | collective-permute-start | bytes 491528 | tf_op jit(solution)/shard_map/ppermute | solution.py:414
  24.6 0.0 collective-permute-start.8
  24.6 1.0 %collective-permute-done.7.low_other = f32[5,4,16,128]{3,2,1,0:T(8,128)S(1)} collective-permute-done((f32[5,4,16,128]{3,2,1,0:T(8,128)S(1)}, f32[5,4,16,128]{3,2,1,0:T(8,128)S(1)}, u32[]{:S(2)}, u32[]{:S(2)}) %collective-permute-start.7) | collective-permute-done | bytes 163872 | tf_op jit(solution)/shard_map/ppermute | solution.py:414
  25.6 0.4 collective-permute-done.8.high_other
  26.0 0.0 collective-permute-start.11
  26.0 3.6 %collective-permute-start.12 = (f32[8,24,128]{2,1,0:T(8,128)S(1)}, f32[8,24,128]{2,1,0:T(8,128)S(1)}, u32[]{:S(2)}, u32[]{:S(2)}) collective-permute-start(f32[8,24,128]{2,1,0:T(8,128)S(1)} %get-tuple-element.35), channel_id=1, source_target_pairs={{0,48},{8,56},{16,0},{24,8},{32,16},{40,24},{48,32},{56,40},{1,49}... | collective-permute-start | bytes 294920 | tf_op jit(solution)/shard_map/ppermute | solution.py:414
  29.5 4.5 %collective-permute-done.11.low2 = f32[8,24,128]{2,1,0:T(8,128)S(1)} collective-permute-done((f32[8,24,128]{2,1,0:T(8,128)S(1)}, f32[8,24,128]{2,1,0:T(8,128)S(1)}, u32[]{:S(2)}, u32[]{:S(2)}) %collective-permute-start.11) | collective-permute-done | bytes 98336 | tf_op jit(solution)/shard_map/ppermute | solution.py:414
  34.1 0.0 collective-permute-done.12.high2
  34.1 0.0 collective-permute-done.10.high
  34.1 0.0 collective-permute-done.9.low
  34.1 20.8 %shard_map.52 = (f32[20,4,16,128]{3,2,1,0:T(8,128)S(1)}, f32[10,4,16,128]{3,2,1,0:T(8,128)S(1)}) custom-call(s32[1]{0:T(128)} %bitcast.core_ref, f32[5,8,16,128]{3,2,1,0:T(8,128)S(1)} %get-tuple-element.20.near_ref.near, f32[5,8,16,128]{3,2,1,0:T(8,128)S(1)} %get-tuple-element.27.own, f32[5,4,16,128]{3,2,1,0:T(8,128)S(1)} %collective-permute-done.5.low_mine, ...), custom_call_target="tpu_custom_call" | custom-call | tf_op jit(solution)/shard_map/pallas_call | solution.py:375
  54.9 3.0 %collective-permute-start.13 = (f32[10,4,16,128]{3,2,1,0:T(8,128)S(1)}, f32[10,4,16,128]{3,2,1,0:T(8,128)S(1)}, u32[]{:S(2)}, u32[]{:S(2)}) collective-permute-start(f32[10,4,16,128]{3,2,1,0:T(8,128)S(1)} %get-tuple-element.37), channel_id=1, source_target_pairs={{0,64},{64,0},{128,192},{192,128},{1,65},{65,1},{129,193},{193,129... | collective-permute-start | bytes 983048 | tf_op jit(solution)/shard_map/ppermute | solution.py:414
  57.9 1.3 %collective-permute-done.13.back_ref = f32[10,4,16,128]{3,2,1,0:T(8,128)S(1)} collective-permute-done((f32[10,4,16,128]{3,2,1,0:T(8,128)S(1)}, f32[10,4,16,128]{3,2,1,0:T(8,128)S(1)}, u32[]{:S(2)}, u32[]{:S(2)}) %collective-permute-start.13) | collective-permute-done | bytes 327712 | tf_op jit(solution)/shard_map/ppermute | solution.py:414
  59.1 1.0 %shard_map.53 = (f32[4,16,128]{2,1,0:T(8,128)}, f32[19,4,16,128]{3,2,1,0:T(8,128)}) custom-call(s32[1]{0:T(128)} %bitcast.core_ref, f32[20,4,16,128]{3,2,1,0:T(8,128)S(1)} %get-tuple-element.36.mine_ref, f32[10,4,16,128]{3,2,1,0:T(8,128)S(1)} %collective-permute-done.13.back_ref), custom_call_target="tpu_custom_call" | custom-call | tf_op jit(solution)/shard_map/pallas_call | solution.py:375
Async XLA Ops:
  1.6 4.5 %collective-permute-start = (f32[5,4,16,128]{3,2,1,0:T(8,128)S(1)}, f32[5,4,16,128]{3,2,1,0:T(8,128)S(1)}, u32[]{:S(2)}, u32[]{:S(2)}) collective-permute-start(f32[5,4,16,128]{3,2,1,0:T(8,128)S(1)} %pad_maximum_fusion.mine_ref), channel_id=1, source_target_pairs={{0,64},{64,0},{128,192},{192,128},{1,65},{65,1},{129,193},{193,129... | collective-permute-start | bytes 491528 | tf_op jit(solution)/shard_map/ppermute | solution.py:414
  4.9 9.5 %collective-permute-start.1 = (f32[5,4,16,128]{3,2,1,0:T(8,128)S(1)}, f32[5,4,16,128]{3,2,1,0:T(8,128)S(1)}, u32[]{:S(2)}, u32[]{:S(2)}) collective-permute-start(f32[5,4,16,128]{3,2,1,0:T(8,128)S(1)} %pad_maximum_fusion.mine_ref), channel_id=1, source_target_pairs={{0,128},{64,192},{128,0},{192,64},{1,129},{65,193},{129,1},{193,65... | collective-permute-start | bytes 491528 | tf_op jit(solution)/shard_map/ppermute | solution.py:414
  6.2 8.1 %collective-permute-start.3 = (f32[8,16,128]{2,1,0:T(8,128)S(1)}, f32[8,16,128]{2,1,0:T(8,128)S(1)}, u32[]{:S(2)}, u32[]{:S(2)}) collective-permute-start(f32[8,16,128]{2,1,0:T(8,128)S(1)} %get-tuple-element.21), channel_id=1, source_target_pairs={{0,199},{1,192},{2,193},{3,194},{4,195},{5,196},{6,197},{7,198},{8... | collective-permute-start | bytes 196616 | tf_op jit(solution)/shard_map/ppermute | solution.py:408
  8.5 5.9 %collective-permute-start.2 = (f32[8,16,128]{2,1,0:T(8,128)S(1)}, f32[8,16,128]{2,1,0:T(8,128)S(1)}, u32[]{:S(2)}, u32[]{:S(2)}) collective-permute-start(f32[8,16,128]{2,1,0:T(8,128)S(1)} %get-tuple-element.21), channel_id=1, source_target_pairs={{0,71},{1,64},{2,65},{3,66},{4,67},{5,68},{6,69},{7,70},{8,79},{9,... | collective-permute-start | bytes 196616 | tf_op jit(solution)/shard_map/ppermute | solution.py:408
  9.6 7.3 %collective-permute-start.6 = (f32[5,4,16,128]{3,2,1,0:T(8,128)S(1)}, f32[5,4,16,128]{3,2,1,0:T(8,128)S(1)}, u32[]{:S(2)}, u32[]{:S(2)}) collective-permute-start(f32[5,4,16,128]{3,2,1,0:T(8,128)S(1)} %pad_maximum_fusion.mine_ref), channel_id=1, source_target_pairs={{0,56},{8,0},{16,8},{24,16},{32,24},{40,32},{48,40},{56,48},{1,57}... | collective-permute-start | bytes 491528 | tf_op jit(solution)/shard_map/ppermute | solution.py:414
  14.4 5.4 %collective-permute-start.5 = (f32[5,4,16,128]{3,2,1,0:T(8,128)S(1)}, f32[5,4,16,128]{3,2,1,0:T(8,128)S(1)}, u32[]{:S(2)}, u32[]{:S(2)}) collective-permute-start(f32[5,4,16,128]{3,2,1,0:T(8,128)S(1)} %pad_maximum_fusion.mine_ref), channel_id=1, source_target_pairs={{0,8},{8,16},{16,24},{24,32},{32,40},{40,48},{48,56},{56,0},{1,9},... | collective-permute-start | bytes 491528 | tf_op jit(solution)/shard_map/ppermute | solution.py:414
  14.4 5.4 %collective-permute-start.4 = (f32[5,4,16,128]{3,2,1,0:T(8,128)S(1)}, f32[5,4,16,128]{3,2,1,0:T(8,128)S(1)}, u32[]{:S(2)}, u32[]{:S(2)}) collective-permute-start(f32[5,4,16,128]{3,2,1,0:T(8,128)S(1)} %collective-permute-done.1.far_ref), channel_id=1, source_target_pairs={{0,64},{64,0},{128,192},{192,128},{1,65},{65,1},{129,193},{193,129... | collective-permute-start | bytes 491528 | tf_op jit(solution)/shard_map/ppermute | solution.py:414
  20.0 14.0 %collective-permute-start.10 = (f32[5,8,16,128]{3,2,1,0:T(8,128)S(1)}, f32[5,8,16,128]{3,2,1,0:T(8,128)S(1)}, u32[]{:S(2)}, u32[]{:S(2)}) collective-permute-start(f32[5,8,16,128]{3,2,1,0:T(8,128)S(1)} %get-tuple-element.27.own), channel_id=1, source_target_pairs={{0,56},{8,0},{16,8},{24,16},{32,24},{40,32},{48,40},{56,48},{1,57}... | collective-permute-start | bytes 983048 | tf_op jit(solution)/shard_map/ppermute | solution.py:414
  22.5 11.6 %collective-permute-start.9 = (f32[5,8,16,128]{3,2,1,0:T(8,128)S(1)}, f32[5,8,16,128]{3,2,1,0:T(8,128)S(1)}, u32[]{:S(2)}, u32[]{:S(2)}) collective-permute-start(f32[5,8,16,128]{3,2,1,0:T(8,128)S(1)} %get-tuple-element.27.own), channel_id=1, source_target_pairs={{0,8},{8,16},{16,24},{24,32},{32,40},{40,48},{48,56},{56,0},{1,9},... | collective-permute-start | bytes 983048 | tf_op jit(solution)/shard_map/ppermute | solution.py:414
  22.5 3.1 %collective-permute-start.7 = (f32[5,4,16,128]{3,2,1,0:T(8,128)S(1)}, f32[5,4,16,128]{3,2,1,0:T(8,128)S(1)}, u32[]{:S(2)}, u32[]{:S(2)}) collective-permute-start(f32[5,4,16,128]{3,2,1,0:T(8,128)S(1)} %collective-permute-done.5.low_mine), channel_id=1, source_target_pairs={{0,64},{64,0},{128,192},{192,128},{1,65},{65,1},{129,193},{193,129... | collective-permute-start | bytes 491528 | tf_op jit(solution)/shard_map/ppermute | solution.py:414
  24.6 1.4 %collective-permute-start.8 = (f32[5,4,16,128]{3,2,1,0:T(8,128)S(1)}, f32[5,4,16,128]{3,2,1,0:T(8,128)S(1)}, u32[]{:S(2)}, u32[]{:S(2)}) collective-permute-start(f32[5,4,16,128]{3,2,1,0:T(8,128)S(1)} %collective-permute-done.6.high_mine), channel_id=1, source_target_pairs={{0,64},{64,0},{128,192},{192,128},{1,65},{65,1},{129,193},{193,129... | collective-permute-start | bytes 491528 | tf_op jit(solution)/shard_map/ppermute | solution.py:414
  26.0 8.1 %collective-permute-start.11 = (f32[8,24,128]{2,1,0:T(8,128)S(1)}, f32[8,24,128]{2,1,0:T(8,128)S(1)}, u32[]{:S(2)}, u32[]{:S(2)}) collective-permute-start(f32[8,24,128]{2,1,0:T(8,128)S(1)} %get-tuple-element.34), channel_id=1, source_target_pairs={{0,16},{8,24},{16,32},{24,40},{32,48},{40,56},{48,0},{56,8},{1,17}... | collective-permute-start | bytes 294920 | tf_op jit(solution)/shard_map/ppermute | solution.py:414
  26.0 8.1 %collective-permute-start.12 = (f32[8,24,128]{2,1,0:T(8,128)S(1)}, f32[8,24,128]{2,1,0:T(8,128)S(1)}, u32[]{:S(2)}, u32[]{:S(2)}) collective-permute-start(f32[8,24,128]{2,1,0:T(8,128)S(1)} %get-tuple-element.35), channel_id=1, source_target_pairs={{0,48},{8,56},{16,0},{24,8},{32,16},{40,24},{48,32},{56,40},{1,49}... | collective-permute-start | bytes 294920 | tf_op jit(solution)/shard_map/ppermute | solution.py:414
  54.9 4.2 %collective-permute-start.13 = (f32[10,4,16,128]{3,2,1,0:T(8,128)S(1)}, f32[10,4,16,128]{3,2,1,0:T(8,128)S(1)}, u32[]{:S(2)}, u32[]{:S(2)}) collective-permute-start(f32[10,4,16,128]{3,2,1,0:T(8,128)S(1)} %get-tuple-element.37), channel_id=1, source_target_pairs={{0,64},{64,0},{128,192},{192,128},{1,65},{65,1},{129,193},{193,129... | collective-permute-start | bytes 983048 | tf_op jit(solution)/shard_map/ppermute | solution.py:414

commit v5 on v4

--- a/solution.py
+++ b/solution.py
@@ -39,6 +39,7 @@
 BY = 16
 LANES = 128
 EDGE = 20
+HALF = 40
 PART = 26
 GAP = 24
 ROWS = 72
@@ -78,6 +79,13 @@
     return pltpu.roll(edge, LANES - GAP * f, 1) if f else edge
 
 
+def far_row_lanes(core, shape):
+    lane = lax.broadcasted_iota(jnp.int32, shape, len(shape) - 1)
+    spare = jnp.where(core == 0, 76, 12)
+    own = jnp.where(core == 0, 120, 56)
+    return (lane >= spare) & (lane < spare + HALF), lax.rem(lane - own + LANES, LANES) < HALF
+
+
 def spare_lanes(core, shape):
     lane = lax.broadcasted_iota(jnp.int32, shape, len(shape) - 1)
     start = jnp.where(core == 0, 82, 18)
@@ -89,6 +97,7 @@
     lo, hi = core * 4, 4 - core * 4
     _, take = lane_masks(core, (BY, LANES))
     spare, _, _ = spare_lanes(core, (BY, LANES))
+    travel, _ = far_row_lanes(core, (2, LANES))
     for n in range(NX):
         if n < 8:
             source, k, x, edge = near_ref, n, n, near_edge[n]
@@ -97,7 +106,6 @@
             source, k, base = (far_ref, n - 8, lo) if n < 12 else (other_ref, n - 12, hi)
             x = base + 8 + n % 4
             edge = far_edge[x - 8]
-        pair, row = (x // 2, (x % 2) * 12) if n < 8 else (lax.div(base, 2) + 4 + n % 4 // 2, (n % 2) * 12)
         order = None
         for f in range(5):
             value = jnp.where(take, unpack_edge(edge, f), source[f, k])
@@ -105,10 +113,11 @@
                 order = value
             elif n >= 8:
                 pack_ref[f - 1, x - 8] = jnp.where(spare, pltpu.roll(order, LANES - PART * f, 1), value)
-            count = 4 if f == 0 else 2
-            up_ref[pair, row : row + count, :] = value[BY - count :]
-            down_ref[pair, row : row + count, :] = value[:count]
-            row += count
+            if f > 0:
+                two, shift = (f - 1) // 2 * 2, LANES - 44 - HALF * ((f - 1) % 2)
+                for target, rows, first in ((up_ref, value[BY - 2 :], BY - 4 + two), (down_ref, value[:2], two)):
+                    part = pltpu.roll(order[first : first + 2], shift, 1)
+                    target[x, 2 * f - 2 : 2 * f, :] = jnp.where(travel, part, rows)
 
 
 def prev_lane(v):
@@ -302,13 +311,18 @@
 
     lax.fori_loop(0, 4, load_block, 0)
 
+    _, first_half = far_row_lanes(core, (2, LANES))
+
     def load(pair, _):
         for half in range(2):
             x = 2 * pair + half
-            for f, target in enumerate(targets):
-                count, row = (4, 12 * half) if f == 0 else (2, 12 * half + 2 + 2 * f)
-                target[x, pl.ds(OWN - 16 - count, count), :] = low2[pair, row : row + count, :]
-                target[x, pl.ds(OWN + 32, count), :] = high2[pair, row : row + count, :]
+            for source, order_row, row in ((low2, OWN - 20, OWN - 18), (high2, OWN + 32, OWN + 32)):
+                rows = [source[x, 2 * k : 2 * k + 2, :] for k in range(4)]
+                for f in range(1, 5):
+                    targets[f][x, pl.ds(row, 2), :] = rows[f - 1]
+                for k in (0, 2):
+                    both = jnp.where(first_half, pltpu.roll(rows[k], 44, 1), pltpu.roll(rows[k + 1], 44 + HALF, 1))
+                    order_a[x, pl.ds(order_row + k, 2), :] = both
         return 0
 
     lax.fori_loop(0, NX // 2, load, 0)
@@ -427,7 +441,7 @@
     far_again, near_edge, far_edge = lax.optimization_barrier((far, near_edge, far_edge))
     other_far = along(far_again, "gx", swap)
     other_far, low_mine, high_mine = lax.optimization_barrier((other_far, low_mine, high_mine))
-    pack, last_rows, first_rows = vmem_call(merge_edges, [(5, 8, BY, LANES), (8, 24, LANES), (8, 24, LANES)])(
+    pack, last_rows, first_rows = vmem_call(merge_edges, [(5, 8, BY, LANES), (NX, 8, LANES), (NX, 8, LANES)])(
         core_arg, near, far_again, other_far, near_edge, far_edge
     )
     low = along(pack, "gy", lambda i: i + 1)

time: 60.2 us -> 59.9 us (level)
  waiting for transfers between devices: 11.2 us -> 10.3 us
  Pallas kernels: 22.2 us -> 22.9 us
    ppermute x12, waiting for transfers between devices: 11.2 us -> 10.3 us  [along(): lax.ppermute(value, axis, [(i, to(i) % lax.axis_size(axis)) for i in rang...]
    pallas_call x4, Pallas kernels: 22.2 us -> 22.9 us  [call(): pl.pallas_call(kernel, out_shape=[jax.ShapeDtypeStruct(s, F32) for s in o...]
where the time goes in v5:
time: 59.9 us; the launch traced here: 59.8 us
  starting transfers between devices  25 us (42%)
  Pallas kernels  22.9 us (38%)
  waiting for transfers between devices  10.3 us (17%)
  other arithmetic  0.93 us (2%)
  between operations  0.68 us (1%)
    pallas_call x4, Pallas kernels, call(): pl.pallas_call(kernel, out_shape=[jax.ShapeDtypeStruct(s, F32) for s in o...  22.9 us
    ppermute x12, starting transfers between devices, along(): lax.ppermute(value, axis, [(i, to(i) % lax.axis_size(axis)) for i in rang...  21.6 us
    ppermute x12, waiting for transfers between devices, along(): lax.ppermute(value, axis, [(i, to(i) % lax.axis_size(axis)) for i in rang...  10.3 us
    ppermute x2, starting transfers between devices, send(): return lax.ppermute(value, AXES, pairs)  3.34 us
  transfers between devices with their start and end apart: 14, of which 6 were waited for; matrix products, arithmetic and copies ran while one was open for 0% of the time, Pallas kernels for 0%

profile of v5, /device:TPU:1, one launch (start us, length us, event | category | flops | bytes accessed | tf_op | source)
XLA Modules:
  0.0 59.8 jit_solution(15620268224719208727)
XLA Ops:
  0.6 0.9 %pad_maximum_fusion.mine_ref = f32[5,4,16,128]{3,2,1,0:T(8,128)S(1)} fusion(f32[3,4,16,128]{3,2,1,0:T(8,128)} %param.5, f32[1,4,16,128]{3,2,1,0:T(8,128)} %bitcast.3, f32[1,4,16,128]{3,2,1,0:T(8,128)} %bitcast.4), kind=kLoop, calls=%fused_computation | loop fusion | flops 81920 | bytes 327680 | tf_op jit(solution)/shard_map/concatenate | solution.py:426
  1.6 3.3 %collective-permute-start = (f32[5,4,16,128]{3,2,1,0:T(8,128)S(1)}, f32[5,4,16,128]{3,2,1,0:T(8,128)S(1)}, u32[]{:S(2)}, u32[]{:S(2)}) collective-permute-start(f32[5,4,16,128]{3,2,1,0:T(8,128)S(1)} %pad_maximum_fusion.mine_ref), channel_id=1, source_target_pairs={{0,64},{64,0},{128,192},{192,128},{1,65},{65,1},{129,193},{193,129... | collective-permute-start | bytes 491528 | tf_op jit(solution)/shard_map/ppermute | solution.py:428
  4.9 1.2 %collective-permute-start.1 = (f32[5,4,16,128]{3,2,1,0:T(8,128)S(1)}, f32[5,4,16,128]{3,2,1,0:T(8,128)S(1)}, u32[]{:S(2)}, u32[]{:S(2)}) collective-permute-start(f32[5,4,16,128]{3,2,1,0:T(8,128)S(1)} %pad_maximum_fusion.mine_ref), channel_id=1, source_target_pairs={{0,128},{64,192},{128,0},{192,64},{1,129},{65,193},{129,1},{193,65... | collective-permute-start | bytes 491528 | tf_op jit(solution)/shard_map/ppermute | solution.py:428
  6.1 0.0 collective-permute-done.other_ref
  6.1 0.1 shard_map.50
  6.2 2.3 %collective-permute-start.3 = (f32[8,16,128]{2,1,0:T(8,128)S(1)}, f32[8,16,128]{2,1,0:T(8,128)S(1)}, u32[]{:S(2)}, u32[]{:S(2)}) collective-permute-start(f32[8,16,128]{2,1,0:T(8,128)S(1)} %get-tuple-element.21), channel_id=1, source_target_pairs={{0,199},{1,192},{2,193},{3,194},{4,195},{5,196},{6,197},{7,198},{8... | collective-permute-start | bytes 196616 | tf_op jit(solution)/shard_map/ppermute | solution.py:422
  8.5 1.1 %collective-permute-start.2 = (f32[8,16,128]{2,1,0:T(8,128)S(1)}, f32[8,16,128]{2,1,0:T(8,128)S(1)}, u32[]{:S(2)}, u32[]{:S(2)}) collective-permute-start(f32[8,16,128]{2,1,0:T(8,128)S(1)} %get-tuple-element.21), channel_id=1, source_target_pairs={{0,71},{1,64},{2,65},{3,66},{4,67},{5,68},{6,69},{7,70},{8,79},{9,... | collective-permute-start | bytes 196616 | tf_op jit(solution)/shard_map/ppermute | solution.py:422
  9.6 4.8 %collective-permute-start.6 = (f32[5,4,16,128]{3,2,1,0:T(8,128)S(1)}, f32[5,4,16,128]{3,2,1,0:T(8,128)S(1)}, u32[]{:S(2)}, u32[]{:S(2)}) collective-permute-start(f32[5,4,16,128]{3,2,1,0:T(8,128)S(1)} %pad_maximum_fusion.mine_ref), channel_id=1, source_target_pairs={{0,56},{8,0},{16,8},{24,16},{32,24},{40,32},{48,40},{56,48},{1,57}... | collective-permute-start | bytes 491528 | tf_op jit(solution)/shard_map/ppermute | solution.py:428
  14.4 0.0 collective-permute-start.5
  14.4 0.0 collective-permute-done.1.far_ref
  14.4 0.0 collective-permute-done.3.far_edge
  14.4 0.0 collective-permute-done.2.near_edge
  14.4 1.3 %collective-permute-start.4 = (f32[5,4,16,128]{3,2,1,0:T(8,128)S(1)}, f32[5,4,16,128]{3,2,1,0:T(8,128)S(1)}, u32[]{:S(2)}, u32[]{:S(2)}) collective-permute-start(f32[5,4,16,128]{3,2,1,0:T(8,128)S(1)} %collective-permute-done.1.far_ref), channel_id=1, source_target_pairs={{0,64},{64,0},{128,192},{192,128},{1,65},{65,1},{129,193},{193,129... | collective-permute-start | bytes 491528 | tf_op jit(solution)/shard_map/ppermute | solution.py:428
  15.7 1.2 %collective-permute-done.6.high_mine = f32[5,4,16,128]{3,2,1,0:T(8,128)S(1)} collective-permute-done((f32[5,4,16,128]{3,2,1,0:T(8,128)S(1)}, f32[5,4,16,128]{3,2,1,0:T(8,128)S(1)}, u32[]{:S(2)}, u32[]{:S(2)}) %collective-permute-start.6) | collective-permute-done | bytes 163872 | tf_op jit(solution)/shard_map/ppermute | solution.py:428
  16.9 2.9 %collective-permute-done.5.low_mine = f32[5,4,16,128]{3,2,1,0:T(8,128)S(1)} collective-permute-done((f32[5,4,16,128]{3,2,1,0:T(8,128)S(1)}, f32[5,4,16,128]{3,2,1,0:T(8,128)S(1)}, u32[]{:S(2)}, u32[]{:S(2)}) %collective-permute-start.5) | collective-permute-done | bytes 163872 | tf_op jit(solution)/shard_map/ppermute | solution.py:428
  19.7 0.0 collective-permute-done.4.other_ref
  19.7 0.4 shard_map.51
  20.2 2.5 %collective-permute-start.10 = (f32[5,8,16,128]{3,2,1,0:T(8,128)S(1)}, f32[5,8,16,128]{3,2,1,0:T(8,128)S(1)}, u32[]{:S(2)}, u32[]{:S(2)}) collective-permute-start(f32[5,8,16,128]{3,2,1,0:T(8,128)S(1)} %get-tuple-element.27.own), channel_id=1, source_target_pairs={{0,56},{8,0},{16,8},{24,16},{32,24},{40,32},{48,40},{56,48},{1,57}... | collective-permute-start | bytes 983048 | tf_op jit(solution)/shard_map/ppermute | solution.py:428
  22.6 0.0 collective-permute-start.9
  22.6 2.1 %collective-permute-start.7 = (f32[5,4,16,128]{3,2,1,0:T(8,128)S(1)}, f32[5,4,16,128]{3,2,1,0:T(8,128)S(1)}, u32[]{:S(2)}, u32[]{:S(2)}) collective-permute-start(f32[5,4,16,128]{3,2,1,0:T(8,128)S(1)} %collective-permute-done.5.low_mine), channel_id=1, source_target_pairs={{0,64},{64,0},{128,192},{192,128},{1,65},{65,1},{129,193},{193,129... | collective-permute-start | bytes 491528 | tf_op jit(solution)/shard_map/ppermute | solution.py:428
  24.7 0.0 collective-permute-start.8
  24.7 1.0 %collective-permute-done.7.low_other = f32[5,4,16,128]{3,2,1,0:T(8,128)S(1)} collective-permute-done((f32[5,4,16,128]{3,2,1,0:T(8,128)S(1)}, f32[5,4,16,128]{3,2,1,0:T(8,128)S(1)}, u32[]{:S(2)}, u32[]{:S(2)}) %collective-permute-start.7) | collective-permute-done | bytes 163872 | tf_op jit(solution)/shard_map/ppermute | solution.py:428
  25.7 0.4 collective-permute-done.8.high_other
  26.1 0.0 collective-permute-start.11
  26.1 3.6 %collective-permute-start.12 = (f32[16,8,128]{2,1,0:T(8,128)S(1)}, f32[16,8,128]{2,1,0:T(8,128)S(1)}, u32[]{:S(2)}, u32[]{:S(2)}) collective-permute-start(f32[16,8,128]{2,1,0:T(8,128)S(1)} %get-tuple-element.35), channel_id=1, source_target_pairs={{0,48},{8,56},{16,0},{24,8},{32,16},{40,24},{48,32},{56,40},{1,49}... | collective-permute-start | bytes 196616 | tf_op jit(solution)/shard_map/ppermute | solution.py:428
  29.7 3.6 %collective-permute-done.11.low2 = f32[16,8,128]{2,1,0:T(8,128)S(1)} collective-permute-done((f32[16,8,128]{2,1,0:T(8,128)S(1)}, f32[16,8,128]{2,1,0:T(8,128)S(1)}, u32[]{:S(2)}, u32[]{:S(2)}) %collective-permute-start.11) | collective-permute-done | bytes 65568 | tf_op jit(solution)/shard_map/ppermute | solution.py:428
  33.3 0.0 collective-permute-done.12.high2
  33.3 0.0 collective-permute-done.10.high
  33.3 0.0 collective-permute-done.9.low
  33.3 21.4 %shard_map.52 = (f32[20,4,16,128]{3,2,1,0:T(8,128)S(1)}, f32[10,4,16,128]{3,2,1,0:T(8,128)S(1)}) custom-call(s32[1]{0:T(128)} %bitcast.core_ref, f32[5,8,16,128]{3,2,1,0:T(8,128)S(1)} %get-tuple-element.20.near_ref.near, f32[5,8,16,128]{3,2,1,0:T(8,128)S(1)} %get-tuple-element.27.own, f32[5,4,16,128]{3,2,1,0:T(8,128)S(1)} %collective-permute-done.5.low_mine, ...), custom_call_target="tpu_custom_call" | custom-call | tf_op jit(solution)/shard_map/pallas_call | solution.py:389
  54.7 2.9 %collective-permute-start.13 = (f32[10,4,16,128]{3,2,1,0:T(8,128)S(1)}, f32[10,4,16,128]{3,2,1,0:T(8,128)S(1)}, u32[]{:S(2)}, u32[]{:S(2)}) collective-permute-start(f32[10,4,16,128]{3,2,1,0:T(8,128)S(1)} %get-tuple-element.37), channel_id=1, source_target_pairs={{0,64},{64,0},{128,192},{192,128},{1,65},{65,1},{129,193},{193,129... | collective-permute-start | bytes 983048 | tf_op jit(solution)/shard_map/ppermute | solution.py:428
  57.6 1.3 %collective-permute-done.13.back_ref = f32[10,4,16,128]{3,2,1,0:T(8,128)S(1)} collective-permute-done((f32[10,4,16,128]{3,2,1,0:T(8,128)S(1)}, f32[10,4,16,128]{3,2,1,0:T(8,128)S(1)}, u32[]{:S(2)}, u32[]{:S(2)}) %collective-permute-start.13) | collective-permute-done | bytes 327712 | tf_op jit(solution)/shard_map/ppermute | solution.py:428
  58.8 1.0 %shard_map.53 = (f32[4,16,128]{2,1,0:T(8,128)}, f32[19,4,16,128]{3,2,1,0:T(8,128)}) custom-call(s32[1]{0:T(128)} %bitcast.core_ref, f32[20,4,16,128]{3,2,1,0:T(8,128)S(1)} %get-tuple-element.36.mine_ref, f32[10,4,16,128]{3,2,1,0:T(8,128)S(1)} %collective-permute-done.13.back_ref), custom_call_target="tpu_custom_call" | custom-call | tf_op jit(solution)/shard_map/pallas_call | solution.py:389
Async XLA Ops:
  1.6 4.5 %collective-permute-start = (f32[5,4,16,128]{3,2,1,0:T(8,128)S(1)}, f32[5,4,16,128]{3,2,1,0:T(8,128)S(1)}, u32[]{:S(2)}, u32[]{:S(2)}) collective-permute-start(f32[5,4,16,128]{3,2,1,0:T(8,128)S(1)} %pad_maximum_fusion.mine_ref), channel_id=1, source_target_pairs={{0,64},{64,0},{128,192},{192,128},{1,65},{65,1},{129,193},{193,129... | collective-permute-start | bytes 491528 | tf_op jit(solution)/shard_map/ppermute | solution.py:428
  4.9 9.5 %collective-permute-start.1 = (f32[5,4,16,128]{3,2,1,0:T(8,128)S(1)}, f32[5,4,16,128]{3,2,1,0:T(8,128)S(1)}, u32[]{:S(2)}, u32[]{:S(2)}) collective-permute-start(f32[5,4,16,128]{3,2,1,0:T(8,128)S(1)} %pad_maximum_fusion.mine_ref), channel_id=1, source_target_pairs={{0,128},{64,192},{128,0},{192,64},{1,129},{65,193},{129,1},{193,65... | collective-permute-start | bytes 491528 | tf_op jit(solution)/shard_map/ppermute | solution.py:428
  6.2 8.1 %collective-permute-start.3 = (f32[8,16,128]{2,1,0:T(8,128)S(1)}, f32[8,16,128]{2,1,0:T(8,128)S(1)}, u32[]{:S(2)}, u32[]{:S(2)}) collective-permute-start(f32[8,16,128]{2,1,0:T(8,128)S(1)} %get-tuple-element.21), channel_id=1, source_target_pairs={{0,199},{1,192},{2,193},{3,194},{4,195},{5,196},{6,197},{7,198},{8... | collective-permute-start | bytes 196616 | tf_op jit(solution)/shard_map/ppermute | solution.py:422
  8.5 5.9 %collective-permute-start.2 = (f32[8,16,128]{2,1,0:T(8,128)S(1)}, f32[8,16,128]{2,1,0:T(8,128)S(1)}, u32[]{:S(2)}, u32[]{:S(2)}) collective-permute-start(f32[8,16,128]{2,1,0:T(8,128)S(1)} %get-tuple-element.21), channel_id=1, source_target_pairs={{0,71},{1,64},{2,65},{3,66},{4,67},{5,68},{6,69},{7,70},{8,79},{9,... | collective-permute-start | bytes 196616 | tf_op jit(solution)/shard_map/ppermute | solution.py:422
  9.6 7.3 %collective-permute-start.6 = (f32[5,4,16,128]{3,2,1,0:T(8,128)S(1)}, f32[5,4,16,128]{3,2,1,0:T(8,128)S(1)}, u32[]{:S(2)}, u32[]{:S(2)}) collective-permute-start(f32[5,4,16,128]{3,2,1,0:T(8,128)S(1)} %pad_maximum_fusion.mine_ref), channel_id=1, source_target_pairs={{0,56},{8,0},{16,8},{24,16},{32,24},{40,32},{48,40},{56,48},{1,57}... | collective-permute-start | bytes 491528 | tf_op jit(solution)/shard_map/ppermute | solution.py:428
  14.4 5.4 %collective-permute-start.5 = (f32[5,4,16,128]{3,2,1,0:T(8,128)S(1)}, f32[5,4,16,128]{3,2,1,0:T(8,128)S(1)}, u32[]{:S(2)}, u32[]{:S(2)}) collective-permute-start(f32[5,4,16,128]{3,2,1,0:T(8,128)S(1)} %pad_maximum_fusion.mine_ref), channel_id=1, source_target_pairs={{0,8},{8,16},{16,24},{24,32},{32,40},{40,48},{48,56},{56,0},{1,9},... | collective-permute-start | bytes 491528 | tf_op jit(solution)/shard_map/ppermute | solution.py:428
  14.4 5.4 %collective-permute-start.4 = (f32[5,4,16,128]{3,2,1,0:T(8,128)S(1)}, f32[5,4,16,128]{3,2,1,0:T(8,128)S(1)}, u32[]{:S(2)}, u32[]{:S(2)}) collective-permute-start(f32[5,4,16,128]{3,2,1,0:T(8,128)S(1)} %collective-permute-done.1.far_ref), channel_id=1, source_target_pairs={{0,64},{64,0},{128,192},{192,128},{1,65},{65,1},{129,193},{193,129... | collective-permute-start | bytes 491528 | tf_op jit(solution)/shard_map/ppermute | solution.py:428
  20.2 13.1 %collective-permute-start.10 = (f32[5,8,16,128]{3,2,1,0:T(8,128)S(1)}, f32[5,8,16,128]{3,2,1,0:T(8,128)S(1)}, u32[]{:S(2)}, u32[]{:S(2)}) collective-permute-start(f32[5,8,16,128]{3,2,1,0:T(8,128)S(1)} %get-tuple-element.27.own), channel_id=1, source_target_pairs={{0,56},{8,0},{16,8},{24,16},{32,24},{40,32},{48,40},{56,48},{1,57}... | collective-permute-start | bytes 983048 | tf_op jit(solution)/shard_map/ppermute | solution.py:428
  22.6 10.6 %collective-permute-start.9 = (f32[5,8,16,128]{3,2,1,0:T(8,128)S(1)}, f32[5,8,16,128]{3,2,1,0:T(8,128)S(1)}, u32[]{:S(2)}, u32[]{:S(2)}) collective-permute-start(f32[5,8,16,128]{3,2,1,0:T(8,128)S(1)} %get-tuple-element.27.own), channel_id=1, source_target_pairs={{0,8},{8,16},{16,24},{24,32},{32,40},{40,48},{48,56},{56,0},{1,9},... | collective-permute-start | bytes 983048 | tf_op jit(solution)/shard_map/ppermute | solution.py:428
  22.6 3.1 %collective-permute-start.7 = (f32[5,4,16,128]{3,2,1,0:T(8,128)S(1)}, f32[5,4,16,128]{3,2,1,0:T(8,128)S(1)}, u32[]{:S(2)}, u32[]{:S(2)}) collective-permute-start(f32[5,4,16,128]{3,2,1,0:T(8,128)S(1)} %collective-permute-done.5.low_mine), channel_id=1, source_target_pairs={{0,64},{64,0},{128,192},{192,128},{1,65},{65,1},{129,193},{193,129... | collective-permute-start | bytes 491528 | tf_op jit(solution)/shard_map/ppermute | solution.py:428
  24.7 1.4 %collective-permute-start.8 = (f32[5,4,16,128]{3,2,1,0:T(8,128)S(1)}, f32[5,4,16,128]{3,2,1,0:T(8,128)S(1)}, u32[]{:S(2)}, u32[]{:S(2)}) collective-permute-start(f32[5,4,16,128]{3,2,1,0:T(8,128)S(1)} %collective-permute-done.6.high_mine), channel_id=1, source_target_pairs={{0,64},{64,0},{128,192},{192,128},{1,65},{65,1},{129,193},{193,129... | collective-permute-start | bytes 491528 | tf_op jit(solution)/shard_map/ppermute | solution.py:428
  26.1 7.2 %collective-permute-start.11 = (f32[16,8,128]{2,1,0:T(8,128)S(1)}, f32[16,8,128]{2,1,0:T(8,128)S(1)}, u32[]{:S(2)}, u32[]{:S(2)}) collective-permute-start(f32[16,8,128]{2,1,0:T(8,128)S(1)} %get-tuple-element.34), channel_id=1, source_target_pairs={{0,16},{8,24},{16,32},{24,40},{32,48},{40,56},{48,0},{56,8},{1,17}... | collective-permute-start | bytes 196616 | tf_op jit(solution)/shard_map/ppermute | solution.py:428
  26.1 7.2 %collective-permute-start.12 = (f32[16,8,128]{2,1,0:T(8,128)S(1)}, f32[16,8,128]{2,1,0:T(8,128)S(1)}, u32[]{:S(2)}, u32[]{:S(2)}) collective-permute-start(f32[16,8,128]{2,1,0:T(8,128)S(1)} %get-tuple-element.35), channel_id=1, source_target_pairs={{0,48},{8,56},{16,0},{24,8},{32,16},{40,24},{48,32},{56,40},{1,49}... | collective-permute-start | bytes 196616 | tf_op jit(solution)/shard_map/ppermute | solution.py:428
  54.7 4.1 %collective-permute-start.13 = (f32[10,4,16,128]{3,2,1,0:T(8,128)S(1)}, f32[10,4,16,128]{3,2,1,0:T(8,128)S(1)}, u32[]{:S(2)}, u32[]{:S(2)}) collective-permute-start(f32[10,4,16,128]{3,2,1,0:T(8,128)S(1)} %get-tuple-element.37), channel_id=1, source_target_pairs={{0,64},{64,0},{128,192},{192,128},{1,65},{65,1},{129,193},{193,129... | collective-permute-start | bytes 983048 | tf_op jit(solution)/shard_map/ppermute | solution.py:428

commit v6 on v5

--- a/solution.py
+++ b/solution.py
@@ -196,8 +196,9 @@
 
 
 class Passes:
-    def __init__(self, pops, order, chem, rho, inv, vel):
+    def __init__(self, pops, order, chem, rho, inv, vel, order_next, chem_next):
         self.pops, self.orders, self.chems, self.rho, self.inv, self.vel = pops, order, chem, rho, inv, vel
+        self.order_next, self.chem_next = order_next, chem_next
 
     def run(self, first, count, names, offset=None, unroll=1):
         behind = {"collide": 0, "flow": -3, "order": -6, "chem": 3}
@@ -221,7 +222,9 @@
             beside = (order[up, pl.ds(r, 8), :] + order[down, pl.ds(r, 8), :]) + (
                 order[x, pl.ds(r + 1, 8), :] + order[x, pl.ds(r - 1, 8), :]
             )
-            beside = beside + (next_lane(here) + prev_lane(here))
+            after = next_lane(here)
+            self.order_next[step % 2][x, pl.ds(r, 8), :] = after
+            beside = beside + (after + prev_lane(here))
             chem[x, pl.ds(r, 8), :] = here * ((quadratic + 6.0 * stiffness) + quartic * (here * here)) - stiffness * beside
 
     def collide(self, step, x, up, down):
@@ -235,10 +238,12 @@
             density = rho[x, at, :]
             inverse = 1.0 / density if step == 0 else inv[x, at, :]
             pull = ((-0.5 * (-4.0) ** max(step - 1, 0)) * order[x, at, :]) * inverse
+            after = next_lane(mu)
+            self.chem_next[step % 2][x, at, :] = after
             kick = [
                 pull * (chem[up, at, :] - chem[down, at, :]),
                 pull * (chem[x, pl.ds(r + 1, 8), :] - chem[x, pl.ds(r - 1, 8), :]),
-                pull * (next_lane(mu) - prev_lane(mu)),
+                pull * (after - prev_lane(mu)),
             ]
             before = None if step == 0 else (lambda i: old[i, x, at, :])
             post = collide(density, [vel[d, x, at, :] for d in range(3)], kick, before)
@@ -273,11 +278,11 @@
             total = total + (uy + vel[1, x, north, :]) * (here + order[x, north, :])
             total = total - (uy + vel[1, x, south, :]) * (here + order[x, south, :])
             spread = (chem[up, at, :] + chem[down, at, :]) + (chem[x, north, :] + chem[x, south, :]) - 4.0 * mu
-            face = (0.25 * (uz + next_lane(uz))) * (here + next_lane(here)) - mobility * (next_lane(mu) - mu)
+            face = (0.25 * (uz + next_lane(uz))) * (here + self.order_next[now][x, at, :]) - mobility * (self.chem_next[now][x, at, :] - mu)
             self.orders[1 - now][x, at, :] = here - ((0.25 * total - mobility * spread) + (face - prev_lane(face)))
 
 
-def steps_kernel(core_ref, near, own, low_mine, low_other, low, high_mine, high_other, high, low2, high2, mine_ref, send_ref, pops_a, pops_b, order_a, order_b, chem_a, chem_b, rho_a, rho_b, inv_a, inv_b, vel_a, vel_b):
+def steps_kernel(core_ref, near, own, low_mine, low_other, low, high_mine, high_other, high, low2, high2, mine_ref, send_ref, pops_a, pops_b, order_a, order_b, chem_a, chem_b, rho_a, rho_b, inv_a, inv_b, vel_a, vel_b, shift_a, shift_b, shift_c, shift_d):
     core = core_ref[0]
 
     targets = (order_a, rho_b, vel_b.at[0], vel_b.at[1], vel_b.at[2])
@@ -327,7 +332,7 @@
 
     lax.fori_loop(0, NX // 2, load, 0)
 
-    passes = Passes((pops_a, pops_b), (order_a, order_b), (chem_a, chem_b), (rho_a, rho_b), (inv_a, inv_b), (vel_a, vel_b))
+    passes = Passes((pops_a, pops_b), (order_a, order_b), (chem_a, chem_b), (rho_a, rho_b), (inv_a, inv_b), (vel_a, vel_b), (shift_a, shift_b), (shift_c, shift_d))
     run = passes.run
     run(0, NX, [("chem", 0)], offset=0, unroll=4)
     for step in range(ITERS - 1):
@@ -403,7 +408,7 @@
     return vmem_call(
         steps_kernel,
         [(20, 4, BY, LANES), (10, 4, BY, LANES)],
-        [(19,) + field] * 2 + [field] * 8 + [(3,) + field] * 2,
+        [(19,) + field] * 2 + [field] * 8 + [(3,) + field] * 2 + [field] * 4,
         40 << 20,
     )
 

time: 59.9 us -> 59.2 us (0.988)
  Pallas kernels: 22.9 us -> 22.3 us
    pallas_call x4, Pallas kernels: 22.9 us -> 22.3 us  [call(): pl.pallas_call(kernel, out_shape=[jax.ShapeDtypeStruct(s, F32) for s in o...]
where the time goes in v6:
time: 59.2 us; the launch traced here: 59.1 us
  starting transfers between devices  25 us (42%)
  Pallas kernels  22.3 us (38%)
  waiting for transfers between devices  10.3 us (17%)
  other arithmetic  0.93 us (2%)
  between operations  0.68 us (1%)
    pallas_call x4, Pallas kernels, call(): pl.pallas_call(kernel, out_shape=[jax.ShapeDtypeStruct(s, F32) for s in o...  22.3 us
    ppermute x12, starting transfers between devices, along(): lax.ppermute(value, axis, [(i, to(i) % lax.axis_size(axis)) for i in rang...  21.6 us
    ppermute x12, waiting for transfers between devices, along(): lax.ppermute(value, axis, [(i, to(i) % lax.axis_size(axis)) for i in rang...  10.3 us
    ppermute x2, starting transfers between devices, send(): return lax.ppermute(value, AXES, pairs)  3.34 us
  transfers between devices with their start and end apart: 14, of which 6 were waited for; matrix products, arithmetic and copies ran while one was open for 0% of the time, Pallas kernels for 0%

profile of v6, /device:TPU:1, one launch (start us, length us, event | category | flops | bytes accessed | tf_op | source)
XLA Modules:
  0.0 59.1 jit_solution(876042116408222872)
XLA Ops:
  0.6 0.9 %pad_maximum_fusion.mine_ref = f32[5,4,16,128]{3,2,1,0:T(8,128)S(1)} fusion(f32[3,4,16,128]{3,2,1,0:T(8,128)} %param.5, f32[1,4,16,128]{3,2,1,0:T(8,128)} %bitcast.3, f32[1,4,16,128]{3,2,1,0:T(8,128)} %bitcast.4), kind=kLoop, calls=%fused_computation | loop fusion | flops 81920 | bytes 327680 | tf_op jit(solution)/shard_map/concatenate | solution.py:431
  1.6 3.3 %collective-permute-start = (f32[5,4,16,128]{3,2,1,0:T(8,128)S(1)}, f32[5,4,16,128]{3,2,1,0:T(8,128)S(1)}, u32[]{:S(2)}, u32[]{:S(2)}) collective-permute-start(f32[5,4,16,128]{3,2,1,0:T(8,128)S(1)} %pad_maximum_fusion.mine_ref), channel_id=1, source_target_pairs={{0,64},{64,0},{128,192},{192,128},{1,65},{65,1},{129,193},{193,129... | collective-permute-start | bytes 491528 | tf_op jit(solution)/shard_map/ppermute | solution.py:433
  4.9 1.2 %collective-permute-start.1 = (f32[5,4,16,128]{3,2,1,0:T(8,128)S(1)}, f32[5,4,16,128]{3,2,1,0:T(8,128)S(1)}, u32[]{:S(2)}, u32[]{:S(2)}) collective-permute-start(f32[5,4,16,128]{3,2,1,0:T(8,128)S(1)} %pad_maximum_fusion.mine_ref), channel_id=1, source_target_pairs={{0,128},{64,192},{128,0},{192,64},{1,129},{65,193},{129,1},{193,65... | collective-permute-start | bytes 491528 | tf_op jit(solution)/shard_map/ppermute | solution.py:433
  6.1 0.0 collective-permute-done.other_ref
  6.1 0.1 shard_map.50
  6.2 2.3 %collective-permute-start.3 = (f32[8,16,128]{2,1,0:T(8,128)S(1)}, f32[8,16,128]{2,1,0:T(8,128)S(1)}, u32[]{:S(2)}, u32[]{:S(2)}) collective-permute-start(f32[8,16,128]{2,1,0:T(8,128)S(1)} %get-tuple-element.21), channel_id=1, source_target_pairs={{0,199},{1,192},{2,193},{3,194},{4,195},{5,196},{6,197},{7,198},{8... | collective-permute-start | bytes 196616 | tf_op jit(solution)/shard_map/ppermute | solution.py:427
  8.5 1.1 %collective-permute-start.2 = (f32[8,16,128]{2,1,0:T(8,128)S(1)}, f32[8,16,128]{2,1,0:T(8,128)S(1)}, u32[]{:S(2)}, u32[]{:S(2)}) collective-permute-start(f32[8,16,128]{2,1,0:T(8,128)S(1)} %get-tuple-element.21), channel_id=1, source_target_pairs={{0,71},{1,64},{2,65},{3,66},{4,67},{5,68},{6,69},{7,70},{8,79},{9,... | collective-permute-start | bytes 196616 | tf_op jit(solution)/shard_map/ppermute | solution.py:427
  9.6 4.8 %collective-permute-start.6 = (f32[5,4,16,128]{3,2,1,0:T(8,128)S(1)}, f32[5,4,16,128]{3,2,1,0:T(8,128)S(1)}, u32[]{:S(2)}, u32[]{:S(2)}) collective-permute-start(f32[5,4,16,128]{3,2,1,0:T(8,128)S(1)} %pad_maximum_fusion.mine_ref), channel_id=1, source_target_pairs={{0,56},{8,0},{16,8},{24,16},{32,24},{40,32},{48,40},{56,48},{1,57}... | collective-permute-start | bytes 491528 | tf_op jit(solution)/shard_map/ppermute | solution.py:433
  14.4 0.0 collective-permute-start.5
  14.4 0.0 collective-permute-done.1.far_ref
  14.4 0.0 collective-permute-done.3.far_edge
  14.4 0.0 collective-permute-done.2.near_edge
  14.4 1.3 %collective-permute-start.4 = (f32[5,4,16,128]{3,2,1,0:T(8,128)S(1)}, f32[5,4,16,128]{3,2,1,0:T(8,128)S(1)}, u32[]{:S(2)}, u32[]{:S(2)}) collective-permute-start(f32[5,4,16,128]{3,2,1,0:T(8,128)S(1)} %collective-permute-done.1.far_ref), channel_id=1, source_target_pairs={{0,64},{64,0},{128,192},{192,128},{1,65},{65,1},{129,193},{193,129... | collective-permute-start | bytes 491528 | tf_op jit(solution)/shard_map/ppermute | solution.py:433
  15.7 1.2 %collective-permute-done.6.high_mine = f32[5,4,16,128]{3,2,1,0:T(8,128)S(1)} collective-permute-done((f32[5,4,16,128]{3,2,1,0:T(8,128)S(1)}, f32[5,4,16,128]{3,2,1,0:T(8,128)S(1)}, u32[]{:S(2)}, u32[]{:S(2)}) %collective-permute-start.6) | collective-permute-done | bytes 163872 | tf_op jit(solution)/shard_map/ppermute | solution.py:433
  16.9 2.9 %collective-permute-done.5.low_mine = f32[5,4,16,128]{3,2,1,0:T(8,128)S(1)} collective-permute-done((f32[5,4,16,128]{3,2,1,0:T(8,128)S(1)}, f32[5,4,16,128]{3,2,1,0:T(8,128)S(1)}, u32[]{:S(2)}, u32[]{:S(2)}) %collective-permute-start.5) | collective-permute-done | bytes 163872 | tf_op jit(solution)/shard_map/ppermute | solution.py:433
  19.7 0.0 collective-permute-done.4.other_ref
  19.7 0.4 shard_map.51
  20.2 2.5 %collective-permute-start.10 = (f32[5,8,16,128]{3,2,1,0:T(8,128)S(1)}, f32[5,8,16,128]{3,2,1,0:T(8,128)S(1)}, u32[]{:S(2)}, u32[]{:S(2)}) collective-permute-start(f32[5,8,16,128]{3,2,1,0:T(8,128)S(1)} %get-tuple-element.27.own), channel_id=1, source_target_pairs={{0,56},{8,0},{16,8},{24,16},{32,24},{40,32},{48,40},{56,48},{1,57}... | collective-permute-start | bytes 983048 | tf_op jit(solution)/shard_map/ppermute | solution.py:433
  22.6 0.0 collective-permute-start.9
  22.6 2.1 %collective-permute-start.7 = (f32[5,4,16,128]{3,2,1,0:T(8,128)S(1)}, f32[5,4,16,128]{3,2,1,0:T(8,128)S(1)}, u32[]{:S(2)}, u32[]{:S(2)}) collective-permute-start(f32[5,4,16,128]{3,2,1,0:T(8,128)S(1)} %collective-permute-done.5.low_mine), channel_id=1, source_target_pairs={{0,64},{64,0},{128,192},{192,128},{1,65},{65,1},{129,193},{193,129... | collective-permute-start | bytes 491528 | tf_op jit(solution)/shard_map/ppermute | solution.py:433
  24.7 0.0 collective-permute-start.8
  24.7 1.0 %collective-permute-done.7.low_other = f32[5,4,16,128]{3,2,1,0:T(8,128)S(1)} collective-permute-done((f32[5,4,16,128]{3,2,1,0:T(8,128)S(1)}, f32[5,4,16,128]{3,2,1,0:T(8,128)S(1)}, u32[]{:S(2)}, u32[]{:S(2)}) %collective-permute-start.7) | collective-permute-done | bytes 163872 | tf_op jit(solution)/shard_map/ppermute | solution.py:433
  25.7 0.4 collective-permute-done.8.high_other
  26.1 0.0 collective-permute-start.11
  26.1 3.6 %collective-permute-start.12 = (f32[16,8,128]{2,1,0:T(8,128)S(1)}, f32[16,8,128]{2,1,0:T(8,128)S(1)}, u32[]{:S(2)}, u32[]{:S(2)}) collective-permute-start(f32[16,8,128]{2,1,0:T(8,128)S(1)} %get-tuple-element.35), channel_id=1, source_target_pairs={{0,48},{8,56},{16,0},{24,8},{32,16},{40,24},{48,32},{56,40},{1,49}... | collective-permute-start | bytes 196616 | tf_op jit(solution)/shard_map/ppermute | solution.py:433
  29.7 3.6 %collective-permute-done.11.low2 = f32[16,8,128]{2,1,0:T(8,128)S(1)} collective-permute-done((f32[16,8,128]{2,1,0:T(8,128)S(1)}, f32[16,8,128]{2,1,0:T(8,128)S(1)}, u32[]{:S(2)}, u32[]{:S(2)}) %collective-permute-start.11) | collective-permute-done | bytes 65568 | tf_op jit(solution)/shard_map/ppermute | solution.py:433
  33.3 0.0 collective-permute-done.12.high2
  33.3 0.0 collective-permute-done.10.high
  33.3 0.0 collective-permute-done.9.low
  33.3 20.7 %shard_map.52 = (f32[20,4,16,128]{3,2,1,0:T(8,128)S(1)}, f32[10,4,16,128]{3,2,1,0:T(8,128)S(1)}) custom-call(s32[1]{0:T(128)} %bitcast.core_ref, f32[5,8,16,128]{3,2,1,0:T(8,128)S(1)} %get-tuple-element.20.near_ref.near, f32[5,8,16,128]{3,2,1,0:T(8,128)S(1)} %get-tuple-element.27.own, f32[5,4,16,128]{3,2,1,0:T(8,128)S(1)} %collective-permute-done.5.low_mine, ...), custom_call_target="tpu_custom_call" | custom-call | tf_op jit(solution)/shard_map/pallas_call | solution.py:394
  54.0 2.9 %collective-permute-start.13 = (f32[10,4,16,128]{3,2,1,0:T(8,128)S(1)}, f32[10,4,16,128]{3,2,1,0:T(8,128)S(1)}, u32[]{:S(2)}, u32[]{:S(2)}) collective-permute-start(f32[10,4,16,128]{3,2,1,0:T(8,128)S(1)} %get-tuple-element.37), channel_id=1, source_target_pairs={{0,64},{64,0},{128,192},{192,128},{1,65},{65,1},{129,193},{193,129... | collective-permute-start | bytes 983048 | tf_op jit(solution)/shard_map/ppermute | solution.py:433
  56.9 1.3 %collective-permute-done.13.back_ref = f32[10,4,16,128]{3,2,1,0:T(8,128)S(1)} collective-permute-done((f32[10,4,16,128]{3,2,1,0:T(8,128)S(1)}, f32[10,4,16,128]{3,2,1,0:T(8,128)S(1)}, u32[]{:S(2)}, u32[]{:S(2)}) %collective-permute-start.13) | collective-permute-done | bytes 327712 | tf_op jit(solution)/shard_map/ppermute | solution.py:433
  58.1 1.0 %shard_map.53 = (f32[4,16,128]{2,1,0:T(8,128)}, f32[19,4,16,128]{3,2,1,0:T(8,128)}) custom-call(s32[1]{0:T(128)} %bitcast.core_ref, f32[20,4,16,128]{3,2,1,0:T(8,128)S(1)} %get-tuple-element.36.mine_ref, f32[10,4,16,128]{3,2,1,0:T(8,128)S(1)} %collective-permute-done.13.back_ref), custom_call_target="tpu_custom_call" | custom-call | tf_op jit(solution)/shard_map/pallas_call | solution.py:394
Async XLA Ops:
  1.6 4.5 %collective-permute-start = (f32[5,4,16,128]{3,2,1,0:T(8,128)S(1)}, f32[5,4,16,128]{3,2,1,0:T(8,128)S(1)}, u32[]{:S(2)}, u32[]{:S(2)}) collective-permute-start(f32[5,4,16,128]{3,2,1,0:T(8,128)S(1)} %pad_maximum_fusion.mine_ref), channel_id=1, source_target_pairs={{0,64},{64,0},{128,192},{192,128},{1,65},{65,1},{129,193},{193,129... | collective-permute-start | bytes 491528 | tf_op jit(solution)/shard_map/ppermute | solution.py:433
  4.9 9.5 %collective-permute-start.1 = (f32[5,4,16,128]{3,2,1,0:T(8,128)S(1)}, f32[5,4,16,128]{3,2,1,0:T(8,128)S(1)}, u32[]{:S(2)}, u32[]{:S(2)}) collective-permute-start(f32[5,4,16,128]{3,2,1,0:T(8,128)S(1)} %pad_maximum_fusion.mine_ref), channel_id=1, source_target_pairs={{0,128},{64,192},{128,0},{192,64},{1,129},{65,193},{129,1},{193,65... | collective-permute-start | bytes 491528 | tf_op jit(solution)/shard_map/ppermute | solution.py:433
  6.2 8.1 %collective-permute-start.3 = (f32[8,16,128]{2,1,0:T(8,128)S(1)}, f32[8,16,128]{2,1,0:T(8,128)S(1)}, u32[]{:S(2)}, u32[]{:S(2)}) collective-permute-start(f32[8,16,128]{2,1,0:T(8,128)S(1)} %get-tuple-element.21), channel_id=1, source_target_pairs={{0,199},{1,192},{2,193},{3,194},{4,195},{5,196},{6,197},{7,198},{8... | collective-permute-start | bytes 196616 | tf_op jit(solution)/shard_map/ppermute | solution.py:427
  8.5 5.9 %collective-permute-start.2 = (f32[8,16,128]{2,1,0:T(8,128)S(1)}, f32[8,16,128]{2,1,0:T(8,128)S(1)}, u32[]{:S(2)}, u32[]{:S(2)}) collective-permute-start(f32[8,16,128]{2,1,0:T(8,128)S(1)} %get-tuple-element.21), channel_id=1, source_target_pairs={{0,71},{1,64},{2,65},{3,66},{4,67},{5,68},{6,69},{7,70},{8,79},{9,... | collective-permute-start | bytes 196616 | tf_op jit(solution)/shard_map/ppermute | solution.py:427
  9.6 7.3 %collective-permute-start.6 = (f32[5,4,16,128]{3,2,1,0:T(8,128)S(1)}, f32[5,4,16,128]{3,2,1,0:T(8,128)S(1)}, u32[]{:S(2)}, u32[]{:S(2)}) collective-permute-start(f32[5,4,16,128]{3,2,1,0:T(8,128)S(1)} %pad_maximum_fusion.mine_ref), channel_id=1, source_target_pairs={{0,56},{8,0},{16,8},{24,16},{32,24},{40,32},{48,40},{56,48},{1,57}... | collective-permute-start | bytes 491528 | tf_op jit(solution)/shard_map/ppermute | solution.py:433
  14.4 5.4 %collective-permute-start.5 = (f32[5,4,16,128]{3,2,1,0:T(8,128)S(1)}, f32[5,4,16,128]{3,2,1,0:T(8,128)S(1)}, u32[]{:S(2)}, u32[]{:S(2)}) collective-permute-start(f32[5,4,16,128]{3,2,1,0:T(8,128)S(1)} %pad_maximum_fusion.mine_ref), channel_id=1, source_target_pairs={{0,8},{8,16},{16,24},{24,32},{32,40},{40,48},{48,56},{56,0},{1,9},... | collective-permute-start | bytes 491528 | tf_op jit(solution)/shard_map/ppermute | solution.py:433
  14.4 5.4 %collective-permute-start.4 = (f32[5,4,16,128]{3,2,1,0:T(8,128)S(1)}, f32[5,4,16,128]{3,2,1,0:T(8,128)S(1)}, u32[]{:S(2)}, u32[]{:S(2)}) collective-permute-start(f32[5,4,16,128]{3,2,1,0:T(8,128)S(1)} %collective-permute-done.1.far_ref), channel_id=1, source_target_pairs={{0,64},{64,0},{128,192},{192,128},{1,65},{65,1},{129,193},{193,129... | collective-permute-start | bytes 491528 | tf_op jit(solution)/shard_map/ppermute | solution.py:433
  20.2 13.1 %collective-permute-start.10 = (f32[5,8,16,128]{3,2,1,0:T(8,128)S(1)}, f32[5,8,16,128]{3,2,1,0:T(8,128)S(1)}, u32[]{:S(2)}, u32[]{:S(2)}) collective-permute-start(f32[5,8,16,128]{3,2,1,0:T(8,128)S(1)} %get-tuple-element.27.own), channel_id=1, source_target_pairs={{0,56},{8,0},{16,8},{24,16},{32,24},{40,32},{48,40},{56,48},{1,57}... | collective-permute-start | bytes 983048 | tf_op jit(solution)/shard_map/ppermute | solution.py:433
  22.6 10.6 %collective-permute-start.9 = (f32[5,8,16,128]{3,2,1,0:T(8,128)S(1)}, f32[5,8,16,128]{3,2,1,0:T(8,128)S(1)}, u32[]{:S(2)}, u32[]{:S(2)}) collective-permute-start(f32[5,8,16,128]{3,2,1,0:T(8,128)S(1)} %get-tuple-element.27.own), channel_id=1, source_target_pairs={{0,8},{8,16},{16,24},{24,32},{32,40},{40,48},{48,56},{56,0},{1,9},... | collective-permute-start | bytes 983048 | tf_op jit(solution)/shard_map/ppermute | solution.py:433
  22.6 3.1 %collective-permute-start.7 = (f32[5,4,16,128]{3,2,1,0:T(8,128)S(1)}, f32[5,4,16,128]{3,2,1,0:T(8,128)S(1)}, u32[]{:S(2)}, u32[]{:S(2)}) collective-permute-start(f32[5,4,16,128]{3,2,1,0:T(8,128)S(1)} %collective-permute-done.5.low_mine), channel_id=1, source_target_pairs={{0,64},{64,0},{128,192},{192,128},{1,65},{65,1},{129,193},{193,129... | collective-permute-start | bytes 491528 | tf_op jit(solution)/shard_map/ppermute | solution.py:433
  24.7 1.4 %collective-permute-start.8 = (f32[5,4,16,128]{3,2,1,0:T(8,128)S(1)}, f32[5,4,16,128]{3,2,1,0:T(8,128)S(1)}, u32[]{:S(2)}, u32[]{:S(2)}) collective-permute-start(f32[5,4,16,128]{3,2,1,0:T(8,128)S(1)} %collective-permute-done.6.high_mine), channel_id=1, source_target_pairs={{0,64},{64,0},{128,192},{192,128},{1,65},{65,1},{129,193},{193,129... | collective-permute-start | bytes 491528 | tf_op jit(solution)/shard_map/ppermute | solution.py:433
  26.1 7.2 %collective-permute-start.11 = (f32[16,8,128]{2,1,0:T(8,128)S(1)}, f32[16,8,128]{2,1,0:T(8,128)S(1)}, u32[]{:S(2)}, u32[]{:S(2)}) collective-permute-start(f32[16,8,128]{2,1,0:T(8,128)S(1)} %get-tuple-element.34), channel_id=1, source_target_pairs={{0,16},{8,24},{16,32},{24,40},{32,48},{40,56},{48,0},{56,8},{1,17}... | collective-permute-start | bytes 196616 | tf_op jit(solution)/shard_map/ppermute | solution.py:433
  26.1 7.2 %collective-permute-start.12 = (f32[16,8,128]{2,1,0:T(8,128)S(1)}, f32[16,8,128]{2,1,0:T(8,128)S(1)}, u32[]{:S(2)}, u32[]{:S(2)}) collective-permute-start(f32[16,8,128]{2,1,0:T(8,128)S(1)} %get-tuple-element.35), channel_id=1, source_target_pairs={{0,48},{8,56},{16,0},{24,8},{32,16},{40,24},{48,32},{56,40},{1,49}... | collective-permute-start | bytes 196616 | tf_op jit(solution)/shard_map/ppermute | solution.py:433
  54.0 4.1 %collective-permute-start.13 = (f32[10,4,16,128]{3,2,1,0:T(8,128)S(1)}, f32[10,4,16,128]{3,2,1,0:T(8,128)S(1)}, u32[]{:S(2)}, u32[]{:S(2)}) collective-permute-start(f32[10,4,16,128]{3,2,1,0:T(8,128)S(1)} %get-tuple-element.37), channel_id=1, source_target_pairs={{0,64},{64,0},{128,192},{192,128},{1,65},{65,1},{129,193},{193,129... | collective-permute-start | bytes 983048 | tf_op jit(solution)/shard_map/ppermute | solution.py:433

commit v7 on v6

--- a/solution.py
+++ b/solution.py
@@ -314,7 +314,7 @@
                 order_a[x + 8, pl.ds(row, 16), :] = order
         return 0
 
-    lax.fori_loop(0, 4, load_block, 0)
+    lax.fori_loop(0, 4, load_block, 0, unroll=2)
 
     _, first_half = far_row_lanes(core, (2, LANES))
 
@@ -330,7 +330,7 @@
                     order_a[x, pl.ds(order_row + k, 2), :] = both
         return 0
 
-    lax.fori_loop(0, NX // 2, load, 0)
+    lax.fori_loop(0, NX // 2, load, 0, unroll=4)
 
     passes = Passes((pops_a, pops_b), (order_a, order_b), (chem_a, chem_b), (rho_a, rho_b), (inv_a, inv_b), (vel_a, vel_b), (shift_a, shift_b), (shift_c, shift_d))
     run = passes.run

time: 59.2 us -> 58.7 us (level)
  Pallas kernels: 22.3 us -> 21.7 us
where the time goes in v7:
time: 58.7 us; the launch traced here: 58.6 us
  starting transfers between devices  25 us (43%)
  Pallas kernels  21.7 us (37%)
  waiting for transfers between devices  10.3 us (18%)
  other arithmetic  0.93 us (2%)
  between operations  0.68 us (1%)
    pallas_call x4, Pallas kernels, call(): pl.pallas_call(kernel, out_shape=[jax.ShapeDtypeStruct(s, F32) for s in o...  21.7 us
    ppermute x12, starting transfers between devices, along(): lax.ppermute(value, axis, [(i, to(i) % lax.axis_size(axis)) for i in rang...  21.6 us
    ppermute x12, waiting for transfers between devices, along(): lax.ppermute(value, axis, [(i, to(i) % lax.axis_size(axis)) for i in rang...  10.3 us
    ppermute x2, starting transfers between devices, send(): return lax.ppermute(value, AXES, pairs)  3.34 us
  transfers between devices with their start and end apart: 14, of which 6 were waited for; matrix products, arithmetic and copies ran while one was open for 0% of the time, Pallas kernels for 0%

profile of v7, /device:TPU:1, one launch (start us, length us, event | category | flops | bytes accessed | tf_op | source)
XLA Modules:
  0.0 58.6 jit_solution(7444238072261796032)
XLA Ops:
  0.6 0.9 %pad_maximum_fusion.mine_ref = f32[5,4,16,128]{3,2,1,0:T(8,128)S(1)} fusion(f32[3,4,16,128]{3,2,1,0:T(8,128)} %param.5, f32[1,4,16,128]{3,2,1,0:T(8,128)} %bitcast.3, f32[1,4,16,128]{3,2,1,0:T(8,128)} %bitcast.4), kind=kLoop, calls=%fused_computation | loop fusion | flops 81920 | bytes 327680 | tf_op jit(solution)/shard_map/concatenate | solution.py:431
  1.6 3.3 %collective-permute-start = (f32[5,4,16,128]{3,2,1,0:T(8,128)S(1)}, f32[5,4,16,128]{3,2,1,0:T(8,128)S(1)}, u32[]{:S(2)}, u32[]{:S(2)}) collective-permute-start(f32[5,4,16,128]{3,2,1,0:T(8,128)S(1)} %pad_maximum_fusion.mine_ref), channel_id=1, source_target_pairs={{0,64},{64,0},{128,192},{192,128},{1,65},{65,1},{129,193},{193,129... | collective-permute-start | bytes 491528 | tf_op jit(solution)/shard_map/ppermute | solution.py:433
  4.9 1.2 %collective-permute-start.1 = (f32[5,4,16,128]{3,2,1,0:T(8,128)S(1)}, f32[5,4,16,128]{3,2,1,0:T(8,128)S(1)}, u32[]{:S(2)}, u32[]{:S(2)}) collective-permute-start(f32[5,4,16,128]{3,2,1,0:T(8,128)S(1)} %pad_maximum_fusion.mine_ref), channel_id=1, source_target_pairs={{0,128},{64,192},{128,0},{192,64},{1,129},{65,193},{129,1},{193,65... | collective-permute-start | bytes 491528 | tf_op jit(solution)/shard_map/ppermute | solution.py:433
  6.1 0.0 collective-permute-done.other_ref
  6.1 0.1 shard_map.50
  6.2 2.3 %collective-permute-start.3 = (f32[8,16,128]{2,1,0:T(8,128)S(1)}, f32[8,16,128]{2,1,0:T(8,128)S(1)}, u32[]{:S(2)}, u32[]{:S(2)}) collective-permute-start(f32[8,16,128]{2,1,0:T(8,128)S(1)} %get-tuple-element.21), channel_id=1, source_target_pairs={{0,199},{1,192},{2,193},{3,194},{4,195},{5,196},{6,197},{7,198},{8... | collective-permute-start | bytes 196616 | tf_op jit(solution)/shard_map/ppermute | solution.py:427
  8.5 1.1 %collective-permute-start.2 = (f32[8,16,128]{2,1,0:T(8,128)S(1)}, f32[8,16,128]{2,1,0:T(8,128)S(1)}, u32[]{:S(2)}, u32[]{:S(2)}) collective-permute-start(f32[8,16,128]{2,1,0:T(8,128)S(1)} %get-tuple-element.21), channel_id=1, source_target_pairs={{0,71},{1,64},{2,65},{3,66},{4,67},{5,68},{6,69},{7,70},{8,79},{9,... | collective-permute-start | bytes 196616 | tf_op jit(solution)/shard_map/ppermute | solution.py:427
  9.6 4.8 %collective-permute-start.6 = (f32[5,4,16,128]{3,2,1,0:T(8,128)S(1)}, f32[5,4,16,128]{3,2,1,0:T(8,128)S(1)}, u32[]{:S(2)}, u32[]{:S(2)}) collective-permute-start(f32[5,4,16,128]{3,2,1,0:T(8,128)S(1)} %pad_maximum_fusion.mine_ref), channel_id=1, source_target_pairs={{0,56},{8,0},{16,8},{24,16},{32,24},{40,32},{48,40},{56,48},{1,57}... | collective-permute-start | bytes 491528 | tf_op jit(solution)/shard_map/ppermute | solution.py:433
  14.4 0.0 collective-permute-start.5
  14.4 0.0 collective-permute-done.1.far_ref
  14.4 0.0 collective-permute-done.3.far_edge
  14.4 0.0 collective-permute-done.2.near_edge
  14.4 1.3 %collective-permute-start.4 = (f32[5,4,16,128]{3,2,1,0:T(8,128)S(1)}, f32[5,4,16,128]{3,2,1,0:T(8,128)S(1)}, u32[]{:S(2)}, u32[]{:S(2)}) collective-permute-start(f32[5,4,16,128]{3,2,1,0:T(8,128)S(1)} %collective-permute-done.1.far_ref), channel_id=1, source_target_pairs={{0,64},{64,0},{128,192},{192,128},{1,65},{65,1},{129,193},{193,129... | collective-permute-start | bytes 491528 | tf_op jit(solution)/shard_map/ppermute | solution.py:433
  15.7 1.2 %collective-permute-done.6.high_mine = f32[5,4,16,128]{3,2,1,0:T(8,128)S(1)} collective-permute-done((f32[5,4,16,128]{3,2,1,0:T(8,128)S(1)}, f32[5,4,16,128]{3,2,1,0:T(8,128)S(1)}, u32[]{:S(2)}, u32[]{:S(2)}) %collective-permute-start.6) | collective-permute-done | bytes 163872 | tf_op jit(solution)/shard_map/ppermute | solution.py:433
  16.9 2.9 %collective-permute-done.5.low_mine = f32[5,4,16,128]{3,2,1,0:T(8,128)S(1)} collective-permute-done((f32[5,4,16,128]{3,2,1,0:T(8,128)S(1)}, f32[5,4,16,128]{3,2,1,0:T(8,128)S(1)}, u32[]{:S(2)}, u32[]{:S(2)}) %collective-permute-start.5) | collective-permute-done | bytes 163872 | tf_op jit(solution)/shard_map/ppermute | solution.py:433
  19.7 0.0 collective-permute-done.4.other_ref
  19.7 0.4 shard_map.51
  20.2 2.5 %collective-permute-start.10 = (f32[5,8,16,128]{3,2,1,0:T(8,128)S(1)}, f32[5,8,16,128]{3,2,1,0:T(8,128)S(1)}, u32[]{:S(2)}, u32[]{:S(2)}) collective-permute-start(f32[5,8,16,128]{3,2,1,0:T(8,128)S(1)} %get-tuple-element.27.own), channel_id=1, source_target_pairs={{0,56},{8,0},{16,8},{24,16},{32,24},{40,32},{48,40},{56,48},{1,57}... | collective-permute-start | bytes 983048 | tf_op jit(solution)/shard_map/ppermute | solution.py:433
  22.6 0.0 collective-permute-start.9
  22.6 2.1 %collective-permute-start.7 = (f32[5,4,16,128]{3,2,1,0:T(8,128)S(1)}, f32[5,4,16,128]{3,2,1,0:T(8,128)S(1)}, u32[]{:S(2)}, u32[]{:S(2)}) collective-permute-start(f32[5,4,16,128]{3,2,1,0:T(8,128)S(1)} %collective-permute-done.5.low_mine), channel_id=1, source_target_pairs={{0,64},{64,0},{128,192},{192,128},{1,65},{65,1},{129,193},{193,129... | collective-permute-start | bytes 491528 | tf_op jit(solution)/shard_map/ppermute | solution.py:433
  24.7 0.0 collective-permute-start.8
  24.7 1.0 %collective-permute-done.7.low_other = f32[5,4,16,128]{3,2,1,0:T(8,128)S(1)} collective-permute-done((f32[5,4,16,128]{3,2,1,0:T(8,128)S(1)}, f32[5,4,16,128]{3,2,1,0:T(8,128)S(1)}, u32[]{:S(2)}, u32[]{:S(2)}) %collective-permute-start.7) | collective-permute-done | bytes 163872 | tf_op jit(solution)/shard_map/ppermute | solution.py:433
  25.7 0.4 collective-permute-done.8.high_other
  26.1 0.0 collective-permute-start.11
  26.1 3.6 %collective-permute-start.12 = (f32[16,8,128]{2,1,0:T(8,128)S(1)}, f32[16,8,128]{2,1,0:T(8,128)S(1)}, u32[]{:S(2)}, u32[]{:S(2)}) collective-permute-start(f32[16,8,128]{2,1,0:T(8,128)S(1)} %get-tuple-element.35), channel_id=1, source_target_pairs={{0,48},{8,56},{16,0},{24,8},{32,16},{40,24},{48,32},{56,40},{1,49}... | collective-permute-start | bytes 196616 | tf_op jit(solution)/shard_map/ppermute | solution.py:433
  29.7 3.6 %collective-permute-done.11.low2 = f32[16,8,128]{2,1,0:T(8,128)S(1)} collective-permute-done((f32[16,8,128]{2,1,0:T(8,128)S(1)}, f32[16,8,128]{2,1,0:T(8,128)S(1)}, u32[]{:S(2)}, u32[]{:S(2)}) %collective-permute-start.11) | collective-permute-done | bytes 65568 | tf_op jit(solution)/shard_map/ppermute | solution.py:433
  33.3 0.0 collective-permute-done.12.high2
  33.3 0.0 collective-permute-done.10.high
  33.3 0.0 collective-permute-done.9.low
  33.3 20.2 %shard_map.52 = (f32[20,4,16,128]{3,2,1,0:T(8,128)S(1)}, f32[10,4,16,128]{3,2,1,0:T(8,128)S(1)}) custom-call(s32[1]{0:T(128)} %bitcast.core_ref, f32[5,8,16,128]{3,2,1,0:T(8,128)S(1)} %get-tuple-element.20.near_ref.near, f32[5,8,16,128]{3,2,1,0:T(8,128)S(1)} %get-tuple-element.27.own, f32[5,4,16,128]{3,2,1,0:T(8,128)S(1)} %collective-permute-done.5.low_mine, ...), custom_call_target="tpu_custom_call" | custom-call | tf_op jit(solution)/shard_map/pallas_call | solution.py:394
  53.5 2.9 %collective-permute-start.13 = (f32[10,4,16,128]{3,2,1,0:T(8,128)S(1)}, f32[10,4,16,128]{3,2,1,0:T(8,128)S(1)}, u32[]{:S(2)}, u32[]{:S(2)}) collective-permute-start(f32[10,4,16,128]{3,2,1,0:T(8,128)S(1)} %get-tuple-element.37), channel_id=1, source_target_pairs={{0,64},{64,0},{128,192},{192,128},{1,65},{65,1},{129,193},{193,129... | collective-permute-start | bytes 983048 | tf_op jit(solution)/shard_map/ppermute | solution.py:433
  56.4 1.3 %collective-permute-done.13.back_ref = f32[10,4,16,128]{3,2,1,0:T(8,128)S(1)} collective-permute-done((f32[10,4,16,128]{3,2,1,0:T(8,128)S(1)}, f32[10,4,16,128]{3,2,1,0:T(8,128)S(1)}, u32[]{:S(2)}, u32[]{:S(2)}) %collective-permute-start.13) | collective-permute-done | bytes 327712 | tf_op jit(solution)/shard_map/ppermute | solution.py:433
  57.6 1.0 %shard_map.53 = (f32[4,16,128]{2,1,0:T(8,128)}, f32[19,4,16,128]{3,2,1,0:T(8,128)}) custom-call(s32[1]{0:T(128)} %bitcast.core_ref, f32[20,4,16,128]{3,2,1,0:T(8,128)S(1)} %get-tuple-element.36.mine_ref, f32[10,4,16,128]{3,2,1,0:T(8,128)S(1)} %collective-permute-done.13.back_ref), custom_call_target="tpu_custom_call" | custom-call | tf_op jit(solution)/shard_map/pallas_call | solution.py:394
Async XLA Ops:
  1.6 4.5 %collective-permute-start = (f32[5,4,16,128]{3,2,1,0:T(8,128)S(1)}, f32[5,4,16,128]{3,2,1,0:T(8,128)S(1)}, u32[]{:S(2)}, u32[]{:S(2)}) collective-permute-start(f32[5,4,16,128]{3,2,1,0:T(8,128)S(1)} %pad_maximum_fusion.mine_ref), channel_id=1, source_target_pairs={{0,64},{64,0},{128,192},{192,128},{1,65},{65,1},{129,193},{193,129... | collective-permute-start | bytes 491528 | tf_op jit(solution)/shard_map/ppermute | solution.py:433
  4.9 9.5 %collective-permute-start.1 = (f32[5,4,16,128]{3,2,1,0:T(8,128)S(1)}, f32[5,4,16,128]{3,2,1,0:T(8,128)S(1)}, u32[]{:S(2)}, u32[]{:S(2)}) collective-permute-start(f32[5,4,16,128]{3,2,1,0:T(8,128)S(1)} %pad_maximum_fusion.mine_ref), channel_id=1, source_target_pairs={{0,128},{64,192},{128,0},{192,64},{1,129},{65,193},{129,1},{193,65... | collective-permute-start | bytes 491528 | tf_op jit(solution)/shard_map/ppermute | solution.py:433
  6.2 8.1 %collective-permute-start.3 = (f32[8,16,128]{2,1,0:T(8,128)S(1)}, f32[8,16,128]{2,1,0:T(8,128)S(1)}, u32[]{:S(2)}, u32[]{:S(2)}) collective-permute-start(f32[8,16,128]{2,1,0:T(8,128)S(1)} %get-tuple-element.21), channel_id=1, source_target_pairs={{0,199},{1,192},{2,193},{3,194},{4,195},{5,196},{6,197},{7,198},{8... | collective-permute-start | bytes 196616 | tf_op jit(solution)/shard_map/ppermute | solution.py:427
  8.5 5.9 %collective-permute-start.2 = (f32[8,16,128]{2,1,0:T(8,128)S(1)}, f32[8,16,128]{2,1,0:T(8,128)S(1)}, u32[]{:S(2)}, u32[]{:S(2)}) collective-permute-start(f32[8,16,128]{2,1,0:T(8,128)S(1)} %get-tuple-element.21), channel_id=1, source_target_pairs={{0,71},{1,64},{2,65},{3,66},{4,67},{5,68},{6,69},{7,70},{8,79},{9,... | collective-permute-start | bytes 196616 | tf_op jit(solution)/shard_map/ppermute | solution.py:427
  9.6 7.3 %collective-permute-start.6 = (f32[5,4,16,128]{3,2,1,0:T(8,128)S(1)}, f32[5,4,16,128]{3,2,1,0:T(8,128)S(1)}, u32[]{:S(2)}, u32[]{:S(2)}) collective-permute-start(f32[5,4,16,128]{3,2,1,0:T(8,128)S(1)} %pad_maximum_fusion.mine_ref), channel_id=1, source_target_pairs={{0,56},{8,0},{16,8},{24,16},{32,24},{40,32},{48,40},{56,48},{1,57}... | collective-permute-start | bytes 491528 | tf_op jit(solution)/shard_map/ppermute | solution.py:433
  14.4 5.4 %collective-permute-start.5 = (f32[5,4,16,128]{3,2,1,0:T(8,128)S(1)}, f32[5,4,16,128]{3,2,1,0:T(8,128)S(1)}, u32[]{:S(2)}, u32[]{:S(2)}) collective-permute-start(f32[5,4,16,128]{3,2,1,0:T(8,128)S(1)} %pad_maximum_fusion.mine_ref), channel_id=1, source_target_pairs={{0,8},{8,16},{16,24},{24,32},{32,40},{40,48},{48,56},{56,0},{1,9},... | collective-permute-start | bytes 491528 | tf_op jit(solution)/shard_map/ppermute | solution.py:433
  14.4 5.4 %collective-permute-start.4 = (f32[5,4,16,128]{3,2,1,0:T(8,128)S(1)}, f32[5,4,16,128]{3,2,1,0:T(8,128)S(1)}, u32[]{:S(2)}, u32[]{:S(2)}) collective-permute-start(f32[5,4,16,128]{3,2,1,0:T(8,128)S(1)} %collective-permute-done.1.far_ref), channel_id=1, source_target_pairs={{0,64},{64,0},{128,192},{192,128},{1,65},{65,1},{129,193},{193,129... | collective-permute-start | bytes 491528 | tf_op jit(solution)/shard_map/ppermute | solution.py:433
  20.2 13.1 %collective-permute-start.10 = (f32[5,8,16,128]{3,2,1,0:T(8,128)S(1)}, f32[5,8,16,128]{3,2,1,0:T(8,128)S(1)}, u32[]{:S(2)}, u32[]{:S(2)}) collective-permute-start(f32[5,8,16,128]{3,2,1,0:T(8,128)S(1)} %get-tuple-element.27.own), channel_id=1, source_target_pairs={{0,56},{8,0},{16,8},{24,16},{32,24},{40,32},{48,40},{56,48},{1,57}... | collective-permute-start | bytes 983048 | tf_op jit(solution)/shard_map/ppermute | solution.py:433
  22.6 10.6 %collective-permute-start.9 = (f32[5,8,16,128]{3,2,1,0:T(8,128)S(1)}, f32[5,8,16,128]{3,2,1,0:T(8,128)S(1)}, u32[]{:S(2)}, u32[]{:S(2)}) collective-permute-start(f32[5,8,16,128]{3,2,1,0:T(8,128)S(1)} %get-tuple-element.27.own), channel_id=1, source_target_pairs={{0,8},{8,16},{16,24},{24,32},{32,40},{40,48},{48,56},{56,0},{1,9},... | collective-permute-start | bytes 983048 | tf_op jit(solution)/shard_map/ppermute | solution.py:433
  22.6 3.1 %collective-permute-start.7 = (f32[5,4,16,128]{3,2,1,0:T(8,128)S(1)}, f32[5,4,16,128]{3,2,1,0:T(8,128)S(1)}, u32[]{:S(2)}, u32[]{:S(2)}) collective-permute-start(f32[5,4,16,128]{3,2,1,0:T(8,128)S(1)} %collective-permute-done.5.low_mine), channel_id=1, source_target_pairs={{0,64},{64,0},{128,192},{192,128},{1,65},{65,1},{129,193},{193,129... | collective-permute-start | bytes 491528 | tf_op jit(solution)/shard_map/ppermute | solution.py:433
  24.7 1.4 %collective-permute-start.8 = (f32[5,4,16,128]{3,2,1,0:T(8,128)S(1)}, f32[5,4,16,128]{3,2,1,0:T(8,128)S(1)}, u32[]{:S(2)}, u32[]{:S(2)}) collective-permute-start(f32[5,4,16,128]{3,2,1,0:T(8,128)S(1)} %collective-permute-done.6.high_mine), channel_id=1, source_target_pairs={{0,64},{64,0},{128,192},{192,128},{1,65},{65,1},{129,193},{193,129... | collective-permute-start | bytes 491528 | tf_op jit(solution)/shard_map/ppermute | solution.py:433
  26.1 7.2 %collective-permute-start.11 = (f32[16,8,128]{2,1,0:T(8,128)S(1)}, f32[16,8,128]{2,1,0:T(8,128)S(1)}, u32[]{:S(2)}, u32[]{:S(2)}) collective-permute-start(f32[16,8,128]{2,1,0:T(8,128)S(1)} %get-tuple-element.34), channel_id=1, source_target_pairs={{0,16},{8,24},{16,32},{24,40},{32,48},{40,56},{48,0},{56,8},{1,17}... | collective-permute-start | bytes 196616 | tf_op jit(solution)/shard_map/ppermute | solution.py:433
  26.1 7.2 %collective-permute-start.12 = (f32[16,8,128]{2,1,0:T(8,128)S(1)}, f32[16,8,128]{2,1,0:T(8,128)S(1)}, u32[]{:S(2)}, u32[]{:S(2)}) collective-permute-start(f32[16,8,128]{2,1,0:T(8,128)S(1)} %get-tuple-element.35), channel_id=1, source_target_pairs={{0,48},{8,56},{16,0},{24,8},{32,16},{40,24},{48,32},{56,40},{1,49}... | collective-permute-start | bytes 196616 | tf_op jit(solution)/shard_map/ppermute | solution.py:433
  53.5 4.1 %collective-permute-start.13 = (f32[10,4,16,128]{3,2,1,0:T(8,128)S(1)}, f32[10,4,16,128]{3,2,1,0:T(8,128)S(1)}, u32[]{:S(2)}, u32[]{:S(2)}) collective-permute-start(f32[10,4,16,128]{3,2,1,0:T(8,128)S(1)} %get-tuple-element.37), channel_id=1, source_target_pairs={{0,64},{64,0},{128,192},{192,128},{1,65},{65,1},{129,193},{193,129... | collective-permute-start | bytes 983048 | tf_op jit(solution)/shard_map/ppermute | solution.py:433
